TPU v7x, 256 devices: a whole 4x4x8 slice. The times are simulated.
256 devices in a mesh: tm: 32 (over x, y, core), row: 8 (over z).
Axes of the slice: x: 4, y: 4, z: 8, core: 2. Of those that a mesh axis runs over, the one named last changes fastest.
Arguments:
- frames_in: bfloat16 [64, 32, 64, 256], P('tm', 'row'), may hold values from -6 to 6
- cotangent: bfloat16 [64, 32, 64, 256], P('tm', 'row'), may hold values from -6 to 6
- kernel: bfloat16 [9, 256, 256], replicated, may hold values from -0.125 to 0.125
- readout: bfloat16 [256, 256], replicated, may hold values from -0.375 to 0.375
- feedthrough: float32 [256], replicated, may hold values from 0.5 to 1.5
- decay_rate: float32 [64, 256], P('tm'), may hold values from 0.05 to 1, as said below
- start_state: float32 [32, 64, 256], P('row'), may hold values from -6 to 6
Outputs:
- grad_frames: bfloat16 [64, 32, 64, 256], P('tm', 'row')
- grad_kernel: float32 [9, 256, 256], P(None, 'row')
- grad_readout: float32 [256, 256], P(None, 'row')
Inputs may be any that keep to these rules, and one draw needn't show every extreme that they name: `decay_rate`: every entry lies strictly between 0 and 1.
All inputs are finite; a program needn't handle non-finite values.
Results may differ from a plain program's by a relative error of at most 0.015.
Values may be sent and summed in bfloat16 or wider, within the bound.
No kernel may reach another device: no remote copies, remote signals or barrier semaphores. Data moves between devices by JAX's collectives and lax.ppermute only.
A program may use at most 64 MiB of HBM per device.

v0:
```python
import math

import jax
import jax.numpy as jnp
from jax import lax
from jax.sharding import PartitionSpec as P

SQRT_TWO_PI = 0.7978845608
CUBIC = 0.044715


def extended(cells, sides, width):
    for axis, dim in sides:
        count = lax.axis_size(axis)
        ends = count - 1
        head = lax.slice_in_dim(cells, 0, width, axis=dim)
        tail = lax.slice_in_dim(cells, cells.shape[dim] - width, cells.shape[dim], axis=dim)
        cells = jnp.concatenate(
            [
                lax.ppermute(tail, axis, [(i, (i + 1) % count) for i in range(ends)]),
                cells,
                lax.ppermute(head, axis, [((i + 1) % count, i) for i in range(ends)]),
            ],
            axis=dim,
        )
    return cells


def carried_in(value, axis, join, neutral, backward):
    count, mine = (lax.axis_size(axis), lax.axis_index(axis))
    pieces = jax.tree.map(lambda part: lax.all_gather(part, axis), value)
    if backward:
        pieces = jax.tree.map(lambda part: part[::-1], pieces)
        mine = count - 1 - mine
    subtotal = jax.tree.map(
        lambda part, zero: jnp.full_like(part, 0) + jnp.asarray(zero, part.dtype), value, neutral
    )

    def turn(position, subtotal):
        longer = join(subtotal, jax.tree.map(lambda part: part[position], pieces))
        return jax.tree.map(lambda new, old: jnp.where(position < mine, new, old), longer, subtotal)

    return lax.fori_loop(0, count - 1, turn, subtotal)


def gelu_slope(mixture):
    inside = SQRT_TWO_PI * (mixture + CUBIC * mixture * mixture * mixture)
    tangent = jnp.tanh(inside)
    return 0.5 * (1.0 + tangent) + 0.5 * mixture * (1.0 - tangent * tangent) * SQRT_TWO_PI * (
        1.0 + 3.0 * CUBIC * mixture * mixture
    )


def block_taps(padded, band_rows, grid_width, flipped):
    pieces = []
    for vertical in range(3):
        for lateral in range(3):
            from_top = 2 - vertical if flipped else vertical
            from_left = 2 - lateral if flipped else lateral
            pieces.append(
                padded[:, from_top : from_top + band_rows, from_left : from_left + grid_width, :]
            )
    return jnp.stack(pieces, axis=3)


def compose(earlier, later):
    return (later[0] * earlier[0], later[0] * earlier[1] + later[1])


def local(frames_in, cotangent, kernel, readout, feedthrough, decay_rate, start_state):
    frames_here, band_rows, grid_width, channels = frames_in.shape
    state_width = kernel.shape[2]
    cell_count = frames_here * band_rows * grid_width
    rimmed = extended(frames_in, (("row", 1),), 1)
    padded = jnp.pad(rimmed, ((0, 0), (0, 0), (1, 1), (0, 0)))
    input_taps = block_taps(padded, band_rows, grid_width, False).reshape(cell_count, 9 * channels)
    driven = jnp.dot(
        input_taps, kernel.reshape(9 * channels, state_width), preferred_element_type=jnp.float32
    )
    driven = driven.reshape(frames_here, band_rows, grid_width, state_width)
    gain_all = jnp.sqrt(1.0 - decay_rate * decay_rate)
    leader = (lax.axis_index("tm") == 0).astype(jnp.float32)

    def advance(carried, inputs):
        driven_now, rate_now, gain_now = inputs
        carried = rate_now * carried + gain_now * driven_now
        return (carried, carried)

    _, local_states = lax.scan(advance, start_state * leader, (driven, decay_rate, gain_all))
    through = jnp.cumprod(decay_rate, axis=0)
    identity = (
        jnp.ones((state_width,), jnp.float32),
        jnp.zeros((band_rows, grid_width, state_width), jnp.float32),
    )
    _, entering = carried_in((through[-1], local_states[-1]), "tm", compose, identity, False)
    states = local_states + through[:, None, None, :] * entering[None]
    state_bf = states.astype(jnp.bfloat16).reshape(cell_count, state_width)
    mixture = jnp.dot(state_bf, readout, preferred_element_type=jnp.float32)
    slope_bf = (
        cotangent.reshape(cell_count, channels).astype(jnp.float32) * gelu_slope(mixture)
    ).astype(jnp.bfloat16)
    pulled = lax.dot_general(
        slope_bf, readout, (((1,), (1,)), ((), ())), preferred_element_type=jnp.float32
    )
    pulled = pulled.reshape(frames_here, band_rows, grid_width, state_width)
    later_rate = jnp.concatenate([decay_rate[1:], jnp.ones((1, state_width), jnp.float32)], axis=0)

    def retreat(carried, inputs):
        pulled_now, rate_next = inputs
        carried = pulled_now + rate_next * carried
        return (carried, carried)

    _, local_adjoint = lax.scan(
        retreat,
        jnp.zeros((band_rows, grid_width, state_width), jnp.float32),
        (pulled, later_rate),
        reverse=True,
    )
    remaining = jnp.flip(jnp.cumprod(jnp.flip(later_rate, 0), axis=0), 0)
    _, arriving = carried_in(
        (through[-1], decay_rate[0][None, None, :] * local_adjoint[0]),
        "tm",
        compose,
        identity,
        True,
    )
    adjoint = local_adjoint + remaining[:, None, None, :] * arriving[None]
    grad_drive = (gain_all[:, None, None, :] * adjoint).astype(jnp.bfloat16)
    rim_adjoint = extended(grad_drive, (("row", 1),), 1)
    padded_drive = jnp.pad(rim_adjoint, ((0, 0), (0, 0), (1, 1), (0, 0)))
    output_taps = block_taps(padded_drive, band_rows, grid_width, True).reshape(
        cell_count, 9, state_width
    )
    spread = lax.dot_general(
        output_taps, kernel, (((1, 2), (0, 2)), ((), ())), preferred_element_type=jnp.float32
    )
    spread = spread.reshape(frames_here, band_rows, grid_width, channels)
    grad_frames = (spread + feedthrough * cotangent.astype(jnp.float32)).astype(jnp.bfloat16)
    kernel_term = lax.dot_general(
        input_taps,
        grad_drive.reshape(cell_count, state_width),
        (((0,), (0,)), ((), ())),
        preferred_element_type=jnp.float32,
    ).reshape(9, channels, state_width)
    readout_term = lax.dot_general(
        state_bf, slope_bf, (((0,), (0,)), ((), ())), preferred_element_type=jnp.float32
    )
    band_count = lax.axis_size("row")
    scaling = 1.0 / math.sqrt(cell_count * lax.axis_size("tm") * band_count)
    share_width = channels // band_count
    kernel_all, readout_all = lax.psum((kernel_term, readout_term), ("tm", "row"))
    offset_start = lax.axis_index("row") * share_width
    kernel_part = lax.dynamic_slice_in_dim(kernel_all, offset_start, share_width, 1)
    readout_part = lax.dynamic_slice_in_dim(readout_all, offset_start, share_width, 1)
    return (grad_frames, kernel_part * scaling, readout_part * scaling)


def solution(mesh):
    placed = (
        P("tm", "row", None, None),
        P("tm", "row", None, None),
        P(),
        P(),
        P(),
        P("tm", None),
        P("row", None, None),
    )
    return jax.shard_map(
        local,
        mesh=mesh,
        in_specs=placed,
        out_specs=(P("tm", "row", None, None), P(None, "row", None), P(None, "row")),
        check_vma=False,
    )
```

profile of v0, /device:TPU:1, one launch (start us, length us, event | category | flops | bytes accessed | tf_op | source)
XLA Modules:
  0.0 509.6 jit_solution(2149309793703916554)
XLA Ops:
  8.2 4.4 collective-permute-start
  12.6 1.3 collective-permute-start.1
  15.6 2.2 collective-permute-done.1
  22.9 26.3 %all-gather = f32[32,1,256]{2,1,0:T(1,128)S(1)} all-gather(f32[1,1,256]{2,1,0:T(1,128)S(1)} %slice_bitcast_fusion.12), channel_id=1, replica_groups=mesh['tm'=32,'row'=8] {'tm'}, dimensions={0}, use_global_device_ids=true | all-gather | bytes 33792 | tf_op jit(solution)/shard_map/all_gather | solution.py:31
  49.2 36.0 %all-gather.4.cloned.1.call-done = f32[32,4,64,256]{3,2,1,0:T(8,128)} async-done(((f32[1,4,64,256]{3,2,1,0:T(8,128)}), f32[32,4,64,256]{3,2,1,0:T(8,128)}) %all-gather.4.cloned.1.call-update) | async-done | bytes 8388624 | tf_op jit(solution)/shard_map/all_gather | solution.py:31
  85.2 36.9 %while.58 = (s32[]{:T(128)}, f32[4,64,256]{2,1,0:T(8,128)S(1)}, s32[]{:T(128)}, f32[32,256]{1,0:T(8,128)S(1)}, f32[32,4,64,256]{3,2,1,0:T(8,128)}, /*index=5*/s32[]{:T(128)}, s32[]{:T(128)}) while((s32[]{:T(128)}, f32[4,64,256]{2,1,0:T(8,128)S(1)}, s32[]{:T(128)}, f32[32,256]{1,0:T(8,128)S(1)}, f32[32,4,64,256]{3,2,1,0:T(8,128)}, ...), condition=%wide.region_4.5_spmd.clone, body=%wide.region_3.4_spmd.clone.sunk | while | flops 262148 | bytes 789609 | solution.py:43
  85.2 1.2 fusion.59
  86.5 1.1 fusion.59
  87.7 1.1 fusion.59
  88.9 1.1 fusion.59
  90.0 1.1 fusion.59
  91.2 1.1 fusion.59
  92.4 1.1 fusion.59
  93.6 1.1 fusion.59
  94.8 1.1 fusion.59
  96.0 1.1 fusion.59
  97.2 1.1 fusion.59
  98.4 1.1 fusion.59
  99.6 1.1 fusion.59
  124.4 3.3 copy.51
  127.8 2.8 copy.57
  130.5 4.3 copy.52
  135.8 45.9 %all-gather.6.cloned.1.call-done = f32[32,4,64,256]{3,2,1,0:T(8,128)} async-done(((f32[1,4,64,256]{3,2,1,0:T(8,128)}), f32[32,4,64,256]{3,2,1,0:T(8,128)}) %all-gather.6.cloned.1.call-update) | async-done | bytes 8388624 | tf_op jit(solution)/shard_map/all_gather | solution.py:31
  181.7 7.7 %rev.16 = f32[32,4,64,256]{3,2,1,0:T(8,128)} reverse(f32[32,4,64,256]{3,2,1,0:T(8,128)} %all-gather.6.cloned.1.call-done), dimensions={0} | reverse | bytes 16777216 | tf_op jit(solution)/shard_map/rev | solution.py:33
  189.4 36.8 %while.60 = (s32[]{:T(128)}, f32[4,64,256]{2,1,0:T(8,128)S(1)}, s32[]{:T(128)}, f32[32,256]{1,0:T(8,128)S(1)}, f32[32,4,64,256]{3,2,1,0:T(8,128)}, /*index=5*/s32[]{:T(128)}, s32[]{:T(128)}) while((s32[]{:T(128)}, f32[4,64,256]{2,1,0:T(8,128)S(1)}, s32[]{:T(128)}, f32[32,256]{1,0:T(8,128)S(1)}, f32[32,4,64,256]{3,2,1,0:T(8,128)}, ...), condition=%wide.region_9.10_spmd.clone, body=%wide.region_8.9_spmd.clone.sunk | while | flops 262148 | bytes 789609 | solution.py:43
  226.3 3.2 collective-permute-start.2
  229.5 1.3 collective-permute-start.3
  230.8 3.9 fusion.45
  235.9 1.5 fusion.4
  237.4 262.6 %all-reduce.6.cloned.1.call-done = (f32[9,256,256]{2,1,0:T(8,128)}, f32[256,256]{0,1:T(8,128)}) async-done(((f32[9,256,256]{2,1,0:T(8,128)}, f32[256,256]{0,1:T(8,128)}), (f32[9,256,256]{2,1,0:T(8,128)}, f32[256,256]{0,1:T(8,128)})) %all-reduce.6.cloned.1.call-update) | async-done | bytes 2621456 | tf_op jit(solution)/shard_map/psum | solution.py:151
  500.0 1.7 dynamic-slice_multiply_fusion
  501.7 1.4 dynamic-slice_multiply_fusion.1
  (192 shorter events, 69.4 us)
Async XLA Ops:
  7.2 13.0 %copy-start = (bf16[9,256,256]{2,1,0:T(8,128)(2,1)S(1)}, bf16[9,256,256]{2,1,0:T(8,128)(2,1)}, u32[]{:S(2)}) copy-start(bf16[9,256,256]{2,1,0:T(8,128)(2,1)} %param.17) | copy-start | bytes 3538948
  7.2 12.8 %copy-start.1 = (bf16[2,4,64,256]{3,2,1,0:T(8,128)(2,1)S(1)}, bf16[2,4,64,256]{3,2,1,0:T(8,128)(2,1)}, u32[]{:S(2)}) copy-start(bf16[2,4,64,256]{3,2,1,0:T(8,128)(2,1)} %param.15) | copy-start | bytes 786436
  7.2 78.0 %all-gather.4.cloned.1.call-start = ((), (), s32[]{:S(2)}) async-start(), calls=%async_computation | async-start | bytes 8650752 | tf_op jit(solution)/shard_map/all_gather | solution.py:31
  8.2 7.3 %collective-permute-start = (bf16[2,1,64,256]{3,2,1,0:T(8,128)(2,1)S(1)}, bf16[2,1,64,256]{3,2,1,0:T(8,128)(2,1)S(1)}, u32[]{:S(2)}, u32[]{:S(2)}) collective-permute-start(bf16[2,1,64,256]{3,2,1,0:T(8,128)(2,1)S(1)} %get-tuple-element.436), channel_id=1, source_target_pairs={{0,1},{1,2},{2,3},{3,4},{4,5},{5,6},{6,7},{8,9},{9,10},{10,11},{11... | collective-permute-start | bytes 196616 | tf_op jit(solution)/shard_map/ppermute | solution.py:20
  12.6 5.2 %collective-permute-start.1 = (bf16[2,1,64,256]{3,2,1,0:T(8,128)(2,1)S(1)}, bf16[2,1,64,256]{3,2,1,0:T(8,128)(2,1)S(1)}, u32[]{:S(2)}, u32[]{:S(2)}) collective-permute-start(bf16[2,1,64,256]{3,2,1,0:T(8,128)(2,1)S(1)} %get-tuple-element.437), channel_id=1, source_target_pairs={{1,0},{2,1},{3,2},{4,3},{5,4},{6,5},{7,6},{9,8},{10,9},{11,10},{12... | collective-permute-start | bytes 196616 | tf_op jit(solution)/shard_map/ppermute | solution.py:22
  20.2 1.5 copy-start.2
  20.2 1.5 copy-start.4
  22.8 158.9 %all-gather.6.cloned.1.call-start = ((), (), s32[]{:S(2)}) async-start(), calls=%async_computation.1 | async-start | bytes 8650752 | tf_op jit(solution)/shard_map/all_gather | solution.py:31
  85.2 37.0 %copy-start.3 = (bf16[256,256]{1,0:T(8,128)(2,1)S(1)}, bf16[256,256]{1,0:T(8,128)(2,1)}, u32[]{:S(2)}) copy-start(bf16[256,256]{1,0:T(8,128)(2,1)} %param.18) | copy-start | bytes 393220
  85.2 37.0 %copy-start.5 = (bf16[2,4,64,256]{3,2,1,0:T(8,128)(2,1)S(1)}, bf16[2,4,64,256]{3,2,1,0:T(8,128)(2,1)}, u32[]{:S(2)}) copy-start(bf16[2,4,64,256]{3,2,1,0:T(8,128)(2,1)} %param.16) | copy-start | bytes 786436
  124.1 375.9 %all-reduce.6.cloned.1.call-start = ((), (), s32[]{:S(2)}) async-start(), calls=%async_computation.2 | async-start | bytes 5242880 | tf_op jit(solution)/shard_map/psum | solution.py:151
  226.3 8.4 %collective-permute-start.2 = (bf16[2,1,64,256]{3,2,1,0:T(8,128)(2,1)S(1)}, bf16[2,1,64,256]{3,2,1,0:T(8,128)(2,1)S(1)}, u32[]{:S(2)}, u32[]{:S(2)}) collective-permute-start(bf16[2,1,64,256]{3,2,1,0:T(8,128)(2,1)S(1)} %get-tuple-element.434), channel_id=1, source_target_pairs={{0,1},{1,2},{2,3},{3,4},{4,5},{5,6},{6,7},{8,9},{9,10},{10,11},{11... | collective-permute-start | bytes 196616 | tf_op jit(solution)/shard_map/ppermute | solution.py:20
  229.5 5.2 %collective-permute-start.3 = (bf16[2,1,64,256]{3,2,1,0:T(8,128)(2,1)S(1)}, bf16[2,1,64,256]{3,2,1,0:T(8,128)(2,1)S(1)}, u32[]{:S(2)}, u32[]{:S(2)}) collective-permute-start(bf16[2,1,64,256]{3,2,1,0:T(8,128)(2,1)S(1)} %get-tuple-element.435), channel_id=1, source_target_pairs={{1,0},{2,1},{3,2},{4,3},{5,4},{6,5},{7,6},{9,8},{10,9},{11,10},{12... | collective-permute-start | bytes 196616 | tf_op jit(solution)/shard_map/ppermute | solution.py:22
  235.0 1.0 copy-start.6
  235.0 0.9 copy-start.7
Sparse Core Ops, SparseCore 0:
  22.9 62.2 all-gather.3
  124.2 57.4 all-gather.5
  234.8 265.1 all-reduce.5
where the time goes:
time: 513 us; the launch traced here: 510 us
  waiting for transfers between devices  347 us (68%)
  other arithmetic  79.8 us (16%)
  blocking collectives  26.3 us (5%)
  local copies, waits for them, and re-layouts  22.5 us (4%)
  between operations  14.2 us (3%)
  starting transfers between devices  10.2 us (2%)
  matrix products  7.92 us (2%)
    psum x1, waiting for transfers between devices, local(): lax.psum((kernel_term, readout_term), ('tm', 'row'))  263 us
    all_gather x2, waiting for transfers between devices, carried_in(): pieces = jax.tree.map(lambda part: lax.all_gather(part, axis), value)  81.9 us
    select_n x62, other arithmetic, turn(): jnp.where(position < mine, new, old)  71.3 us
    all_gather x1, blocking collectives, carried_in(): pieces = jax.tree.map(lambda part: lax.all_gather(part, axis), value)  26.3 us
  transfers between devices with their start and end apart: 7, of which 4 were waited for; matrix products, arithmetic and copies ran while one was open for 4% of the time, Pallas kernels for 0%

commit v1 on v0

v1 whole, which is shorter than its diff:
```python
import functools
import math

import jax
import jax.numpy as jnp
from jax import lax
from jax.experimental import pallas as pl
from jax.experimental.pallas import tpu as pltpu
from jax.sharding import PartitionSpec as P

SQRT_TWO_PI = 0.7978845608
CUBIC = 0.044715
BF = jnp.bfloat16
F32 = jnp.float32
PAD = 8
CELLS = ((0, 0), (0, 1), (2, 0), (2, 1), (1, 0), (1, 1), (3, 0), (3, 1))
VMEM = pl.BlockSpec(memory_space=pltpu.VMEM)


def call(body, name, outs, ins, scratch, flops=1 << 20, moved=1 << 20):
    many = isinstance(outs, (list, tuple))
    return pl.pallas_call(
        body,
        name=name,
        out_shape=outs,
        in_specs=[VMEM] * ins,
        out_specs=[VMEM] * len(outs) if many else VMEM,
        scratch_shapes=scratch,
        cost_estimate=pl.CostEstimate(flops=flops, bytes_accessed=moved, transcendentals=0),
        compiler_params=pltpu.CompilerParams(vmem_limit_bytes=40 << 20),
    )


def split3(value):
    high = value.astype(BF).astype(F32)
    rest = value - high
    middle = rest.astype(BF).astype(F32)
    return high, middle, rest - middle


def sublane(shape):
    return lax.broadcasted_iota(jnp.int32, shape, len(shape) - 2)


def gelu_slope(mixture):
    inside = SQRT_TWO_PI * (mixture + CUBIC * mixture * mixture * mixture)
    tangent = jnp.tanh(inside)
    return 0.5 * (1.0 + tangent) + 0.5 * mixture * (1.0 - tangent * tangent) * SQRT_TWO_PI * (
        1.0 + 3.0 * CUBIC * mixture * mixture
    )


def halo_body(frames, cotangent, start, out, parts):
    wide = frames.shape[2]
    for f in range(2):
        for row in range(2):
            out[pl.ds((2 * f + row) * wide, wide), :] = frames[f, 2 + row]
        out[pl.ds((4 + f) * wide, wide), :] = cotangent[f, 3]
    for place, piece in enumerate(split3(start[3])):
        parts[pl.ds(2 * place, 2), :] = piece
    parts[6:8, :] = jnp.zeros_like(parts[6:8, :])
    out[pl.ds(6 * wide, 8), :] = parts[...].astype(BF)


def spread_body(frames, cotangent, decay, halo, out, grid, slopes, parts):
    wide = frames.shape[2]
    for f in range(2):
        for row in range(6):
            grid[f, row, 0:PAD, :] = jnp.zeros((PAD, grid.shape[3]), F32)
            grid[f, row, PAD + wide :, :] = jnp.zeros((PAD, grid.shape[3]), F32)
            source = halo[pl.ds((2 * f + row) * wide, wide), :] if row < 2 else frames[f, row - 2]
            grid[f, row, PAD : PAD + wide, :] = source.astype(F32)
        for row in range(4):
            source = halo[pl.ds((4 + f) * wide, wide), :] if row < 1 else cotangent[f, row - 1]
            slopes[f, row, PAD : PAD + wide, :] = source.astype(F32)
    for place, piece in enumerate(split3(decay[...])):
        parts[pl.ds(2 * place, 2), :] = piece
    parts[6:8, :] = jnp.zeros_like(parts[6:8, :])
    rates = parts[...].astype(BF)
    step = sublane((8, grid.shape[3]))
    for target in range(wide // 2):
        first = PAD + 2 * target
        for f in range(2):
            for pair in range(3):
                begin = first - 1
                block = jnp.where(
                    step < 4,
                    grid[f, 2 * pair, begin : begin + 8, :],
                    grid[f, 2 * pair + 1, begin - 4 : begin + 4, :],
                )
                out[target, 32 * f + 8 * pair : 32 * f + 8 * pair + 8, :] = block.astype(BF)
            block = slopes[f, 0, first : first + 8, :]
            for place, row in ((2, 2), (4, 1), (6, 3)):
                block = jnp.where(step < place, block, slopes[f, row, first - place : first - place + 8, :])
            out[target, 32 * f + 24 : 32 * f + 32, :] = block.astype(BF)
        out[target, 64:72, :] = rates


def cell_body(
    got, kernel, readout, start, halo, out, grid, decay, gain, taps, driven, states, slopes, drive, turned, begin
):
    sources = got.shape[0]
    count = sources * 16
    wide = (halo.shape[0] - 8) // 6
    lanes = got.shape[2]
    step = sublane((8, lanes))
    is_first = lax.axis_index("row") == 0
    low = jnp.where(is_first & (step < 2), 0.0, 1.0)
    high = jnp.where(is_first & (step >= 4) & (step < 6), 0.0, 1.0)
    near = (step % 4) < 2

    def unpack(source, _):
        for f in range(2):
            grid[2 * source + f] = got[source, 32 * f : 32 * f + 24, :].astype(F32)
        piece = got[source, 64:72, :].astype(F32)
        rate = piece + pltpu.roll(piece, 6, 0) + pltpu.roll(piece, 4, 0)
        decay[source] = rate
        gain[source] = jnp.sqrt(1.0 - rate * rate)
        return _

    lax.fori_loop(0, sources, unpack, 0, unroll=4)

    def gather(source, _):
        rows = pl.ds(pl.multiple_of(16 * source, 16), 16)
        for i in range(3):
            for j in range(3):
                place = 4 * i + j
                pair = []
                for f in range(2):
                    value = jnp.where(
                        near,
                        grid[2 * source + f, place : place + 8, :],
                        grid[2 * source + f, place + 6 : place + 14, :],
                    )
                    if i == 2:
                        value = value * low
                    if i == 0:
                        value = value * high
                    pair.append(value)
                tap = 3 * i + j
                taps[rows, lanes * tap : lanes * tap + lanes] = jnp.concatenate(pair, axis=0).astype(BF)
        return _

    lax.fori_loop(0, sources, gather, 0, unroll=2)

    chunk = min(count, 256)

    def convolve(part, _):
        rows = pl.ds(pl.multiple_of(part * chunk, chunk), chunk)
        driven[rows, :] = jnp.dot(taps[rows, :], kernel[...], preferred_element_type=F32)
        return _

    lax.fori_loop(0, count // chunk, convolve, 0)

    tail = halo[6 * wide : 6 * wide + 8, :].astype(F32)
    begin[0:8, :] = tail
    top = begin[0:2, :] + begin[2:4, :] + begin[4:6, :]
    begin[0:2, :] = top
    begin[2:4, :] = start[1]
    begin[4:6, :] = start[0]
    begin[6:8, :] = start[2]

    def advance(source, state):
        pair = []
        for f in range(2):
            rate = jnp.broadcast_to(decay[source, f : f + 1, :], state.shape)
            size = jnp.broadcast_to(gain[source, f : f + 1, :], state.shape)
            now = driven[pl.ds(pl.multiple_of(16 * source + 8 * f, 8), 8), :]
            state = rate * state + size * now
            pair.append(state)
        states[pl.ds(pl.multiple_of(16 * source, 16), 16), :] = jnp.concatenate(pair, axis=0).astype(BF)
        return state

    lax.fori_loop(0, sources, advance, begin[...], unroll=4)

    def mix(part, _):
        rows = pl.ds(pl.multiple_of(part * 64, 64), 64)
        mixture = jnp.dot(states[rows, :], readout[...], preferred_element_type=F32)
        upstream = jnp.concatenate(
            [
                got[4 * part + source, 32 * f + 24 : 32 * f + 32, :].astype(F32)
                for source in range(4)
                for f in range(2)
            ],
            axis=0,
        )
        slope = (upstream * gelu_slope(mixture)).astype(BF)
        slopes[rows, :] = slope
        driven[rows, :] = lax.dot_general(
            slope, readout[...], (((1,), (1,)), ((), ())), preferred_element_type=F32
        )
        return _

    lax.fori_loop(0, count // 64, mix, 0, unroll=2)

    def retreat(turn, carried):
        adjoint, later = carried
        source = sources - 1 - turn
        pair = []
        for f in (1, 0):
            now = driven[pl.ds(pl.multiple_of(16 * source + 8 * f, 8), 8), :]
            adjoint = now + later * adjoint
            later = jnp.broadcast_to(decay[source, f : f + 1, :], adjoint.shape)
            value = jnp.broadcast_to(gain[source, f : f + 1, :], adjoint.shape) * adjoint
            pair.append(value)
            out[source, 0:8, 10 * lanes + f * lanes : 11 * lanes + f * lanes] = value.astype(BF)
        drive[pl.ds(pl.multiple_of(16 * source, 16), 16), :] = jnp.concatenate(pair[::-1], axis=0)
        return adjoint, later

    nothing = jnp.zeros((8, lanes), F32)
    lax.fori_loop(0, sources, retreat, (nothing, nothing), unroll=4)

    turned[...] = drive[...].astype(BF).T
    share = lanes // sources
    for tap in range(9):
        term = jnp.dot(turned[...], taps[:, lanes * tap : lanes * tap + lanes], preferred_element_type=F32)
        out[:, :, lanes * tap : lanes * tap + lanes] = term.astype(BF).reshape(sources, share, lanes)
    term = jnp.dot(states[...].T, slopes[...], preferred_element_type=F32)
    out[:, :, 9 * lanes : 10 * lanes] = term.astype(BF).reshape(sources, share, lanes)


def join_body(bands, got, total, frames, cells, grid):
    sources, share, width = got.shape
    lanes = width // 12

    def add(source, carried):
        return carried + got[source, :, : 10 * lanes].astype(F32)

    sums = lax.fori_loop(0, sources, add, jnp.zeros((share, 10 * lanes), F32), unroll=2)
    block = lanes // bands
    for band in range(bands):
        total[band] = jnp.concatenate(
            [sums[:, lanes * k + block * band : lanes * k + block * band + block] for k in range(10)], axis=1
        )

    for f in range(2):
        for part in range(lanes // 128):
            for source in range(sources):
                first = (10 + f) * lanes + 128 * part
                cells[8 * source : 8 * source + 8, :] = got[source, 0:8, first : first + 128].astype(F32)
            for place, (row, column) in enumerate(CELLS):
                grid[pl.ds(column, sources, stride=2), :] = cells[pl.ds(place, sources, stride=8), :]
                if column == 1:
                    frames[f, row, :, 128 * part : 128 * part + 128] = grid[...].astype(BF)


def back_body(bands, drive, below, kernel, cotangent, feedthrough, out, grid, moved):
    wide = drive.shape[2]
    lanes = drive.shape[3]
    band = lax.axis_index("row")
    for row in range(6):
        keep = None
        if row == 0:
            keep = jnp.where(band == 0, 0.0, 1.0)
        if row == 5:
            keep = jnp.where(band == bands - 1, 0.0, 1.0)
        for f in range(2):
            source = (drive[f, row] if row < 4 else below[f, row - 4]).astype(F32)
            if keep is not None:
                source = source * keep
            grid[0:PAD, :] = jnp.zeros((PAD, lanes), F32)
            grid[PAD + wide :, :] = jnp.zeros((PAD, lanes), F32)
            grid[PAD : PAD + wide, :] = source
            for shift in range(3):
                moved[shift, f, row] = grid[PAD - 1 + shift : PAD - 1 + shift + wide, :].astype(BF)
    for f in range(2):
        for half in range(2):
            total = jnp.zeros((2 * wide, lanes), F32)
            for i in range(3):
                for j in range(3):
                    first = 2 - i + 2 * half
                    cells = moved[2 - j, f, first : first + 2].reshape(2 * wide, lanes)
                    total = total + lax.dot_general(
                        cells, kernel[3 * i + j], (((1,), (1,)), ((), ())), preferred_element_type=F32
                    )
            total = total.reshape(2, wide, lanes)
            for row in range(2):
                place = 2 * half + row
                out[f, place] = (total[row] + feedthrough[...] * cotangent[f, place].astype(F32)).astype(BF)


def sum_body(scaling, got, out):
    total = got[0]
    for band in range(1, got.shape[0]):
        total = total + got[band]
    total = total * scaling
    for target in range(out.shape[0]):
        out[target] = total


def last_body(got, kernel_out, readout_out):
    sources, share, width = got.shape
    turned = got[...].reshape(sources * share, width).T
    block = width // 10
    for k in range(9):
        kernel_out[k] = turned[block * k : block * k + block]
    readout_out[...] = turned[9 * block :]


def local(frames_in, cotangent, kernel, readout, feedthrough, decay_rate, start_state):
    here, band_rows, wide, lanes = frames_in.shape
    sources, bands = lax.axis_size("tm"), lax.axis_size("row")
    cells = sources * 16
    share = lanes // sources
    block = lanes // bands
    shape = jax.ShapeDtypeStruct
    down = [(i, (i + 1) % bands) for i in range(bands)]
    up = [((i + 1) % bands, i) for i in range(bands)]

    start = lax.dynamic_slice_in_dim(start_state, 2 * lax.axis_index("tm"), 2, 1)
    edge = call(
        halo_body, "halo", shape((6 * wide + 8, lanes), BF), 3, [pltpu.VMEM((8, lanes), F32)]
    )(frames_in, cotangent, start)
    edge = lax.ppermute(edge, "row", down)
    send = call(
        spread_body,
        "spread",
        shape((sources, 72, lanes), BF),
        4,
        [
            pltpu.VMEM((2, 6, wide + 2 * PAD, lanes), F32),
            pltpu.VMEM((2, 4, wide + 2 * PAD, lanes), F32),
            pltpu.VMEM((8, lanes), F32),
        ],
    )(frames_in, cotangent, decay_rate, edge)
    got = lax.all_to_all(send, "tm", 0, 0)
    send = call(
        cell_body,
        "cells",
        shape((sources, max(8, share), 12 * lanes), BF),
        5,
        [
            pltpu.VMEM((2 * sources, 24, lanes), F32),
            pltpu.VMEM((sources, 8, lanes), F32),
            pltpu.VMEM((sources, 8, lanes), F32),
            pltpu.VMEM((cells, 9 * lanes), BF),
            pltpu.VMEM((cells, lanes), F32),
            pltpu.VMEM((cells, lanes), BF),
            pltpu.VMEM((cells, lanes), BF),
            pltpu.VMEM((cells, lanes), F32),
            pltpu.VMEM((lanes, cells), BF),
            pltpu.VMEM((8, lanes), F32),
        ],
        flops=2 * cells * lanes * lanes * 21,
        moved=4 << 20,
    )(got, kernel.reshape(9 * lanes, lanes), readout, start, edge)
    got = lax.all_to_all(send, "tm", 0, 0)
    partial, drive = call(
        functools.partial(join_body, bands),
        "join",
        (shape((bands, share, 10 * block), F32), shape((2, 4, wide, lanes), BF)),
        1,
        [pltpu.VMEM((8 * sources, 128), F32), pltpu.VMEM((wide, 128), F32)],
    )(got)
    below = lax.ppermute(drive[:, :2], "row", up)
    partial = lax.all_to_all(partial, "row", 0, 0)
    scaling = 1.0 / math.sqrt(here * sources * band_rows * bands * wide)
    partial = call(
        functools.partial(sum_body, scaling), "sum", shape((sources, share, 10 * block), F32), 1, []
    )(partial)
    grad_frames = call(
        functools.partial(back_body, bands),
        "back",
        shape(frames_in.shape, BF),
        5,
        [
            pltpu.VMEM((wide + 2 * PAD, lanes), F32),
            pltpu.VMEM((3, 2, 6, wide, lanes), BF),
        ],
        flops=2 * cells * lanes * lanes * 9,
        moved=2 << 20,
    )(drive, below, kernel, cotangent, feedthrough.reshape(1, lanes))
    whole = lax.all_to_all(partial, "tm", 0, 0)
    grad_kernel, grad_readout = call(
        last_body, "last", (shape((9, block, lanes), F32), shape((block, lanes), F32)), 1, []
    )(whole)
    return grad_frames, grad_kernel, grad_readout.T


def solution(mesh):
    placed = (
        P("tm", "row", None, None),
        P("tm", "row", None, None),
        P(),
        P(),
        P(),
        P("tm", None),
        P("row", None, None),
    )
    return jax.shard_map(
        local,
        mesh=mesh,
        in_specs=placed,
        out_specs=(P("tm", "row", None, None), P(None, "row", None), P(None, "row")),
        check_vma=False,
    )
```

time: 513 us -> 106 us (0.21)
  waiting for transfers between devices: 347 us -> 16.5 us
  other arithmetic: 79.8 us -> 0 us
  blocking collectives: 26.3 us -> 66.8 us
  local copies, waits for them, and re-layouts: 22.5 us -> 3.56 us
  between operations: 14.2 us -> 0.73 us
  Pallas kernels: 0 us -> 10.3 us
  matrix products: 7.92 us -> 0 us
    psum x1 -> x0, waiting for transfers between devices: 263 us -> none  [local(): lax.psum((kernel_term, readout_term), ('tm', 'row'))]
    all_gather x2 -> x0, waiting for transfers between devices: 81.9 us -> none  [carried_in(): pieces = jax.tree.map(lambda part: lax.all_gather(part, axis), value)]
    select_n x62 -> x0, other arithmetic: 71.3 us -> none  [turn(): jnp.where(position < mine, new, old)]
    all_to_all x0 -> x3, blocking collectives: none -> 66.8 us  [the longest x2 53.6 us: local(): got = lax.all_to_all(send, 'tm', 0, 0)]
    all_gather x1 -> x0, blocking collectives: 26.3 us -> none  [carried_in(): pieces = jax.tree.map(lambda part: lax.all_gather(part, axis), value)]
    ppermute x4 -> x2, waiting for transfers between devices: 2.22 us -> 13.3 us  [the longest x1 8.63 us: local(): edge = lax.ppermute(edge, 'row', down)]
    pallas_call x0 -> x7, Pallas kernels: none -> 10.3 us  [the longest x1 4.96 us: local(): call(cell_body, 'cells', shape((sources, max(8, share), 12 * lanes), BF),...]
    rev x4 -> x0, local copies, waits for them, and re-layouts: 7.94 us -> none  [the longest x2 7.79 us: carried_in(): pieces = jax.tree.map(lambda part: part[::-1], pieces)]
  transfers between devices with their start and end apart: 7 -> 3, of which waited for: 4 -> 3; matrix products, arithmetic and copies ran while one was open for 4% -> 0% of each run, Pallas kernels for 0% -> 2%
where the time goes in v1:
time: 106 us; the launch traced here: 105 us
  blocking collectives  66.8 us (63%)
  waiting for transfers between devices  16.5 us (16%)
  Pallas kernels  10.3 us (10%)
  starting transfers between devices  7.42 us (7%)
  local copies, waits for them, and re-layouts  3.56 us (3%)
    all_to_all x2, blocking collectives, local(): got = lax.all_to_all(send, 'tm', 0, 0)  53.6 us
    all_to_all x1, blocking collectives, local(): partial = lax.all_to_all(partial, 'row', 0, 0)  13.2 us
    ppermute x1, waiting for transfers between devices, local(): edge = lax.ppermute(edge, 'row', down)  8.63 us
    pallas_call x1, Pallas kernels, local(): call(cell_body, 'cells', shape((sources, max(8, share), 12 * lanes), BF),...  4.96 us
    all_to_all x1, starting transfers between devices, local(): whole = lax.all_to_all(partial, 'tm', 0, 0)  4.82 us
    ppermute x1, waiting for transfers between devices, local(): below = lax.ppermute(drive[:, :2], 'row', up)  4.69 us
    unnamed x16, local copies, waits for them, and re-layouts  3.54 us
    all_to_all x1, waiting for transfers between devices, local(): whole = lax.all_to_all(partial, 'tm', 0, 0)  3.17 us
  transfers between devices with their start and end apart: 3, of which 3 were waited for; matrix products, arithmetic and copies ran while one was open for 0% of the time, Pallas kernels for 2%

profile of v1, /device:TPU:1, one launch (start us, length us, event | category | flops | bytes accessed | tf_op | source)
XLA Modules:
  0.0 105.4 jit_solution(11570596231106078559)
XLA Ops:
  0.6 0.0 copy-start
  0.6 0.9 copy-done
  1.6 0.0 copy-start.1
  1.6 0.9 copy-done.1
  2.5 0.0 copy-start.2
  2.5 0.9 copy-done.2
  3.5 2.5 %collective-permute-start = (bf16[392,256]{1,0:T(8,128)(2,1)S(1)}, bf16[392,256]{1,0:T(8,128)(2,1)S(1)}, u32[]{:S(2)}, u32[]{:S(2)}) collective-permute-start(bf16[392,256]{1,0:T(8,128)(2,1)S(1)} %halo.1), channel_id=1, source_target_pairs={{0,1},{1,2},{2,3},{3,4},{4,5},{5,6},{6,7},{7,0},{8,9},{9,10},{10,1... | collective-permute-start | bytes 602120 | tf_op jit(solution)/shard_map/ppermute | solution.py:314
  6.1 8.6 %collective-permute-done.halo = bf16[392,256]{1,0:T(8,128)(2,1)S(1)} collective-permute-done((bf16[392,256]{1,0:T(8,128)(2,1)S(1)}, bf16[392,256]{1,0:T(8,128)(2,1)S(1)}, u32[]{:S(2)}, u32[]{:S(2)}) %collective-permute-start) | collective-permute-done | bytes 200736 | tf_op jit(solution)/shard_map/ppermute | solution.py:314
  14.7 0.0 copy-start.4
  14.7 0.7 copy-done.4
  15.4 0.8 spread.1
  16.1 0.0 copy-start.5
  16.1 0.0 copy-start.6
  16.2 27.2 %all_to_all.20.got = bf16[32,72,256]{2,1,0:T(8,128)(2,1)S(1)} all-to-all(bf16[32,72,256]{2,1,0:T(8,128)(2,1)S(1)} %spread.1), channel_id=1, replica_groups=mesh['tm'=32,'row'=8] {'tm'}, dimensions={0} | all-to-all | bytes 2359296 | tf_op jit(solution)/shard_map/all_to_all | solution.py:326
  43.3 0.0 copy-done.5
  43.3 0.0 copy-done.6
  43.3 5.0 %cells.1 = bf16[32,8,3072]{2,1,0:T(8,128)(2,1)S(1)} custom-call(bf16[32,72,256]{2,1,0:T(8,128)(2,1)S(1)} %all_to_all.20.got, bf16[2304,256]{1,0:T(8,128)(2,1)S(1)} %bitcast.3, bf16[256,256]{1,0:T(8,128)(2,1)S(1)} %copy-done.6, f32[4,2,256]{2,1,0:T(2,128)S(1)} %constant_dynamic-slice_fusion.start, bf16[392,256]{1,0:T(8,128)(2,1)S(1)} %collective-permute-done.halo), custom_call_target="tpu_custom_call" | custom-call | flops 1409286144 | bytes 4194304 | tf_op jit(solution)/shard_map/cells/pallas_call | solution.py:327
  48.3 26.4 %all_to_all.21.got = bf16[32,8,3072]{2,1,0:T(8,128)(2,1)S(1)} all-to-all(bf16[32,8,3072]{2,1,0:T(8,128)(2,1)S(1)} %cells.1), channel_id=1, replica_groups=mesh['tm'=32,'row'=8] {'tm'}, dimensions={0} | all-to-all | bytes 3145728 | tf_op jit(solution)/shard_map/all_to_all | solution.py:347
  74.7 0.5 join.1
  75.2 0.0 copy-start.3
  75.2 0.0 copy-start.7
  75.2 13.2 %all_to_all.22.got = f32[8,8,320]{2,1,0:T(8,128)S(1)} all-to-all(f32[8,8,320]{2,1,0:T(8,128)S(1)} %get-tuple-element.8), channel_id=1, replica_groups=mesh['tm'=32,'row'=8] {'row'}, dimensions={0} | all-to-all | bytes 163840 | tf_op jit(solution)/shard_map/all_to_all | solution.py:356
  88.5 0.8 sum.1
  89.3 4.8 %all-to-all-start.3 = ((f32[32,8,320]{2,1,0:T(8,128)}), f32[32,8,320]{2,1,0:T(8,128)S(1)}, u32[]{:S(2)}, u32[]{:S(2)}) async-start(f32[32,8,320]{2,1,0:T(8,128)} %sum.1), calls=%async_computation.3 | async-start | bytes 786432 | tf_op jit(solution)/shard_map/all_to_all | solution.py:373
  94.1 0.1 collective-permute-start.1
  94.2 4.7 %collective-permute-done.1.below = bf16[2,2,64,256]{3,2,1,0:T(8,128)(2,1)S(1)} collective-permute-done((bf16[2,2,64,256]{3,2,1,0:T(8,128)(2,1)S(1)}, bf16[2,2,64,256]{3,2,1,0:T(8,128)(2,1)S(1)}, u32[]{:S(2)}, u32[]{:S(2)}) %collective-permute-start.1) | collective-permute-done | bytes 131104 | tf_op jit(solution)/shard_map/ppermute | solution.py:355
  98.9 0.0 copy-done.3
  98.9 0.0 copy-done.7
  98.9 2.4 %back.1 = bf16[2,4,64,256]{3,2,1,0:T(8,128)(2,1)} custom-call(bf16[2,4,64,256]{3,2,1,0:T(8,128)(2,1)S(1)} %get-tuple-element.7.drive, bf16[2,2,64,256]{3,2,1,0:T(8,128)(2,1)S(1)} %collective-permute-done.1.below, bf16[9,256,256]{2,1,0:T(8,128)(2,1)S(1)} %copy-done.5, bf16[2,4,64,256]{3,2,1,0:T(8,128)(2,1)S(1)} %copy-done.3, f32[1,256]{1,0:T(1,128)S(1)} %bitcast.4), custom_call_target="tpu_custom_call" | custom-call | flops 603979776 | bytes 2097152 | tf_op jit(solution)/shard_map/back/pallas_call | solution.py:361
  101.3 3.2 %all-to-all-done.3.got = f32[32,8,320]{2,1,0:T(8,128)S(1)} async-done(((f32[32,8,320]{2,1,0:T(8,128)}), f32[32,8,320]{2,1,0:T(8,128)S(1)}, u32[]{:S(2)}, u32[]{:S(2)}) %all-to-all-start.3) | async-done | bytes 327712 | tf_op jit(solution)/shard_map/all_to_all | solution.py:373
  104.5 0.9 last.1
  (3 shorter events, 0.1 us)
Async XLA Ops:
  0.6 1.0 copy-start
  1.6 0.9 copy-start.1
  2.5 0.9 copy-start.2
  3.5 11.2 %collective-permute-start = (bf16[392,256]{1,0:T(8,128)(2,1)S(1)}, bf16[392,256]{1,0:T(8,128)(2,1)S(1)}, u32[]{:S(2)}, u32[]{:S(2)}) collective-permute-start(bf16[392,256]{1,0:T(8,128)(2,1)S(1)} %halo.1), channel_id=1, source_target_pairs={{0,1},{1,2},{2,3},{3,4},{4,5},{5,6},{6,7},{7,0},{8,9},{9,10},{10,1... | collective-permute-start | bytes 602120 | tf_op jit(solution)/shard_map/ppermute | solution.py:314
  14.7 0.7 copy-start.4
  16.1 27.2 %copy-start.5 = (bf16[9,256,256]{2,1,0:T(8,128)(2,1)S(1)}, bf16[9,256,256]{2,1,0:T(8,128)(2,1)}, u32[]{:S(2)}) copy-start(bf16[9,256,256]{2,1,0:T(8,128)(2,1)} %kernel.1) | copy-start | bytes 3538948
  16.1 27.2 %copy-start.6 = (bf16[256,256]{1,0:T(8,128)(2,1)S(1)}, bf16[256,256]{1,0:T(8,128)(2,1)}, u32[]{:S(2)}) copy-start(bf16[256,256]{1,0:T(8,128)(2,1)} %readout.1) | copy-start | bytes 393220
  75.2 23.7 %copy-start.3 = (bf16[2,4,64,256]{3,2,1,0:T(8,128)(2,1)S(1)}, bf16[2,4,64,256]{3,2,1,0:T(8,128)(2,1)}, u32[]{:S(2)}) copy-start(bf16[2,4,64,256]{3,2,1,0:T(8,128)(2,1)} %cotangent.5) | copy-start | bytes 786436
  75.2 23.7 %copy-start.7 = (f32[256]{0:T(256)S(1)}, f32[256]{0:T(256)}, u32[]{:S(2)}) copy-start(f32[256]{0:T(256)} %param.11) | copy-start | bytes 3076
  89.3 15.2 %all-to-all-start.3 = ((f32[32,8,320]{2,1,0:T(8,128)}), f32[32,8,320]{2,1,0:T(8,128)S(1)}, u32[]{:S(2)}, u32[]{:S(2)}) async-start(f32[32,8,320]{2,1,0:T(8,128)} %sum.1), calls=%async_computation.3 | async-start | bytes 786432 | tf_op jit(solution)/shard_map/all_to_all | solution.py:373
  94.1 4.8 %collective-permute-start.1 = (bf16[2,2,64,256]{3,2,1,0:T(8,128)(2,1)S(1)}, bf16[2,2,64,256]{3,2,1,0:T(8,128)(2,1)S(1)}, u32[]{:S(2)}, u32[]{:S(2)}) collective-permute-start(bf16[2,2,64,256]{3,2,1,0:T(8,128)(2,1)S(1)} %slice.3), channel_id=1, source_target_pairs={{1,0},{2,1},{3,2},{4,3},{5,4},{6,5},{7,6},{0,7},{9,8},{10,9},{11,1... | collective-permute-start | bytes 393224 | tf_op jit(solution)/shard_map/ppermute | solution.py:355

commit v2 on v1

--- a/solution.py
+++ b/solution.py
@@ -15,19 +15,20 @@
 PAD = 8
 CELLS = ((0, 0), (0, 1), (2, 0), (2, 1), (1, 0), (1, 1), (3, 0), (3, 1))
 VMEM = pl.BlockSpec(memory_space=pltpu.VMEM)
-
-
-def call(body, name, outs, ins, scratch, flops=1 << 20, moved=1 << 20):
+HBM = pl.BlockSpec(memory_space=pltpu.MemorySpace.HBM)
+
+
+def call(body, name, outs, ins, scratch, flops=1 << 20, moved=1 << 20, grant=40 << 20):
     many = isinstance(outs, (list, tuple))
     return pl.pallas_call(
         body,
         name=name,
         out_shape=outs,
-        in_specs=[VMEM] * ins,
+        in_specs=ins,
         out_specs=[VMEM] * len(outs) if many else VMEM,
         scratch_shapes=scratch,
         cost_estimate=pl.CostEstimate(flops=flops, bytes_accessed=moved, transcendentals=0),
-        compiler_params=pltpu.CompilerParams(vmem_limit_bytes=40 << 20),
+        compiler_params=pltpu.CompilerParams(vmem_limit_bytes=grant),
     )
 
 
@@ -50,69 +51,85 @@
     )
 
 
-def halo_body(frames, cotangent, start, out, parts):
-    wide = frames.shape[2]
+def spread_body(frames, cotangent, decay, out, grid, slopes, rows, given, rates, parts, sems):
+    wide, lanes = frames.shape[2:]
+    copies = (
+        pltpu.make_async_copy(frames, rows, sems.at[0]),
+        pltpu.make_async_copy(cotangent, given, sems.at[1]),
+        pltpu.make_async_copy(decay, rates, sems.at[2]),
+    )
+    for copy in copies:
+        copy.start()
     for f in range(2):
-        for row in range(2):
-            out[pl.ds((2 * f + row) * wide, wide), :] = frames[f, 2 + row]
-        out[pl.ds((4 + f) * wide, wide), :] = cotangent[f, 3]
-    for place, piece in enumerate(split3(start[3])):
-        parts[pl.ds(2 * place, 2), :] = piece
-    parts[6:8, :] = jnp.zeros_like(parts[6:8, :])
-    out[pl.ds(6 * wide, 8), :] = parts[...].astype(BF)
-
-
-def spread_body(frames, cotangent, decay, halo, out, grid, slopes, parts):
-    wide = frames.shape[2]
+        for row in range(4):
+            grid[f, row, 0:PAD, :] = jnp.zeros((PAD, lanes), F32)
+            grid[f, row, PAD + wide :, :] = jnp.zeros((PAD, lanes), F32)
+    for copy in copies:
+        copy.wait()
     for f in range(2):
-        for row in range(6):
-            grid[f, row, 0:PAD, :] = jnp.zeros((PAD, grid.shape[3]), F32)
-            grid[f, row, PAD + wide :, :] = jnp.zeros((PAD, grid.shape[3]), F32)
-            source = halo[pl.ds((2 * f + row) * wide, wide), :] if row < 2 else frames[f, row - 2]
-            grid[f, row, PAD : PAD + wide, :] = source.astype(F32)
         for row in range(4):
-            source = halo[pl.ds((4 + f) * wide, wide), :] if row < 1 else cotangent[f, row - 1]
-            slopes[f, row, PAD : PAD + wide, :] = source.astype(F32)
-    for place, piece in enumerate(split3(decay[...])):
-        parts[pl.ds(2 * place, 2), :] = piece
-    parts[6:8, :] = jnp.zeros_like(parts[6:8, :])
-    rates = parts[...].astype(BF)
-    step = sublane((8, grid.shape[3]))
+            grid[f, row, PAD : PAD + wide, :] = rows[f, row].astype(F32)
+            slopes[f, row, PAD : PAD + wide, :] = given[f, row].astype(F32)
+    for place, piece in enumerate(split3(rates[...])):
+        parts[2 * place : 2 * place + 2, :] = piece
+    parts[6:8, :] = jnp.zeros((2, lanes), F32)
+    pieces = parts[...].astype(BF)
+    step = sublane((8, lanes))
     for target in range(wide // 2):
         first = PAD + 2 * target
+        for row in range(4):
+            start = first - 1
+            block = jnp.where(
+                step < 4, grid[0, row, start : start + 8, :], grid[1, row, start - 4 : start + 4, :]
+            )
+            out[target, 8 * row : 8 * row + 8, :] = block.astype(BF)
         for f in range(2):
-            for pair in range(3):
-                begin = first - 1
-                block = jnp.where(
-                    step < 4,
-                    grid[f, 2 * pair, begin : begin + 8, :],
-                    grid[f, 2 * pair + 1, begin - 4 : begin + 4, :],
-                )
-                out[target, 32 * f + 8 * pair : 32 * f + 8 * pair + 8, :] = block.astype(BF)
             block = slopes[f, 0, first : first + 8, :]
             for place, row in ((2, 2), (4, 1), (6, 3)):
                 block = jnp.where(step < place, block, slopes[f, row, first - place : first - place + 8, :])
-            out[target, 32 * f + 24 : 32 * f + 32, :] = block.astype(BF)
-        out[target, 64:72, :] = rates
+            out[target, 32 + 8 * f : 40 + 8 * f, :] = block.astype(BF)
+        out[target, 48:56, :] = pieces
 
 
 def cell_body(
-    got, kernel, readout, start, halo, out, grid, decay, gain, taps, driven, states, slopes, drive, turned, begin
+    got,
+    above,
+    below,
+    kernel,
+    readout,
+    start,
+    out,
+    grid,
+    decay,
+    gain,
+    taps,
+    driven,
+    states,
+    slopes,
+    drive,
+    turned,
+    starts,
+    sem,
 ):
     sources = got.shape[0]
     count = sources * 16
-    wide = (halo.shape[0] - 8) // 6
     lanes = got.shape[2]
     step = sublane((8, lanes))
-    is_first = lax.axis_index("row") == 0
-    low = jnp.where(is_first & (step < 2), 0.0, 1.0)
-    high = jnp.where(is_first & (step >= 4) & (step < 6), 0.0, 1.0)
     near = (step % 4) < 2
+    mine = lax.axis_index("tm")
+    fetch = pltpu.make_async_copy(start.at[:, pl.ds(pl.multiple_of(8 * (mine // 4), 8), 8)], starts, sem)
+    fetch.start()
 
     def unpack(source, _):
-        for f in range(2):
-            grid[2 * source + f] = got[source, 32 * f : 32 * f + 24, :].astype(F32)
-        piece = got[source, 64:72, :].astype(F32)
+        groups = [above[source], got[source, 0:8, :], got[source, 8:16, :]]
+        groups += [got[source, 16:24, :], got[source, 24:32, :], below[source]]
+        groups = [group.astype(F32) for group in groups]
+        for pair in range(3):
+            first, second = groups[2 * pair : 2 * pair + 2]
+            rows = slice(8 * pair, 8 * pair + 8)
+            grid[2 * source, rows, :] = jnp.where(step < 4, first, pltpu.roll(second, 4, 0))
+            grid[2 * source + 1, rows, :] = jnp.where(step < 4, pltpu.roll(first, 4, 0), second)
+        piece = got[source, 48:56, :].astype(F32)
         rate = piece + pltpu.roll(piece, 6, 0) + pltpu.roll(piece, 4, 0)
         decay[source] = rate
         gain[source] = jnp.sqrt(1.0 - rate * rate)
@@ -132,10 +149,6 @@
                         grid[2 * source + f, place : place + 8, :],
                         grid[2 * source + f, place + 6 : place + 14, :],
                     )
-                    if i == 2:
-                        value = value * low
-                    if i == 0:
-                        value = value * high
                     pair.append(value)
                 tap = 3 * i + j
                 taps[rows, lanes * tap : lanes * tap + lanes] = jnp.concatenate(pair, axis=0).astype(BF)
@@ -152,13 +165,11 @@
 
     lax.fori_loop(0, count // chunk, convolve, 0)
 
-    tail = halo[6 * wide : 6 * wide + 8, :].astype(F32)
-    begin[0:8, :] = tail
-    top = begin[0:2, :] + begin[2:4, :] + begin[4:6, :]
-    begin[0:2, :] = top
-    begin[2:4, :] = start[1]
-    begin[4:6, :] = start[0]
-    begin[6:8, :] = start[2]
+    fetch.wait()
+    offset = 2 * (mine % 4)
+    begin = pltpu.roll(starts[0], (8 - offset) % 8, 0)
+    for place, row in ((2, 2), (4, 1), (6, 3)):
+        begin = jnp.where(step < place, begin, pltpu.roll(starts[row], (8 + place - offset) % 8, 0))
 
     def advance(source, state):
         pair = []
@@ -171,14 +182,14 @@
         states[pl.ds(pl.multiple_of(16 * source, 16), 16), :] = jnp.concatenate(pair, axis=0).astype(BF)
         return state
 
-    lax.fori_loop(0, sources, advance, begin[...], unroll=4)
+    lax.fori_loop(0, sources, advance, begin, unroll=4)
 
     def mix(part, _):
         rows = pl.ds(pl.multiple_of(part * 64, 64), 64)
         mixture = jnp.dot(states[rows, :], readout[...], preferred_element_type=F32)
         upstream = jnp.concatenate(
             [
-                got[4 * part + source, 32 * f + 24 : 32 * f + 32, :].astype(F32)
+                got[4 * part + source, 32 + 8 * f : 40 + 8 * f, :].astype(F32)
                 for source in range(4)
                 for f in range(2)
             ],
@@ -219,7 +230,7 @@
     out[:, :, 9 * lanes : 10 * lanes] = term.astype(BF).reshape(sources, share, lanes)
 
 
-def join_body(bands, got, total, frames, cells, grid):
+def join_body(bands, got, total, frames, top, bottom, cells, grid):
     sources, share, width = got.shape
     lanes = width // 12
 
@@ -241,26 +252,28 @@
             for place, (row, column) in enumerate(CELLS):
                 grid[pl.ds(column, sources, stride=2), :] = cells[pl.ds(place, sources, stride=8), :]
                 if column == 1:
-                    frames[f, row, :, 128 * part : 128 * part + 128] = grid[...].astype(BF)
-
-
-def back_body(bands, drive, below, kernel, cotangent, feedthrough, out, grid, moved):
+                    value = grid[...].astype(BF)
+                    frames[f, row, :, 128 * part : 128 * part + 128] = value
+                    if row == 0:
+                        top[f, :, 128 * part : 128 * part + 128] = value
+                    if row == 3:
+                        bottom[f, :, 128 * part : 128 * part + 128] = value
+
+
+def back_body(drive, above, below, kernel, cotangent, feedthrough, out, grid, moved):
     wide = drive.shape[2]
     lanes = drive.shape[3]
-    band = lax.axis_index("row")
     for row in range(6):
-        keep = None
-        if row == 0:
-            keep = jnp.where(band == 0, 0.0, 1.0)
-        if row == 5:
-            keep = jnp.where(band == bands - 1, 0.0, 1.0)
         for f in range(2):
-            source = (drive[f, row] if row < 4 else below[f, row - 4]).astype(F32)
-            if keep is not None:
-                source = source * keep
+            if row == 0:
+                source = above[f]
+            elif row == 5:
+                source = below[f]
+            else:
+                source = drive[f, row - 1]
             grid[0:PAD, :] = jnp.zeros((PAD, lanes), F32)
             grid[PAD + wide :, :] = jnp.zeros((PAD, lanes), F32)
-            grid[PAD : PAD + wide, :] = source
+            grid[PAD : PAD + wide, :] = source.astype(F32)
             for shift in range(3):
                 moved[shift, f, row] = grid[PAD - 1 + shift : PAD - 1 + shift + wide, :].astype(BF)
     for f in range(2):
@@ -304,31 +317,33 @@
     share = lanes // sources
     block = lanes // bands
     shape = jax.ShapeDtypeStruct
-    down = [(i, (i + 1) % bands) for i in range(bands)]
-    up = [((i + 1) % bands, i) for i in range(bands)]
-
-    start = lax.dynamic_slice_in_dim(start_state, 2 * lax.axis_index("tm"), 2, 1)
-    edge = call(
-        halo_body, "halo", shape((6 * wide + 8, lanes), BF), 3, [pltpu.VMEM((8, lanes), F32)]
-    )(frames_in, cotangent, start)
-    edge = lax.ppermute(edge, "row", down)
+    down = [(i, i + 1) for i in range(bands - 1)]
+    up = [(i + 1, i) for i in range(bands - 1)]
+
     send = call(
         spread_body,
         "spread",
-        shape((sources, 72, lanes), BF),
-        4,
+        shape((sources, 56, lanes), BF),
+        [HBM] * 3,
         [
-            pltpu.VMEM((2, 6, wide + 2 * PAD, lanes), F32),
             pltpu.VMEM((2, 4, wide + 2 * PAD, lanes), F32),
+            pltpu.VMEM((2, 4, wide + 2 * PAD, lanes), F32),
+            pltpu.VMEM((2, 4, wide, lanes), BF),
+            pltpu.VMEM((2, 4, wide, lanes), BF),
+            pltpu.VMEM((2, lanes), F32),
             pltpu.VMEM((8, lanes), F32),
+            pltpu.SemaphoreType.DMA((3,)),
         ],
-    )(frames_in, cotangent, decay_rate, edge)
+        grant=63 << 20,
+    )(frames_in, cotangent, decay_rate)
     got = lax.all_to_all(send, "tm", 0, 0)
+    above = lax.ppermute(got[:, 24:32], "row", down)
+    below = lax.ppermute(got[:, 0:8], "row", up)
     send = call(
         cell_body,
         "cells",
         shape((sources, max(8, share), 12 * lanes), BF),
-        5,
+        [VMEM] * 5 + [HBM],
         [
             pltpu.VMEM((2 * sources, 24, lanes), F32),
             pltpu.VMEM((sources, 8, lanes), F32),
@@ -339,40 +354,44 @@
             pltpu.VMEM((cells, lanes), BF),
             pltpu.VMEM((cells, lanes), F32),
             pltpu.VMEM((lanes, cells), BF),
-            pltpu.VMEM((8, lanes), F32),
+            pltpu.VMEM((4, 8, lanes), F32),
+            pltpu.SemaphoreType.DMA,
         ],
         flops=2 * cells * lanes * lanes * 21,
         moved=4 << 20,
-    )(got, kernel.reshape(9 * lanes, lanes), readout, start, edge)
+    )(got, above, below, kernel.reshape(9 * lanes, lanes), readout, start_state)
     got = lax.all_to_all(send, "tm", 0, 0)
-    partial, drive = call(
+    edge = shape((2, wide, lanes), BF)
+    partial, drive, top, bottom = call(
         functools.partial(join_body, bands),
         "join",
-        (shape((bands, share, 10 * block), F32), shape((2, 4, wide, lanes), BF)),
-        1,
+        (shape((bands, share, 10 * block), F32), shape((2, 4, wide, lanes), BF), edge, edge),
+        [VMEM],
         [pltpu.VMEM((8 * sources, 128), F32), pltpu.VMEM((wide, 128), F32)],
     )(got)
-    below = lax.ppermute(drive[:, :2], "row", up)
+    above = lax.ppermute(bottom, "row", down)
+    below = lax.ppermute(top, "row", up)
     partial = lax.all_to_all(partial, "row", 0, 0)
+    partial, above, below = lax.optimization_barrier((partial, above, below))
     scaling = 1.0 / math.sqrt(here * sources * band_rows * bands * wide)
     partial = call(
-        functools.partial(sum_body, scaling), "sum", shape((sources, share, 10 * block), F32), 1, []
+        functools.partial(sum_body, scaling), "sum", shape((sources, share, 10 * block), F32), [VMEM], []
     )(partial)
     grad_frames = call(
-        functools.partial(back_body, bands),
+        back_body,
         "back",
         shape(frames_in.shape, BF),
-        5,
+        [VMEM] * 6,
         [
             pltpu.VMEM((wide + 2 * PAD, lanes), F32),
             pltpu.VMEM((3, 2, 6, wide, lanes), BF),
         ],
         flops=2 * cells * lanes * lanes * 9,
         moved=2 << 20,
-    )(drive, below, kernel, cotangent, feedthrough.reshape(1, lanes))
+    )(drive, above, below, kernel, cotangent, feedthrough.reshape(1, lanes))
     whole = lax.all_to_all(partial, "tm", 0, 0)
     grad_kernel, grad_readout = call(
-        last_body, "last", (shape((9, block, lanes), F32), shape((block, lanes), F32)), 1, []
+        last_body, "last", (shape((9, block, lanes), F32), shape((block, lanes), F32)), [VMEM], []
     )(whole)
     return grad_frames, grad_kernel, grad_readout.T
 

time: 106 us -> 106 us (level)
  starting transfers between devices: 7.42 us -> 25.4 us
  blocking collectives: 66.8 us -> 51.3 us
  local copies, waits for them, and re-layouts: 3.56 us -> 0.04 us
  Pallas kernels: 10.3 us -> 12.9 us
  waiting for transfers between devices: 16.5 us -> 14.6 us
    all_to_all x1 -> x0, blocking collectives: 13.2 us -> none  [local(): partial = lax.all_to_all(partial, 'row', 0, 0)]
    all_to_all x0 -> x1, starting transfers between devices: none -> 9.97 us  [local(): partial = lax.all_to_all(partial, 'row', 0, 0)]
    ppermute x2 -> x4, starting transfers between devices: 2.61 us -> 10.1 us  [the longest x1 4.18 us: local(): above = lax.ppermute(got[:, 24:32], 'row', down)]
    ppermute x2 -> x4, waiting for transfers between devices: 13.3 us -> 6.74 us  [the longest x1 3.54 us: local(): below = lax.ppermute(top, 'row', up)]
    all_to_all x1, waiting for transfers between devices: 3.17 us -> 7.87 us  [local(): whole = lax.all_to_all(partial, 'tm', 0, 0)]
    unnamed x16 -> x10, local copies, waits for them, and re-layouts: 3.54 us -> 0.02 us
    all_to_all x2, blocking collectives: 53.6 us -> 51.3 us  [local(): got = lax.all_to_all(send, 'tm', 0, 0)]
    pallas_call x3 -> x2, Pallas kernels: 3.2 us -> 5 us  [the longest x1 2.61 us: local(): call(spread_body, 'spread', shape((sources, 56, lanes), BF), [HBM] * 3, [...]
  transfers between devices with their start and end apart: 3 -> 6, of which waited for: 3 -> 5; matrix products, arithmetic and copies ran while one was open for 0% -> 0% of each run, Pallas kernels for 2% -> 2%
where the time goes in v2:
time: 106 us; the launch traced here: 105 us
  blocking collectives  51.3 us (48%)
  starting transfers between devices  25.4 us (24%)
  waiting for transfers between devices  14.6 us (14%)
  Pallas kernels  12.9 us (12%)
    all_to_all x2, blocking collectives, local(): got = lax.all_to_all(send, 'tm', 0, 0)  51.3 us
    all_to_all x1, starting transfers between devices, local(): partial = lax.all_to_all(partial, 'row', 0, 0)  9.97 us
    all_to_all x1, waiting for transfers between devices, local(): whole = lax.all_to_all(partial, 'tm', 0, 0)  7.87 us
    all_to_all x1, starting transfers between devices, local(): whole = lax.all_to_all(partial, 'tm', 0, 0)  5.31 us
    pallas_call x1, Pallas kernels, local(): call(cell_body, 'cells', shape((sources, max(8, share), 12 * lanes), BF),...  5.04 us
    ppermute x1, starting transfers between devices, local(): above = lax.ppermute(got[:, 24:32], 'row', down)  4.18 us
    ppermute x1, waiting for transfers between devices, local(): below = lax.ppermute(top, 'row', up)  3.54 us
    ppermute x1, starting transfers between devices, local(): above = lax.ppermute(bottom, 'row', down)  3.36 us
  transfers between devices with their start and end apart: 6, of which 5 were waited for; matrix products, arithmetic and copies ran while one was open for 0% of the time, Pallas kernels for 2%

profile of v2, /device:TPU:1, one launch (start us, length us, event | category | flops | bytes accessed | tf_op | source)
XLA Modules:
  0.0 105.0 jit_solution(346651976578439791)
XLA Ops:
  0.6 0.0 copy-start.2
  0.6 0.0 copy-start.3
  0.7 2.6 %spread.1 = bf16[32,56,256]{2,1,0:T(8,128)(2,1)} custom-call(bf16[2,4,64,256]{3,2,1,0:T(8,128)(2,1)} %frames.1, bf16[2,4,64,256]{3,2,1,0:T(8,128)(2,1)} %cotangent.3, f32[2,256]{1,0:T(2,128)} %decay.1), custom_call_target="tpu_custom_call" | custom-call | flops 1048576 | bytes 1048576 | tf_op jit(solution)/shard_map/spread/pallas_call | solution.py:323
  3.3 0.0 copy-start.1
  3.3 24.3 %all_to_all.20.got = bf16[32,56,256]{2,1,0:T(8,128)(2,1)S(1)} all-to-all(bf16[32,56,256]{2,1,0:T(8,128)(2,1)} %spread.1), channel_id=1, replica_groups=mesh['tm'=32,'row'=8] {'tm'}, dimensions={0} | all-to-all | bytes 1835008 | tf_op jit(solution)/shard_map/all_to_all | solution.py:339
  27.6 1.3 %collective-permute-start.1 = (bf16[32,8,256]{2,1,0:T(8,128)(2,1)S(1)}, bf16[32,8,256]{2,1,0:T(8,128)(2,1)S(1)}, u32[]{:S(2)}, u32[]{:S(2)}) collective-permute-start(bf16[32,8,256]{2,1,0:T(8,128)(2,1)S(1)} %get-tuple-element.21), channel_id=1, source_target_pairs={{1,0},{2,1},{3,2},{4,3},{5,4},{6,5},{7,6},{9,8},{10,9},{11,10},{12... | collective-permute-start | bytes 393224 | tf_op jit(solution)/shard_map/ppermute | solution.py:341
  28.9 4.2 %collective-permute-start = (bf16[32,8,256]{2,1,0:T(8,128)(2,1)S(1)}, bf16[32,8,256]{2,1,0:T(8,128)(2,1)S(1)}, u32[]{:S(2)}, u32[]{:S(2)}) collective-permute-start(bf16[32,8,256]{2,1,0:T(8,128)(2,1)S(1)} %get-tuple-element.22), channel_id=1, source_target_pairs={{0,1},{1,2},{2,3},{3,4},{4,5},{5,6},{6,7},{8,9},{9,10},{10,11},{11... | collective-permute-start | bytes 393224 | tf_op jit(solution)/shard_map/ppermute | solution.py:340
  33.1 1.8 %collective-permute-done.1.below = bf16[32,8,256]{2,1,0:T(8,128)(2,1)S(1)} collective-permute-done((bf16[32,8,256]{2,1,0:T(8,128)(2,1)S(1)}, bf16[32,8,256]{2,1,0:T(8,128)(2,1)S(1)}, u32[]{:S(2)}, u32[]{:S(2)}) %collective-permute-start.1) | collective-permute-done | bytes 131104 | tf_op jit(solution)/shard_map/ppermute | solution.py:341
  34.9 0.9 collective-permute-done.above
  35.8 0.0 copy-done.2
  35.8 0.0 copy-done.3
  35.8 0.0 copy-done.1
  35.8 5.0 %cells.1 = bf16[32,8,3072]{2,1,0:T(8,128)(2,1)S(1)} custom-call(bf16[32,56,256]{2,1,0:T(8,128)(2,1)S(1)} %all_to_all.20.got, bf16[32,8,256]{2,1,0:T(8,128)(2,1)S(1)} %collective-permute-done.above, bf16[32,8,256]{2,1,0:T(8,128)(2,1)S(1)} %collective-permute-done.1.below, bf16[2304,256]{1,0:T(8,128)(2,1)S(1)} %bitcast.3, bf16[256,256]{1,0:T(8,128)(2,1)S(1)} %copy-done.3, ...), custom_call_target="tpu_custom_call" | custom-call | flops 1409286144 | bytes 4194304 | tf_op jit(solution)/shard_map/cells/pallas_call | solution.py:342
  40.8 27.1 %all_to_all.21.got = bf16[32,8,3072]{2,1,0:T(8,128)(2,1)S(1)} all-to-all(bf16[32,8,3072]{2,1,0:T(8,128)(2,1)S(1)} %cells.1), channel_id=1, replica_groups=mesh['tm'=32,'row'=8] {'tm'}, dimensions={0} | all-to-all | bytes 3145728 | tf_op jit(solution)/shard_map/all_to_all | solution.py:363
  67.9 0.0 copy-start
  67.9 0.0 copy-start.4
  67.9 1.2 %join.1 = (f32[8,8,320]{2,1,0:T(8,128)}, bf16[2,4,64,256]{3,2,1,0:T(8,128)(2,1)S(1)}, bf16[2,64,256]{2,1,0:T(8,128)(2,1)S(1)}, bf16[2,64,256]{2,1,0:T(8,128)(2,1)S(1)}) custom-call(bf16[32,8,3072]{2,1,0:T(8,128)(2,1)S(1)} %all_to_all.21.got), custom_call_target="tpu_custom_call" | custom-call | flops 1048576 | bytes 1048576 | tf_op jit(solution)/shard_map/join/pallas_call | solution.py:365
  69.1 10.0 %all-to-all-start.2 = ((f32[8,8,320]{2,1,0:T(8,128)}), f32[8,8,320]{2,1,0:T(8,128)S(1)}, u32[]{:S(2)}, u32[]{:S(2)}) async-start(f32[8,8,320]{2,1,0:T(8,128)} %get-tuple-element.13), calls=%async_computation.2 | async-start | bytes 196608 | tf_op jit(solution)/shard_map/all_to_all | solution.py:374
  79.0 3.4 %collective-permute-start.2 = (bf16[2,64,256]{2,1,0:T(8,128)(2,1)S(1)}, bf16[2,64,256]{2,1,0:T(8,128)(2,1)S(1)}, u32[]{:S(2)}, u32[]{:S(2)}) collective-permute-start(bf16[2,64,256]{2,1,0:T(8,128)(2,1)S(1)} %get-tuple-element.14), channel_id=1, source_target_pairs={{0,1},{1,2},{2,3},{3,4},{4,5},{5,6},{6,7},{8,9},{9,10},{10,11},{11... | collective-permute-start | bytes 196616 | tf_op jit(solution)/shard_map/ppermute | solution.py:372
  82.4 1.3 %collective-permute-start.3 = (bf16[2,64,256]{2,1,0:T(8,128)(2,1)S(1)}, bf16[2,64,256]{2,1,0:T(8,128)(2,1)S(1)}, u32[]{:S(2)}, u32[]{:S(2)}) collective-permute-start(bf16[2,64,256]{2,1,0:T(8,128)(2,1)S(1)} %get-tuple-element.15), channel_id=1, source_target_pairs={{1,0},{2,1},{3,2},{4,3},{5,4},{6,5},{7,6},{9,8},{10,9},{11,10},{12... | collective-permute-start | bytes 196616 | tf_op jit(solution)/shard_map/ppermute | solution.py:373
  83.7 0.5 collective-permute-done.2.above
  84.2 3.5 %collective-permute-done.3.below = bf16[2,64,256]{2,1,0:T(8,128)(2,1)S(1)} collective-permute-done((bf16[2,64,256]{2,1,0:T(8,128)(2,1)S(1)}, bf16[2,64,256]{2,1,0:T(8,128)(2,1)S(1)}, u32[]{:S(2)}, u32[]{:S(2)}) %collective-permute-start.3) | collective-permute-done | bytes 65568 | tf_op jit(solution)/shard_map/ppermute | solution.py:373
  87.7 0.0 all-to-all-done.2.got
  87.7 0.8 sum.1
  88.5 5.3 %all-to-all-start.3 = ((f32[32,8,320]{2,1,0:T(8,128)}), f32[32,8,320]{2,1,0:T(8,128)S(1)}, u32[]{:S(2)}, u32[]{:S(2)}) async-start(f32[32,8,320]{2,1,0:T(8,128)} %sum.1), calls=%async_computation.3 | async-start | bytes 786432 | tf_op jit(solution)/shard_map/all_to_all | solution.py:392
  93.8 0.0 copy-done
  93.8 0.0 copy-done.4
  93.8 2.4 %back.1 = bf16[2,4,64,256]{3,2,1,0:T(8,128)(2,1)} custom-call(bf16[2,4,64,256]{3,2,1,0:T(8,128)(2,1)S(1)} %get-tuple-element.12.drive, bf16[2,64,256]{2,1,0:T(8,128)(2,1)S(1)} %collective-permute-done.2.above, bf16[2,64,256]{2,1,0:T(8,128)(2,1)S(1)} %collective-permute-done.3.below, bf16[9,256,256]{2,1,0:T(8,128)(2,1)S(1)} %copy-done.1, ...), custom_call_target="tpu_custom_call" | custom-call | flops 603979776 | bytes 2097152 | tf_op jit(solution)/shard_map/back/pallas_call | solution.py:380
  96.2 7.9 %all-to-all-done.3.got = f32[32,8,320]{2,1,0:T(8,128)S(1)} async-done(((f32[32,8,320]{2,1,0:T(8,128)}), f32[32,8,320]{2,1,0:T(8,128)S(1)}, u32[]{:S(2)}, u32[]{:S(2)}) %all-to-all-start.3) | async-done | bytes 327712 | tf_op jit(solution)/shard_map/all_to_all | solution.py:392
  104.1 0.9 last.1
  (1 shorter events, 0.0 us)
Async XLA Ops:
  0.6 35.2 %copy-start.2 = (f32[4,64,256]{2,1,0:T(8,128)S(1)}, f32[4,64,256]{2,1,0:T(8,128)}, u32[]{:S(2)}) copy-start(f32[4,64,256]{2,1,0:T(8,128)} %start.1) | copy-start | bytes 786436
  0.6 35.1 %copy-start.3 = (bf16[256,256]{1,0:T(8,128)(2,1)S(1)}, bf16[256,256]{1,0:T(8,128)(2,1)}, u32[]{:S(2)}) copy-start(bf16[256,256]{1,0:T(8,128)(2,1)} %readout.1) | copy-start | bytes 393220
  3.3 32.5 %copy-start.1 = (bf16[9,256,256]{2,1,0:T(8,128)(2,1)S(1)}, bf16[9,256,256]{2,1,0:T(8,128)(2,1)}, u32[]{:S(2)}) copy-start(bf16[9,256,256]{2,1,0:T(8,128)(2,1)} %kernel.1) | copy-start | bytes 3538948
  27.6 7.3 %collective-permute-start.1 = (bf16[32,8,256]{2,1,0:T(8,128)(2,1)S(1)}, bf16[32,8,256]{2,1,0:T(8,128)(2,1)S(1)}, u32[]{:S(2)}, u32[]{:S(2)}) collective-permute-start(bf16[32,8,256]{2,1,0:T(8,128)(2,1)S(1)} %get-tuple-element.21), channel_id=1, source_target_pairs={{1,0},{2,1},{3,2},{4,3},{5,4},{6,5},{7,6},{9,8},{10,9},{11,10},{12... | collective-permute-start | bytes 393224 | tf_op jit(solution)/shard_map/ppermute | solution.py:341
  28.9 6.9 %collective-permute-start = (bf16[32,8,256]{2,1,0:T(8,128)(2,1)S(1)}, bf16[32,8,256]{2,1,0:T(8,128)(2,1)S(1)}, u32[]{:S(2)}, u32[]{:S(2)}) collective-permute-start(bf16[32,8,256]{2,1,0:T(8,128)(2,1)S(1)} %get-tuple-element.22), channel_id=1, source_target_pairs={{0,1},{1,2},{2,3},{3,4},{4,5},{5,6},{6,7},{8,9},{9,10},{10,11},{11... | collective-permute-start | bytes 393224 | tf_op jit(solution)/shard_map/ppermute | solution.py:340
  67.9 25.9 %copy-start = (bf16[2,4,64,256]{3,2,1,0:T(8,128)(2,1)S(1)}, bf16[2,4,64,256]{3,2,1,0:T(8,128)(2,1)}, u32[]{:S(2)}) copy-start(bf16[2,4,64,256]{3,2,1,0:T(8,128)(2,1)} %cotangent.3) | copy-start | bytes 786436
  67.9 25.9 %copy-start.4 = (f32[256]{0:T(256)S(1)}, f32[256]{0:T(256)}, u32[]{:S(2)}) copy-start(f32[256]{0:T(256)} %param.11) | copy-start | bytes 3076
  69.1 18.6 %all-to-all-start.2 = ((f32[8,8,320]{2,1,0:T(8,128)}), f32[8,8,320]{2,1,0:T(8,128)S(1)}, u32[]{:S(2)}, u32[]{:S(2)}) async-start(f32[8,8,320]{2,1,0:T(8,128)} %get-tuple-element.13), calls=%async_computation.2 | async-start | bytes 196608 | tf_op jit(solution)/shard_map/all_to_all | solution.py:374
  79.0 5.1 %collective-permute-start.2 = (bf16[2,64,256]{2,1,0:T(8,128)(2,1)S(1)}, bf16[2,64,256]{2,1,0:T(8,128)(2,1)S(1)}, u32[]{:S(2)}, u32[]{:S(2)}) collective-permute-start(bf16[2,64,256]{2,1,0:T(8,128)(2,1)S(1)} %get-tuple-element.14), channel_id=1, source_target_pairs={{0,1},{1,2},{2,3},{3,4},{4,5},{5,6},{6,7},{8,9},{9,10},{10,11},{11... | collective-permute-start | bytes 196616 | tf_op jit(solution)/shard_map/ppermute | solution.py:372
  82.4 5.3 %collective-permute-start.3 = (bf16[2,64,256]{2,1,0:T(8,128)(2,1)S(1)}, bf16[2,64,256]{2,1,0:T(8,128)(2,1)S(1)}, u32[]{:S(2)}, u32[]{:S(2)}) collective-permute-start(bf16[2,64,256]{2,1,0:T(8,128)(2,1)S(1)} %get-tuple-element.15), channel_id=1, source_target_pairs={{1,0},{2,1},{3,2},{4,3},{5,4},{6,5},{7,6},{9,8},{10,9},{11,10},{12... | collective-permute-start | bytes 196616 | tf_op jit(solution)/shard_map/ppermute | solution.py:373
  88.5 15.6 %all-to-all-start.3 = ((f32[32,8,320]{2,1,0:T(8,128)}), f32[32,8,320]{2,1,0:T(8,128)S(1)}, u32[]{:S(2)}, u32[]{:S(2)}) async-start(f32[32,8,320]{2,1,0:T(8,128)} %sum.1), calls=%async_computation.3 | async-start | bytes 786432 | tf_op jit(solution)/shard_map/all_to_all | solution.py:392

commit v3 on v2

--- a/solution.py
+++ b/solution.py
@@ -242,7 +242,7 @@
     for band in range(bands):
         total[band] = jnp.concatenate(
             [sums[:, lanes * k + block * band : lanes * k + block * band + block] for k in range(10)], axis=1
-        )
+        ).astype(BF)
 
     for f in range(2):
         for part in range(lanes // 128):
@@ -293,17 +293,17 @@
 
 
 def sum_body(scaling, got, out):
-    total = got[0]
+    total = got[0].astype(F32)
     for band in range(1, got.shape[0]):
-        total = total + got[band]
-    total = total * scaling
+        total = total + got[band].astype(F32)
+    total = (total * scaling).astype(BF)
     for target in range(out.shape[0]):
         out[target] = total
 
 
 def last_body(got, kernel_out, readout_out):
     sources, share, width = got.shape
-    turned = got[...].reshape(sources * share, width).T
+    turned = got[...].astype(F32).reshape(sources * share, width).T
     block = width // 10
     for k in range(9):
         kernel_out[k] = turned[block * k : block * k + block]
@@ -365,17 +365,16 @@
     partial, drive, top, bottom = call(
         functools.partial(join_body, bands),
         "join",
-        (shape((bands, share, 10 * block), F32), shape((2, 4, wide, lanes), BF), edge, edge),
+        (shape((bands, share, 10 * block), BF), shape((2, 4, wide, lanes), BF), edge, edge),
         [VMEM],
         [pltpu.VMEM((8 * sources, 128), F32), pltpu.VMEM((wide, 128), F32)],
     )(got)
     above = lax.ppermute(bottom, "row", down)
     below = lax.ppermute(top, "row", up)
     partial = lax.all_to_all(partial, "row", 0, 0)
-    partial, above, below = lax.optimization_barrier((partial, above, below))
     scaling = 1.0 / math.sqrt(here * sources * band_rows * bands * wide)
     partial = call(
-        functools.partial(sum_body, scaling), "sum", shape((sources, share, 10 * block), F32), [VMEM], []
+        functools.partial(sum_body, scaling), "sum", shape((sources, share, 10 * block), BF), [VMEM], []
     )(partial)
     grad_frames = call(
         back_body,

time: 106 us -> 102 us (0.962)
  blocking collectives: 51.3 us -> 68.2 us
  starting transfers between devices: 25.4 us -> 14 us
  waiting for transfers between devices: 14.6 us -> 6.74 us
    all_to_all x0 -> x1, blocking collectives: none -> 16.8 us  [local(): partial = lax.all_to_all(partial, 'row', 0, 0)]
    all_to_all x1 -> x0, starting transfers between devices: 9.97 us -> none  [local(): partial = lax.all_to_all(partial, 'row', 0, 0)]
    all_to_all x1, waiting for transfers between devices: 7.87 us -> 0.01 us  [local(): whole = lax.all_to_all(partial, 'tm', 0, 0)]
    ppermute x1, starting transfers between devices: 3.36 us -> 2.19 us  [local(): above = lax.ppermute(bottom, 'row', down)]
  transfers between devices with their start and end apart: 6 -> 5, of which waited for: 5 -> 3; matrix products, arithmetic and copies ran while one was open for 0% -> 0% of each run, Pallas kernels for 2% -> 2%
where the time goes in v3:
time: 102 us
  blocking collectives  68.2 us (67%)
  starting transfers between devices  14 us (14%)
  Pallas kernels  12.1 us (12%)
  waiting for transfers between devices  6.74 us (7%)
    all_to_all x2, blocking collectives, local(): got = lax.all_to_all(send, 'tm', 0, 0)  51.3 us
    all_to_all x1, blocking collectives, local(): partial = lax.all_to_all(partial, 'row', 0, 0)  16.8 us
    all_to_all x1, starting transfers between devices, local(): whole = lax.all_to_all(partial, 'tm', 0, 0)  5.05 us
    pallas_call x1, Pallas kernels, local(): call(cell_body, 'cells', shape((sources, max(8, share), 12 * lanes), BF),...  5.04 us
    ppermute x1, starting transfers between devices, local(): above = lax.ppermute(got[:, 24:32], 'row', down)  4.18 us
    ppermute x1, waiting for transfers between devices, local(): below = lax.ppermute(top, 'row', up)  3.99 us
    pallas_call x1, Pallas kernels, local(): call(spread_body, 'spread', shape((sources, 56, lanes), BF), [HBM] * 3, [...  2.61 us
    pallas_call x1, Pallas kernels, local(): call(back_body, 'back', shape(frames_in.shape, BF), [VMEM] * 6, [pltpu.VM...  2.38 us
  transfers between devices with their start and end apart: 5, of which 3 were waited for; matrix products, arithmetic and copies ran while one was open for 0% of the time, Pallas kernels for 2%

profile of v3, /device:TPU:1, one launch (start us, length us, event | category | flops | bytes accessed | tf_op | source)
XLA Modules:
  0.0 101.7 jit_solution(111332649874984909)
XLA Ops:
  0.6 0.0 copy-start.2
  0.6 0.0 copy-start.3
  0.7 2.6 %spread.1 = bf16[32,56,256]{2,1,0:T(8,128)(2,1)} custom-call(bf16[2,4,64,256]{3,2,1,0:T(8,128)(2,1)} %frames.1, bf16[2,4,64,256]{3,2,1,0:T(8,128)(2,1)} %cotangent.3, f32[2,256]{1,0:T(2,128)} %decay.1), custom_call_target="tpu_custom_call" | custom-call | flops 1048576 | bytes 1048576 | tf_op jit(solution)/shard_map/spread/pallas_call | solution.py:323
  3.3 0.0 copy-start.1
  3.3 24.3 %all_to_all.20.got = bf16[32,56,256]{2,1,0:T(8,128)(2,1)S(1)} all-to-all(bf16[32,56,256]{2,1,0:T(8,128)(2,1)} %spread.1), channel_id=1, replica_groups=mesh['tm'=32,'row'=8] {'tm'}, dimensions={0} | all-to-all | bytes 1835008 | tf_op jit(solution)/shard_map/all_to_all | solution.py:339
  27.6 1.3 %collective-permute-start.1 = (bf16[32,8,256]{2,1,0:T(8,128)(2,1)S(1)}, bf16[32,8,256]{2,1,0:T(8,128)(2,1)S(1)}, u32[]{:S(2)}, u32[]{:S(2)}) collective-permute-start(bf16[32,8,256]{2,1,0:T(8,128)(2,1)S(1)} %get-tuple-element.15), channel_id=1, source_target_pairs={{1,0},{2,1},{3,2},{4,3},{5,4},{6,5},{7,6},{9,8},{10,9},{11,10},{12... | collective-permute-start | bytes 393224 | tf_op jit(solution)/shard_map/ppermute | solution.py:341
  28.9 4.2 %collective-permute-start = (bf16[32,8,256]{2,1,0:T(8,128)(2,1)S(1)}, bf16[32,8,256]{2,1,0:T(8,128)(2,1)S(1)}, u32[]{:S(2)}, u32[]{:S(2)}) collective-permute-start(bf16[32,8,256]{2,1,0:T(8,128)(2,1)S(1)} %get-tuple-element.16), channel_id=1, source_target_pairs={{0,1},{1,2},{2,3},{3,4},{4,5},{5,6},{6,7},{8,9},{9,10},{10,11},{11... | collective-permute-start | bytes 393224 | tf_op jit(solution)/shard_map/ppermute | solution.py:340
  33.0 1.8 %collective-permute-done.1.below = bf16[32,8,256]{2,1,0:T(8,128)(2,1)S(1)} collective-permute-done((bf16[32,8,256]{2,1,0:T(8,128)(2,1)S(1)}, bf16[32,8,256]{2,1,0:T(8,128)(2,1)S(1)}, u32[]{:S(2)}, u32[]{:S(2)}) %collective-permute-start.1) | collective-permute-done | bytes 131104 | tf_op jit(solution)/shard_map/ppermute | solution.py:341
  34.9 0.9 collective-permute-done.above
  35.8 0.0 copy-done.2
  35.8 0.0 copy-done.3
  35.8 0.0 copy-done.1
  35.8 5.0 %cells.1 = bf16[32,8,3072]{2,1,0:T(8,128)(2,1)S(1)} custom-call(bf16[32,56,256]{2,1,0:T(8,128)(2,1)S(1)} %all_to_all.20.got, bf16[32,8,256]{2,1,0:T(8,128)(2,1)S(1)} %collective-permute-done.above, bf16[32,8,256]{2,1,0:T(8,128)(2,1)S(1)} %collective-permute-done.1.below, bf16[2304,256]{1,0:T(8,128)(2,1)S(1)} %bitcast.3, bf16[256,256]{1,0:T(8,128)(2,1)S(1)} %copy-done.3, ...), custom_call_target="tpu_custom_call" | custom-call | flops 1409286144 | bytes 4194304 | tf_op jit(solution)/shard_map/cells/pallas_call | solution.py:342
  40.8 27.1 %all_to_all.21.got = bf16[32,8,3072]{2,1,0:T(8,128)(2,1)S(1)} all-to-all(bf16[32,8,3072]{2,1,0:T(8,128)(2,1)S(1)} %cells.1), channel_id=1, replica_groups=mesh['tm'=32,'row'=8] {'tm'}, dimensions={0} | all-to-all | bytes 3145728 | tf_op jit(solution)/shard_map/all_to_all | solution.py:363
  67.9 0.0 copy-start
  67.9 0.0 copy-start.4
  67.9 0.5 join.1
  68.4 16.8 %all_to_all.22.got = bf16[8,8,320]{2,1,0:T(8,128)(2,1)S(1)} all-to-all(bf16[8,8,320]{2,1,0:T(8,128)(2,1)S(1)} %get-tuple-element.12), channel_id=1, replica_groups=mesh['tm'=32,'row'=8] {'row'}, dimensions={0} | all-to-all | bytes 81920 | tf_op jit(solution)/shard_map/all_to_all | solution.py:374
  85.2 0.7 sum.1
  85.9 5.0 %all-to-all-start.3 = ((bf16[32,8,320]{2,1,0:T(8,128)(2,1)}), bf16[32,8,320]{2,1,0:T(8,128)(2,1)S(1)}, u32[]{:S(2)}, u32[]{:S(2)}) async-start(bf16[32,8,320]{2,1,0:T(8,128)(2,1)} %sum.1), calls=%async_computation.3 | async-start | bytes 393216 | tf_op jit(solution)/shard_map/all_to_all | solution.py:391
  91.0 2.2 %collective-permute-start.2 = (bf16[2,64,256]{2,1,0:T(8,128)(2,1)S(1)}, bf16[2,64,256]{2,1,0:T(8,128)(2,1)S(1)}, u32[]{:S(2)}, u32[]{:S(2)}) collective-permute-start(bf16[2,64,256]{2,1,0:T(8,128)(2,1)S(1)} %get-tuple-element.10), channel_id=1, source_target_pairs={{0,1},{1,2},{2,3},{3,4},{4,5},{5,6},{6,7},{8,9},{9,10},{10,11},{11... | collective-permute-start | bytes 196616 | tf_op jit(solution)/shard_map/ppermute | solution.py:372
  93.2 1.3 %collective-permute-start.3 = (bf16[2,64,256]{2,1,0:T(8,128)(2,1)S(1)}, bf16[2,64,256]{2,1,0:T(8,128)(2,1)S(1)}, u32[]{:S(2)}, u32[]{:S(2)}) collective-permute-start(bf16[2,64,256]{2,1,0:T(8,128)(2,1)S(1)} %get-tuple-element.11), channel_id=1, source_target_pairs={{1,0},{2,1},{3,2},{4,3},{5,4},{6,5},{7,6},{9,8},{10,9},{11,10},{12... | collective-permute-start | bytes 196616 | tf_op jit(solution)/shard_map/ppermute | solution.py:373
  94.5 0.0 collective-permute-done.2.above
  94.5 4.0 %collective-permute-done.3.below = bf16[2,64,256]{2,1,0:T(8,128)(2,1)S(1)} collective-permute-done((bf16[2,64,256]{2,1,0:T(8,128)(2,1)S(1)}, bf16[2,64,256]{2,1,0:T(8,128)(2,1)S(1)}, u32[]{:S(2)}, u32[]{:S(2)}) %collective-permute-start.3) | collective-permute-done | bytes 65568 | tf_op jit(solution)/shard_map/ppermute | solution.py:373
  98.5 0.0 copy-done
  98.5 0.0 copy-done.4
  98.5 2.4 %back.1 = bf16[2,4,64,256]{3,2,1,0:T(8,128)(2,1)} custom-call(bf16[2,4,64,256]{3,2,1,0:T(8,128)(2,1)S(1)} %get-tuple-element.9.drive, bf16[2,64,256]{2,1,0:T(8,128)(2,1)S(1)} %collective-permute-done.2.above, bf16[2,64,256]{2,1,0:T(8,128)(2,1)S(1)} %collective-permute-done.3.below, bf16[9,256,256]{2,1,0:T(8,128)(2,1)S(1)} %copy-done.1, ...), custom_call_target="tpu_custom_call" | custom-call | flops 603979776 | bytes 2097152 | tf_op jit(solution)/shard_map/back/pallas_call | solution.py:379
  100.9 0.0 all-to-all-done.3.got
  100.9 0.9 last.1
  (1 shorter events, 0.0 us)
Async XLA Ops:
  0.6 35.2 %copy-start.2 = (f32[4,64,256]{2,1,0:T(8,128)S(1)}, f32[4,64,256]{2,1,0:T(8,128)}, u32[]{:S(2)}) copy-start(f32[4,64,256]{2,1,0:T(8,128)} %start.1) | copy-start | bytes 786436
  0.6 35.1 %copy-start.3 = (bf16[256,256]{1,0:T(8,128)(2,1)S(1)}, bf16[256,256]{1,0:T(8,128)(2,1)}, u32[]{:S(2)}) copy-start(bf16[256,256]{1,0:T(8,128)(2,1)} %readout.1) | copy-start | bytes 393220
  3.3 32.5 %copy-start.1 = (bf16[9,256,256]{2,1,0:T(8,128)(2,1)S(1)}, bf16[9,256,256]{2,1,0:T(8,128)(2,1)}, u32[]{:S(2)}) copy-start(bf16[9,256,256]{2,1,0:T(8,128)(2,1)} %kernel.1) | copy-start | bytes 3538948
  27.6 7.3 %collective-permute-start.1 = (bf16[32,8,256]{2,1,0:T(8,128)(2,1)S(1)}, bf16[32,8,256]{2,1,0:T(8,128)(2,1)S(1)}, u32[]{:S(2)}, u32[]{:S(2)}) collective-permute-start(bf16[32,8,256]{2,1,0:T(8,128)(2,1)S(1)} %get-tuple-element.15), channel_id=1, source_target_pairs={{1,0},{2,1},{3,2},{4,3},{5,4},{6,5},{7,6},{9,8},{10,9},{11,10},{12... | collective-permute-start | bytes 393224 | tf_op jit(solution)/shard_map/ppermute | solution.py:341
  28.9 6.9 %collective-permute-start = (bf16[32,8,256]{2,1,0:T(8,128)(2,1)S(1)}, bf16[32,8,256]{2,1,0:T(8,128)(2,1)S(1)}, u32[]{:S(2)}, u32[]{:S(2)}) collective-permute-start(bf16[32,8,256]{2,1,0:T(8,128)(2,1)S(1)} %get-tuple-element.16), channel_id=1, source_target_pairs={{0,1},{1,2},{2,3},{3,4},{4,5},{5,6},{6,7},{8,9},{9,10},{10,11},{11... | collective-permute-start | bytes 393224 | tf_op jit(solution)/shard_map/ppermute | solution.py:340
  67.9 30.6 %copy-start = (bf16[2,4,64,256]{3,2,1,0:T(8,128)(2,1)S(1)}, bf16[2,4,64,256]{3,2,1,0:T(8,128)(2,1)}, u32[]{:S(2)}) copy-start(bf16[2,4,64,256]{3,2,1,0:T(8,128)(2,1)} %cotangent.3) | copy-start | bytes 786436
  67.9 30.6 %copy-start.4 = (f32[256]{0:T(256)S(1)}, f32[256]{0:T(256)}, u32[]{:S(2)}) copy-start(f32[256]{0:T(256)} %param.11) | copy-start | bytes 3076
  85.9 15.0 %all-to-all-start.3 = ((bf16[32,8,320]{2,1,0:T(8,128)(2,1)}), bf16[32,8,320]{2,1,0:T(8,128)(2,1)S(1)}, u32[]{:S(2)}, u32[]{:S(2)}) async-start(bf16[32,8,320]{2,1,0:T(8,128)(2,1)} %sum.1), calls=%async_computation.3 | async-start | bytes 393216 | tf_op jit(solution)/shard_map/all_to_all | solution.py:391
  91.0 3.5 %collective-permute-start.2 = (bf16[2,64,256]{2,1,0:T(8,128)(2,1)S(1)}, bf16[2,64,256]{2,1,0:T(8,128)(2,1)S(1)}, u32[]{:S(2)}, u32[]{:S(2)}) collective-permute-start(bf16[2,64,256]{2,1,0:T(8,128)(2,1)S(1)} %get-tuple-element.10), channel_id=1, source_target_pairs={{0,1},{1,2},{2,3},{3,4},{4,5},{5,6},{6,7},{8,9},{9,10},{10,11},{11... | collective-permute-start | bytes 196616 | tf_op jit(solution)/shard_map/ppermute | solution.py:372
  93.2 5.3 %collective-permute-start.3 = (bf16[2,64,256]{2,1,0:T(8,128)(2,1)S(1)}, bf16[2,64,256]{2,1,0:T(8,128)(2,1)S(1)}, u32[]{:S(2)}, u32[]{:S(2)}) collective-permute-start(bf16[2,64,256]{2,1,0:T(8,128)(2,1)S(1)} %get-tuple-element.11), channel_id=1, source_target_pairs={{1,0},{2,1},{3,2},{4,3},{5,4},{6,5},{7,6},{9,8},{10,9},{11,10},{12... | collective-permute-start | bytes 196616 | tf_op jit(solution)/shard_map/ppermute | solution.py:373

commit v4 on v1

--- a/solution.py
+++ b/solution.py
@@ -15,19 +15,21 @@
 PAD = 8
 CELLS = ((0, 0), (0, 1), (2, 0), (2, 1), (1, 0), (1, 1), (3, 0), (3, 1))
 VMEM = pl.BlockSpec(memory_space=pltpu.VMEM)
-
-
-def call(body, name, outs, ins, scratch, flops=1 << 20, moved=1 << 20):
+HBM = pl.BlockSpec(memory_space=pltpu.MemorySpace.HBM)
+
+
+def call(body, name, outs, ins, scratch, flops=1 << 20, moved=1 << 20, grant=40 << 20, to=None, alias=None):
     many = isinstance(outs, (list, tuple))
     return pl.pallas_call(
         body,
         name=name,
         out_shape=outs,
-        in_specs=[VMEM] * ins,
-        out_specs=[VMEM] * len(outs) if many else VMEM,
+        in_specs=ins,
+        out_specs=[VMEM] * len(outs) if many else (to or VMEM),
+        input_output_aliases=alias or {},
         scratch_shapes=scratch,
         cost_estimate=pl.CostEstimate(flops=flops, bytes_accessed=moved, transcendentals=0),
-        compiler_params=pltpu.CompilerParams(vmem_limit_bytes=40 << 20),
+        compiler_params=pltpu.CompilerParams(vmem_limit_bytes=grant),
     )
 
 
@@ -50,54 +52,104 @@
     )
 
 
-def halo_body(frames, cotangent, start, out, parts):
+def halo_body(frames, cotangent, start, out, begin, rows, slopes, starts, sems):
     wide = frames.shape[2]
+    mine = lax.axis_index("tm")
+    group = pl.multiple_of(8 * (mine // 4), 8)
+    copies = (
+        pltpu.make_async_copy(start.at[:, pl.ds(group, 8)], starts, sems.at[0]),
+        pltpu.make_async_copy(frames.at[:, 2:4], rows, sems.at[1]),
+        pltpu.make_async_copy(cotangent.at[:, 3], slopes, sems.at[2]),
+    )
+    for copy in copies:
+        copy.start()
+    for copy in copies:
+        copy.wait()
     for f in range(2):
         for row in range(2):
-            out[pl.ds((2 * f + row) * wide, wide), :] = frames[f, 2 + row]
-        out[pl.ds((4 + f) * wide, wide), :] = cotangent[f, 3]
-    for place, piece in enumerate(split3(start[3])):
-        parts[pl.ds(2 * place, 2), :] = piece
-    parts[6:8, :] = jnp.zeros_like(parts[6:8, :])
-    out[pl.ds(6 * wide, 8), :] = parts[...].astype(BF)
-
-
-def spread_body(frames, cotangent, decay, halo, out, grid, slopes, parts):
-    wide = frames.shape[2]
-    for f in range(2):
-        for row in range(6):
-            grid[f, row, 0:PAD, :] = jnp.zeros((PAD, grid.shape[3]), F32)
-            grid[f, row, PAD + wide :, :] = jnp.zeros((PAD, grid.shape[3]), F32)
-            source = halo[pl.ds((2 * f + row) * wide, wide), :] if row < 2 else frames[f, row - 2]
-            grid[f, row, PAD : PAD + wide, :] = source.astype(F32)
+            out[pl.ds((2 * f + row) * wide, wide), :] = rows[f, row]
+        out[pl.ds((4 + f) * wide, wide), :] = slopes[f]
+    offset = 2 * (mine % 4)
+    step = sublane(begin.shape)
+    total = jnp.zeros(begin.shape, F32)
+    for place, row in ((2, 1), (4, 0), (6, 2)):
+        moved = pltpu.roll(starts[row], (8 + place - offset) % 8, 0)
+        total = jnp.where((step >= place) & (step < place + 2), moved, total)
+    begin[...] = total
+    pieces = split3(pltpu.roll(starts[3], (8 - offset) % 8, 0))
+    total = jnp.where(step < 2, pieces[0], 0.0)
+    total = jnp.where((step >= 2) & (step < 4), pltpu.roll(pieces[1], 2, 0), total)
+    total = jnp.where((step >= 4) & (step < 6), pltpu.roll(pieces[2], 4, 0), total)
+    out[pl.ds(6 * wide, 8), :] = total.astype(BF)
+
+
+def own_body(frames, cotangent, decay, out, pieces, grid, slopes, rows, given, rates, parts, sems):
+    wide, lanes = frames.shape[2:]
+    copies = (
+        pltpu.make_async_copy(frames, rows, sems.at[0]),
+        pltpu.make_async_copy(cotangent, given, sems.at[1]),
+        pltpu.make_async_copy(decay, rates, sems.at[2]),
+    )
+    for copy in copies:
+        copy.start()
+    for f in range(2):
         for row in range(4):
-            source = halo[pl.ds((4 + f) * wide, wide), :] if row < 1 else cotangent[f, row - 1]
-            slopes[f, row, PAD : PAD + wide, :] = source.astype(F32)
-    for place, piece in enumerate(split3(decay[...])):
-        parts[pl.ds(2 * place, 2), :] = piece
-    parts[6:8, :] = jnp.zeros_like(parts[6:8, :])
-    rates = parts[...].astype(BF)
-    step = sublane((8, grid.shape[3]))
+            grid[f, row, 0:PAD, :] = jnp.zeros((PAD, lanes), F32)
+            grid[f, row, PAD + wide :, :] = jnp.zeros((PAD, lanes), F32)
+    for copy in copies:
+        copy.wait()
+    for f in range(2):
+        for row in range(4):
+            grid[f, row, PAD : PAD + wide, :] = rows[f, row].astype(F32)
+        for row in range(3):
+            slopes[f, row, PAD : PAD + wide, :] = given[f, row].astype(F32)
+    for place, piece in enumerate(split3(rates[...])):
+        parts[2 * place : 2 * place + 2, :] = piece
+    parts[6:8, :] = jnp.zeros((2, lanes), F32)
+    pieces[...] = parts[...].astype(BF)
+    step = sublane((8, lanes))
     for target in range(wide // 2):
         first = PAD + 2 * target
         for f in range(2):
-            for pair in range(3):
-                begin = first - 1
+            for pair in range(2):
+                start = first - 1
                 block = jnp.where(
                     step < 4,
-                    grid[f, 2 * pair, begin : begin + 8, :],
-                    grid[f, 2 * pair + 1, begin - 4 : begin + 4, :],
+                    grid[f, 2 * pair, start : start + 8, :],
+                    grid[f, 2 * pair + 1, start - 4 : start + 4, :],
                 )
-                out[target, 32 * f + 8 * pair : 32 * f + 8 * pair + 8, :] = block.astype(BF)
-            block = slopes[f, 0, first : first + 8, :]
-            for place, row in ((2, 2), (4, 1), (6, 3)):
+                out[target, 16 * f + 8 * pair : 16 * f + 8 * pair + 8, :] = block.astype(BF)
+            block = slopes[f, 1, first - 2 : first + 6, :]
+            for place, row in ((4, 0), (6, 2)):
                 block = jnp.where(step < place, block, slopes[f, row, first - place : first - place + 8, :])
+            out[target, 32 + 8 * f : 40 + 8 * f, :] = block.astype(BF)
+
+
+def spread_body(own, pieces, halo, out, grid, slopes):
+    wide = (halo.shape[0] - 8) // 6
+    lanes = halo.shape[1]
+    for f in range(2):
+        for row in range(2):
+            grid[f, row, 0:PAD, :] = jnp.zeros((PAD, lanes), F32)
+            grid[f, row, PAD + wide :, :] = jnp.zeros((PAD, lanes), F32)
+            grid[f, row, PAD : PAD + wide, :] = halo[pl.ds((2 * f + row) * wide, wide), :].astype(F32)
+        slopes[f, PAD : PAD + wide, :] = halo[pl.ds((4 + f) * wide, wide), :].astype(F32)
+    step = sublane((8, lanes))
+    for target in range(wide // 2):
+        first = PAD + 2 * target
+        for f in range(2):
+            start = first - 1
+            block = jnp.where(step < 4, grid[f, 0, start : start + 8, :], grid[f, 1, start - 4 : start + 4, :])
+            out[target, 32 * f : 32 * f + 8, :] = block.astype(BF)
+            out[target, 32 * f + 8 : 32 * f + 24, :] = own[target, 16 * f : 16 * f + 16, :]
+            block = own[target, 32 + 8 * f : 40 + 8 * f, :].astype(F32)
+            block = jnp.where(step < 2, slopes[f, first : first + 8, :], block)
             out[target, 32 * f + 24 : 32 * f + 32, :] = block.astype(BF)
-        out[target, 64:72, :] = rates
+        out[target, 64:72, :] = pieces[...]
 
 
 def cell_body(
-    got, kernel, readout, start, halo, out, grid, decay, gain, taps, driven, states, slopes, drive, turned, begin
+    got, kernel, readout, start, halo, out, grid, decay, gain, taps, driven, states, slopes, drive, turned
 ):
     sources = got.shape[0]
     count = sources * 16
@@ -153,12 +205,8 @@
     lax.fori_loop(0, count // chunk, convolve, 0)
 
     tail = halo[6 * wide : 6 * wide + 8, :].astype(F32)
-    begin[0:8, :] = tail
-    top = begin[0:2, :] + begin[2:4, :] + begin[4:6, :]
-    begin[0:2, :] = top
-    begin[2:4, :] = start[1]
-    begin[4:6, :] = start[0]
-    begin[6:8, :] = start[2]
+    tail = tail + pltpu.roll(tail, 6, 0) + pltpu.roll(tail, 4, 0)
+    begin = jnp.where(step < 2, tail, start[...])
 
     def advance(source, state):
         pair = []
@@ -171,7 +219,7 @@
         states[pl.ds(pl.multiple_of(16 * source, 16), 16), :] = jnp.concatenate(pair, axis=0).astype(BF)
         return state
 
-    lax.fori_loop(0, sources, advance, begin[...], unroll=4)
+    lax.fori_loop(0, sources, advance, begin, unroll=4)
 
     def mix(part, _):
         rows = pl.ds(pl.multiple_of(part * 64, 64), 64)
@@ -191,7 +239,7 @@
         )
         return _
 
-    lax.fori_loop(0, count // 64, mix, 0, unroll=2)
+    lax.fori_loop(0, count // 64, mix, 0, unroll=4)
 
     def retreat(turn, carried):
         adjoint, later = carried
@@ -219,7 +267,7 @@
     out[:, :, 9 * lanes : 10 * lanes] = term.astype(BF).reshape(sources, share, lanes)
 
 
-def join_body(bands, got, total, frames, cells, grid):
+def join_body(bands, got, total, frames, top, cells, grid):
     sources, share, width = got.shape
     lanes = width // 12
 
@@ -231,7 +279,7 @@
     for band in range(bands):
         total[band] = jnp.concatenate(
             [sums[:, lanes * k + block * band : lanes * k + block * band + block] for k in range(10)], axis=1
-        )
+        ).astype(BF)
 
     for f in range(2):
         for part in range(lanes // 128):
@@ -241,14 +289,20 @@
             for place, (row, column) in enumerate(CELLS):
                 grid[pl.ds(column, sources, stride=2), :] = cells[pl.ds(place, sources, stride=8), :]
                 if column == 1:
-                    frames[f, row, :, 128 * part : 128 * part + 128] = grid[...].astype(BF)
-
-
-def back_body(bands, drive, below, kernel, cotangent, feedthrough, out, grid, moved):
-    wide = drive.shape[2]
-    lanes = drive.shape[3]
+                    value = grid[...].astype(BF)
+                    frames[f, row, :, 128 * part : 128 * part + 128] = value
+                    if row < 2:
+                        top[f, row, :, 128 * part : 128 * part + 128] = value
+
+
+def back_body(first, bands, *refs):
+    if first:
+        drive, below, kernel, cotangent, feedthrough, _, out, grid, moved, done, sem = refs
+    else:
+        drive, kernel, cotangent, feedthrough, out, grid, moved, done, sem = refs
+    wide, lanes = drive.shape[2:]
     band = lax.axis_index("row")
-    for row in range(6):
+    for row in range(first, first + 4):
         keep = None
         if row == 0:
             keep = jnp.where(band == 0, 0.0, 1.0)
@@ -258,39 +312,39 @@
             source = (drive[f, row] if row < 4 else below[f, row - 4]).astype(F32)
             if keep is not None:
                 source = source * keep
-            grid[0:PAD, :] = jnp.zeros((PAD, lanes), F32)
-            grid[PAD + wide :, :] = jnp.zeros((PAD, lanes), F32)
-            grid[PAD : PAD + wide, :] = source
+            grid[f, row - first, 0:PAD, :] = jnp.zeros((PAD, lanes), F32)
+            grid[f, row - first, PAD + wide :, :] = jnp.zeros((PAD, lanes), F32)
+            grid[f, row - first, PAD : PAD + wide, :] = source
             for shift in range(3):
-                moved[shift, f, row] = grid[PAD - 1 + shift : PAD - 1 + shift + wide, :].astype(BF)
-    for f in range(2):
-        for half in range(2):
-            total = jnp.zeros((2 * wide, lanes), F32)
-            for i in range(3):
-                for j in range(3):
-                    first = 2 - i + 2 * half
-                    cells = moved[2 - j, f, first : first + 2].reshape(2 * wide, lanes)
-                    total = total + lax.dot_general(
-                        cells, kernel[3 * i + j], (((1,), (1,)), ((), ())), preferred_element_type=F32
-                    )
-            total = total.reshape(2, wide, lanes)
-            for row in range(2):
-                place = 2 * half + row
-                out[f, place] = (total[row] + feedthrough[...] * cotangent[f, place].astype(F32)).astype(BF)
+                begin = PAD - 1 + shift
+                moved[shift, f, row - first] = grid[f, row - first, begin : begin + wide, :].astype(BF)
+    for f in range(2):
+        total = jnp.zeros((2 * wide, lanes), F32)
+        for i in range(3):
+            for j in range(3):
+                cells = moved[2 - j, f, 2 - i : 4 - i].reshape(2 * wide, lanes)
+                total = total + lax.dot_general(
+                    cells, kernel[3 * i + j], (((1,), (1,)), ((), ())), preferred_element_type=F32
+                )
+        given = cotangent[f, first : first + 2].astype(F32).reshape(2 * wide, lanes)
+        done[f] = (total + feedthrough[...] * given).astype(BF).reshape(2, wide, lanes)
+    store = pltpu.make_async_copy(done, out.at[:, first : first + 2], sem)
+    store.start()
+    store.wait()
 
 
 def sum_body(scaling, got, out):
-    total = got[0]
+    total = got[0].astype(F32)
     for band in range(1, got.shape[0]):
-        total = total + got[band]
-    total = total * scaling
+        total = total + got[band].astype(F32)
+    total = (total * scaling).astype(BF)
     for target in range(out.shape[0]):
         out[target] = total
 
 
 def last_body(got, kernel_out, readout_out):
     sources, share, width = got.shape
-    turned = got[...].reshape(sources * share, width).T
+    turned = got[...].astype(F32).reshape(sources * share, width).T
     block = width // 10
     for k in range(9):
         kernel_out[k] = turned[block * k : block * k + block]
@@ -307,28 +361,52 @@
     down = [(i, (i + 1) % bands) for i in range(bands)]
     up = [((i + 1) % bands, i) for i in range(bands)]
 
-    start = lax.dynamic_slice_in_dim(start_state, 2 * lax.axis_index("tm"), 2, 1)
-    edge = call(
-        halo_body, "halo", shape((6 * wide + 8, lanes), BF), 3, [pltpu.VMEM((8, lanes), F32)]
-    )(frames_in, cotangent, start)
+    edge, begin = call(
+        halo_body,
+        "halo",
+        (shape((6 * wide + 8, lanes), BF), shape((8, lanes), F32)),
+        [HBM] * 3,
+        [
+            pltpu.VMEM((2, 2, wide, lanes), BF),
+            pltpu.VMEM((2, wide, lanes), BF),
+            pltpu.VMEM((4, 8, lanes), F32),
+            pltpu.SemaphoreType.DMA((3,)),
+        ],
+        grant=63 << 20,
+    )(frames_in, cotangent, start_state)
     edge = lax.ppermute(edge, "row", down)
+    own, pieces = call(
+        own_body,
+        "own",
+        (shape((sources, 48, lanes), BF), shape((8, lanes), BF)),
+        [HBM] * 3,
+        [
+            pltpu.VMEM((2, 4, wide + 2 * PAD, lanes), F32),
+            pltpu.VMEM((2, 3, wide + 2 * PAD, lanes), F32),
+            pltpu.VMEM((2, 4, wide, lanes), BF),
+            pltpu.VMEM((2, 4, wide, lanes), BF),
+            pltpu.VMEM((2, lanes), F32),
+            pltpu.VMEM((8, lanes), F32),
+            pltpu.SemaphoreType.DMA((3,)),
+        ],
+        moved=8 << 20,
+    )(frames_in, cotangent, decay_rate)
     send = call(
         spread_body,
         "spread",
         shape((sources, 72, lanes), BF),
-        4,
+        [VMEM] * 3,
         [
-            pltpu.VMEM((2, 6, wide + 2 * PAD, lanes), F32),
-            pltpu.VMEM((2, 4, wide + 2 * PAD, lanes), F32),
-            pltpu.VMEM((8, lanes), F32),
+            pltpu.VMEM((2, 2, wide + 2 * PAD, lanes), F32),
+            pltpu.VMEM((2, wide + 2 * PAD, lanes), F32),
         ],
-    )(frames_in, cotangent, decay_rate, edge)
+    )(own, pieces, edge)
     got = lax.all_to_all(send, "tm", 0, 0)
     send = call(
         cell_body,
         "cells",
         shape((sources, max(8, share), 12 * lanes), BF),
-        5,
+        [VMEM] * 5,
         [
             pltpu.VMEM((2 * sources, 24, lanes), F32),
             pltpu.VMEM((sources, 8, lanes), F32),
@@ -339,40 +417,55 @@
             pltpu.VMEM((cells, lanes), BF),
             pltpu.VMEM((cells, lanes), F32),
             pltpu.VMEM((lanes, cells), BF),
-            pltpu.VMEM((8, lanes), F32),
         ],
         flops=2 * cells * lanes * lanes * 21,
         moved=4 << 20,
-    )(got, kernel.reshape(9 * lanes, lanes), readout, start, edge)
+    )(got, kernel.reshape(9 * lanes, lanes), readout, begin, edge)
     got = lax.all_to_all(send, "tm", 0, 0)
-    partial, drive = call(
+    partial, drive, top = call(
         functools.partial(join_body, bands),
         "join",
-        (shape((bands, share, 10 * block), F32), shape((2, 4, wide, lanes), BF)),
-        1,
+        (
+            shape((bands, share, 10 * block), BF),
+            shape((2, 4, wide, lanes), BF),
+            shape((2, 2, wide, lanes), BF),
+        ),
+        [VMEM],
         [pltpu.VMEM((8 * sources, 128), F32), pltpu.VMEM((wide, 128), F32)],
     )(got)
-    below = lax.ppermute(drive[:, :2], "row", up)
+    below = lax.ppermute(top, "row", up)
     partial = lax.all_to_all(partial, "row", 0, 0)
     scaling = 1.0 / math.sqrt(here * sources * band_rows * bands * wide)
     partial = call(
-        functools.partial(sum_body, scaling), "sum", shape((sources, share, 10 * block), F32), 1, []
+        functools.partial(sum_body, scaling), "sum", shape((sources, share, 10 * block), BF), [VMEM], []
     )(partial)
-    grad_frames = call(
-        functools.partial(back_body, bands),
-        "back",
-        shape(frames_in.shape, BF),
-        5,
-        [
-            pltpu.VMEM((wide + 2 * PAD, lanes), F32),
-            pltpu.VMEM((3, 2, 6, wide, lanes), BF),
-        ],
-        flops=2 * cells * lanes * lanes * 9,
-        moved=2 << 20,
-    )(drive, below, kernel, cotangent, feedthrough.reshape(1, lanes))
+
+    def back(first, ins, **more):
+        return call(
+            functools.partial(back_body, first, bands),
+            "back",
+            shape(frames_in.shape, BF),
+            ins,
+            [
+                pltpu.VMEM((2, 4, wide + 2 * PAD, lanes), F32),
+                pltpu.VMEM((3, 2, 4, wide, lanes), BF),
+                pltpu.VMEM((2, 2, wide, lanes), BF),
+                pltpu.SemaphoreType.DMA,
+            ],
+            flops=cells * lanes * lanes * 9,
+            moved=2 << 20,
+            to=HBM,
+            **more,
+        )
+
+    through = feedthrough.reshape(1, lanes)
+    grad_frames = back(0, [VMEM] * 4)(drive, kernel, cotangent, through)
+    grad_frames = back(2, [VMEM] * 5 + [HBM], alias={5: 0})(
+        drive, below, kernel, cotangent, through, grad_frames
+    )
     whole = lax.all_to_all(partial, "tm", 0, 0)
     grad_kernel, grad_readout = call(
-        last_body, "last", (shape((9, block, lanes), F32), shape((block, lanes), F32)), 1, []
+        last_body, "last", (shape((9, block, lanes), F32), shape((block, lanes), F32)), [VMEM], []
     )(whole)
     return grad_frames, grad_kernel, grad_readout.T
 

time: 106 us -> 101 us (0.953)
  blocking collectives: 66.8 us -> 53.6 us
  starting transfers between devices: 7.42 us -> 15.5 us
  Pallas kernels: 10.3 us -> 13 us
  waiting for transfers between devices: 16.5 us -> 15.2 us
    all_to_all x1 -> x0, blocking collectives: 13.2 us -> none  [local(): partial = lax.all_to_all(partial, 'row', 0, 0)]
    all_to_all x0 -> x1, starting transfers between devices: none -> 5.29 us  [local(): partial = lax.all_to_all(partial, 'row', 0, 0)]
    ppermute x1, waiting for transfers between devices: 4.69 us -> 0.01 us  [local(): below = lax.ppermute(top, 'row', up)]
    all_to_all x0 -> x1, waiting for transfers between devices: none -> 4.38 us  [local(): partial = lax.all_to_all(partial, 'row', 0, 0)]
    ppermute x1, waiting for transfers between devices: 8.63 us -> 5.65 us  [local(): edge = lax.ppermute(edge, 'row', down)]
    ppermute x1, starting transfers between devices: 0.08 us -> 2.67 us  [local(): below = lax.ppermute(top, 'row', up)]
    pallas_call x3 -> x5, Pallas kernels: 3.2 us -> 5.69 us  [the longest x1 1.68 us: local(): call(halo_body, 'halo', (shape((6 * wide + 8, lanes), BF), shape((8, lane...]
    all_to_all x1, waiting for transfers between devices: 3.17 us -> 5.15 us  [local(): whole = lax.all_to_all(partial, 'tm', 0, 0)]
  transfers between devices with their start and end apart: 3 -> 4, of which waited for: 3 -> 3; matrix products, arithmetic and copies ran while one was open for 0% -> 0% of each run, Pallas kernels for 2% -> 4%
where the time goes in v4:
time: 101 us
  blocking collectives  53.6 us (53%)
  starting transfers between devices  15.5 us (15%)
  waiting for transfers between devices  15.2 us (15%)
  Pallas kernels  13 us (13%)
  local copies, waits for them, and re-layouts  2.61 us (3%)
    all_to_all x2, blocking collectives, local(): got = lax.all_to_all(send, 'tm', 0, 0)  53.6 us
    ppermute x1, waiting for transfers between devices, local(): edge = lax.ppermute(edge, 'row', down)  5.65 us
    all_to_all x1, starting transfers between devices, local(): partial = lax.all_to_all(partial, 'row', 0, 0)  5.29 us
    all_to_all x1, waiting for transfers between devices, local(): whole = lax.all_to_all(partial, 'tm', 0, 0)  5.15 us
    all_to_all x1, starting transfers between devices, local(): whole = lax.all_to_all(partial, 'tm', 0, 0)  5.05 us
    pallas_call x1, Pallas kernels, local(): call(cell_body, 'cells', shape((sources, max(8, share), 12 * lanes), BF),...  4.65 us
    all_to_all x1, waiting for transfers between devices, local(): partial = lax.all_to_all(partial, 'row', 0, 0)  4.38 us
    ppermute x1, starting transfers between devices, local(): below = lax.ppermute(top, 'row', up)  2.67 us
  transfers between devices with their start and end apart: 4, of which 3 were waited for; matrix products, arithmetic and copies ran while one was open for 0% of the time, Pallas kernels for 4%

profile of v4, /device:TPU:1, one launch (start us, length us, event | category | flops | bytes accessed | tf_op | source)
XLA Modules:
  0.0 100.6 jit_solution(7868109869567253711)
XLA Ops:
  0.6 1.7 %halo.1 = (bf16[392,256]{1,0:T(8,128)(2,1)}, f32[8,256]{1,0:T(8,128)}) custom-call(bf16[2,4,64,256]{3,2,1,0:T(8,128)(2,1)} %frames.3, bf16[2,4,64,256]{3,2,1,0:T(8,128)(2,1)} %refs_3_.1, f32[4,64,256]{2,1,0:T(8,128)} %start.1), custom_call_target="tpu_custom_call" | custom-call | flops 1048576 | bytes 1048576 | tf_op jit(solution)/shard_map/halo/pallas_call | solution.py:364
  2.3 2.5 %collective-permute-start = (bf16[392,256]{1,0:T(8,128)(2,1)}, bf16[392,256]{1,0:T(8,128)(2,1)S(1)}, u32[]{:S(2)}, u32[]{:S(2)}) collective-permute-start(bf16[392,256]{1,0:T(8,128)(2,1)} %get-tuple-element.14), channel_id=1, source_target_pairs={{0,1},{1,2},{2,3},{3,4},{4,5},{5,6},{6,7},{7,0},{8,9},{9,10},{10,1... | collective-permute-start | bytes 602120 | tf_op jit(solution)/shard_map/ppermute | solution.py:377
  4.8 0.0 copy-start.1
  4.8 0.9 copy-done.1
  5.8 0.0 copy-start.3
  5.8 0.9 copy-done.3
  6.8 0.7 copy-done.5
  7.4 0.6 own.1
  8.0 5.7 %collective-permute-done.halo = bf16[392,256]{1,0:T(8,128)(2,1)S(1)} collective-permute-done((bf16[392,256]{1,0:T(8,128)(2,1)}, bf16[392,256]{1,0:T(8,128)(2,1)S(1)}, u32[]{:S(2)}, u32[]{:S(2)}) %collective-permute-start) | collective-permute-done | bytes 200736 | tf_op jit(solution)/shard_map/ppermute | solution.py:377
  13.7 0.3 spread.1
  14.0 0.0 copy-start
  14.0 0.0 copy-start.6
  14.0 0.0 copy-start.7
  14.0 27.2 %all_to_all.20.got = bf16[32,72,256]{2,1,0:T(8,128)(2,1)S(1)} all-to-all(bf16[32,72,256]{2,1,0:T(8,128)(2,1)S(1)} %spread.1), channel_id=1, replica_groups=mesh['tm'=32,'row'=8] {'tm'}, dimensions={0} | all-to-all | bytes 2359296 | tf_op jit(solution)/shard_map/all_to_all | solution.py:404
  41.2 0.0 copy-done
  41.2 0.0 copy-done.6
  41.2 0.0 copy-done.7
  41.2 4.7 %cells.1 = bf16[32,8,3072]{2,1,0:T(8,128)(2,1)S(1)} custom-call(bf16[32,72,256]{2,1,0:T(8,128)(2,1)S(1)} %all_to_all.20.got, bf16[2304,256]{1,0:T(8,128)(2,1)S(1)} %bitcast.3, bf16[256,256]{1,0:T(8,128)(2,1)S(1)} %copy-done.6, f32[8,256]{1,0:T(8,128)S(1)} %copy-done.7, bf16[392,256]{1,0:T(8,128)(2,1)S(1)} %collective-permute-done.halo), custom_call_target="tpu_custom_call" | custom-call | flops 1409286144 | bytes 4194304 | tf_op jit(solution)/shard_map/cells/pallas_call | solution.py:405
  45.9 26.4 %all_to_all.21.got = bf16[32,8,3072]{2,1,0:T(8,128)(2,1)S(1)} all-to-all(bf16[32,8,3072]{2,1,0:T(8,128)(2,1)S(1)} %cells.1), channel_id=1, replica_groups=mesh['tm'=32,'row'=8] {'tm'}, dimensions={0} | all-to-all | bytes 3145728 | tf_op jit(solution)/shard_map/all_to_all | solution.py:424
  72.3 1.1 %join.1 = (bf16[8,8,320]{2,1,0:T(8,128)(2,1)}, bf16[2,4,64,256]{3,2,1,0:T(8,128)(2,1)S(1)}, bf16[2,2,64,256]{3,2,1,0:T(8,128)(2,1)S(1)}) custom-call(bf16[32,8,3072]{2,1,0:T(8,128)(2,1)S(1)} %all_to_all.21.got), custom_call_target="tpu_custom_call" | custom-call | flops 1048576 | bytes 1048576 | tf_op jit(solution)/shard_map/join/pallas_call | solution.py:425
  73.4 5.3 %all-to-all-start.2 = ((bf16[8,8,320]{2,1,0:T(8,128)(2,1)}), bf16[8,8,320]{2,1,0:T(8,128)(2,1)S(1)}, u32[]{:S(2)}, u32[]{:S(2)}) async-start(bf16[8,8,320]{2,1,0:T(8,128)(2,1)} %get-tuple-element.18), calls=%async_computation.2 | async-start | bytes 98304 | tf_op jit(solution)/shard_map/all_to_all | solution.py:437
  78.7 2.7 %collective-permute-start.1 = (bf16[2,2,64,256]{3,2,1,0:T(8,128)(2,1)S(1)}, bf16[2,2,64,256]{3,2,1,0:T(8,128)(2,1)S(1)}, u32[]{:S(2)}, u32[]{:S(2)}) collective-permute-start(bf16[2,2,64,256]{3,2,1,0:T(8,128)(2,1)S(1)} %get-tuple-element.17), channel_id=1, source_target_pairs={{1,0},{2,1},{3,2},{4,3},{5,4},{6,5},{7,6},{0,7},{9,8},{10,9},{11,1... | collective-permute-start | bytes 393224 | tf_op jit(solution)/shard_map/ppermute | solution.py:436
  81.3 4.4 %all-to-all-done.2.got = bf16[8,8,320]{2,1,0:T(8,128)(2,1)S(1)} async-done(((bf16[8,8,320]{2,1,0:T(8,128)(2,1)}), bf16[8,8,320]{2,1,0:T(8,128)(2,1)S(1)}, u32[]{:S(2)}, u32[]{:S(2)}) %all-to-all-start.2) | async-done | bytes 40992 | tf_op jit(solution)/shard_map/all_to_all | solution.py:437
  85.7 0.7 sum.1
  86.4 5.0 %all-to-all-start.3 = ((bf16[32,8,320]{2,1,0:T(8,128)(2,1)}), bf16[32,8,320]{2,1,0:T(8,128)(2,1)S(1)}, u32[]{:S(2)}, u32[]{:S(2)}) async-start(bf16[32,8,320]{2,1,0:T(8,128)(2,1)} %sum.1), calls=%async_computation.3 | async-start | bytes 393216 | tf_op jit(solution)/shard_map/all_to_all | solution.py:466
  91.5 0.0 copy-done.2
  91.5 0.0 copy-done.4
  91.5 1.6 %back.2.refs_5_ = bf16[2,4,64,256]{3,2,1,0:T(8,128)(2,1)} custom-call(bf16[2,4,64,256]{3,2,1,0:T(8,128)(2,1)S(1)} %get-tuple-element.16.refs_0_, bf16[9,256,256]{2,1,0:T(8,128)(2,1)S(1)} %copy-done, bf16[2,4,64,256]{3,2,1,0:T(8,128)(2,1)S(1)} %copy-done.2, f32[1,256]{1,0:T(1,128)S(1)} %bitcast.4), custom_call_target="tpu_custom_call" | custom-call | flops 301989888 | bytes 2097152 | tf_op jit(solution)/shard_map/back/pallas_call | solution.py:462
  93.1 0.0 collective-permute-done.1.refs_1_
  93.1 1.6 %back.3 = bf16[2,4,64,256]{3,2,1,0:T(8,128)(2,1)} custom-call(bf16[2,4,64,256]{3,2,1,0:T(8,128)(2,1)S(1)} %get-tuple-element.16.refs_0_, bf16[2,2,64,256]{3,2,1,0:T(8,128)(2,1)S(1)} %collective-permute-done.1.refs_1_, bf16[9,256,256]{2,1,0:T(8,128)(2,1)S(1)} %copy-done, bf16[2,4,64,256]{3,2,1,0:T(8,128)(2,1)S(1)} %copy-done.2, ...), custom_call_target="tpu_custom_call", output_to_operand_aliasing={{}: (5, {})} | custom-call | flops 301989888 | bytes 2097152 | tf_op jit(solution)/shard_map/back/pallas_call | solution.py:463
  94.6 5.1 %all-to-all-done.3.got = bf16[32,8,320]{2,1,0:T(8,128)(2,1)S(1)} async-done(((bf16[32,8,320]{2,1,0:T(8,128)(2,1)}), bf16[32,8,320]{2,1,0:T(8,128)(2,1)S(1)}, u32[]{:S(2)}, u32[]{:S(2)}) %all-to-all-start.3) | async-done | bytes 163872 | tf_op jit(solution)/shard_map/all_to_all | solution.py:466
  99.8 0.9 last.1
  (3 shorter events, 0.0 us)
Async XLA Ops:
  2.3 11.4 %collective-permute-start = (bf16[392,256]{1,0:T(8,128)(2,1)}, bf16[392,256]{1,0:T(8,128)(2,1)S(1)}, u32[]{:S(2)}, u32[]{:S(2)}) collective-permute-start(bf16[392,256]{1,0:T(8,128)(2,1)} %get-tuple-element.14), channel_id=1, source_target_pairs={{0,1},{1,2},{2,3},{3,4},{4,5},{5,6},{6,7},{7,0},{8,9},{9,10},{10,1... | collective-permute-start | bytes 602120 | tf_op jit(solution)/shard_map/ppermute | solution.py:377
  4.8 0.9 copy-start.1
  5.8 0.9 copy-start.3
  6.7 0.7 copy-start.5
  14.0 27.2 %copy-start = (bf16[9,256,256]{2,1,0:T(8,128)(2,1)S(1)}, bf16[9,256,256]{2,1,0:T(8,128)(2,1)}, u32[]{:S(2)}) copy-start(bf16[9,256,256]{2,1,0:T(8,128)(2,1)} %refs_2_.3) | copy-start | bytes 3538948
  14.0 27.2 %copy-start.6 = (bf16[256,256]{1,0:T(8,128)(2,1)S(1)}, bf16[256,256]{1,0:T(8,128)(2,1)}, u32[]{:S(2)}) copy-start(bf16[256,256]{1,0:T(8,128)(2,1)} %readout.1) | copy-start | bytes 393220
  14.0 27.2 %copy-start.7 = (f32[8,256]{1,0:T(8,128)S(1)}, f32[8,256]{1,0:T(8,128)}, u32[]{:S(2)}) copy-start(f32[8,256]{1,0:T(8,128)} %get-tuple-element.15.start) | copy-start | bytes 24580
  72.3 19.2 %copy-start.2 = (bf16[2,4,64,256]{3,2,1,0:T(8,128)(2,1)S(1)}, bf16[2,4,64,256]{3,2,1,0:T(8,128)(2,1)}, u32[]{:S(2)}) copy-start(bf16[2,4,64,256]{3,2,1,0:T(8,128)(2,1)} %refs_3_.1) | copy-start | bytes 786436
  72.3 19.2 %copy-start.4 = (f32[256]{0:T(256)S(1)}, f32[256]{0:T(256)}, u32[]{:S(2)}) copy-start(f32[256]{0:T(256)} %param.11) | copy-start | bytes 3076
  73.4 12.3 %all-to-all-start.2 = ((bf16[8,8,320]{2,1,0:T(8,128)(2,1)}), bf16[8,8,320]{2,1,0:T(8,128)(2,1)S(1)}, u32[]{:S(2)}, u32[]{:S(2)}) async-start(bf16[8,8,320]{2,1,0:T(8,128)(2,1)} %get-tuple-element.18), calls=%async_computation.2 | async-start | bytes 98304 | tf_op jit(solution)/shard_map/all_to_all | solution.py:437
  78.7 14.4 %collective-permute-start.1 = (bf16[2,2,64,256]{3,2,1,0:T(8,128)(2,1)S(1)}, bf16[2,2,64,256]{3,2,1,0:T(8,128)(2,1)S(1)}, u32[]{:S(2)}, u32[]{:S(2)}) collective-permute-start(bf16[2,2,64,256]{3,2,1,0:T(8,128)(2,1)S(1)} %get-tuple-element.17), channel_id=1, source_target_pairs={{1,0},{2,1},{3,2},{4,3},{5,4},{6,5},{7,6},{0,7},{9,8},{10,9},{11,1... | collective-permute-start | bytes 393224 | tf_op jit(solution)/shard_map/ppermute | solution.py:436
  86.4 13.4 %all-to-all-start.3 = ((bf16[32,8,320]{2,1,0:T(8,128)(2,1)}), bf16[32,8,320]{2,1,0:T(8,128)(2,1)S(1)}, u32[]{:S(2)}, u32[]{:S(2)}) async-start(bf16[32,8,320]{2,1,0:T(8,128)(2,1)} %sum.1), calls=%async_computation.3 | async-start | bytes 393216 | tf_op jit(solution)/shard_map/all_to_all | solution.py:466

commit v5 on v4

--- a/solution.py
+++ b/solution.py
@@ -149,7 +149,7 @@
 
 
 def cell_body(
-    got, kernel, readout, start, halo, out, grid, decay, gain, taps, driven, states, slopes, drive, turned
+    got, kernel, readout, start, halo, give, keep, stay, grid, decay, gain, taps, driven, states, slopes, drive, turned
 ):
     sources = got.shape[0]
     count = sources * 16
@@ -251,30 +251,69 @@
             later = jnp.broadcast_to(decay[source, f : f + 1, :], adjoint.shape)
             value = jnp.broadcast_to(gain[source, f : f + 1, :], adjoint.shape) * adjoint
             pair.append(value)
-            out[source, 0:8, 10 * lanes + f * lanes : 11 * lanes + f * lanes] = value.astype(BF)
         drive[pl.ds(pl.multiple_of(16 * source, 16), 16), :] = jnp.concatenate(pair[::-1], axis=0)
         return adjoint, later
 
     nothing = jnp.zeros((8, lanes), F32)
     lax.fori_loop(0, sources, retreat, (nothing, nothing), unroll=4)
 
-    turned[...] = drive[...].astype(BF).T
+    half = sources // 2
     share = lanes // sources
+    is_even = lax.axis_index("tm") % 2 == 0
+
+    def partners_first(value):
+        blocks = value.astype(F32).reshape(half, 2, share, count)
+        even, odd = blocks[:, 0].reshape(lanes // 2, count), blocks[:, 1].reshape(lanes // 2, count)
+        order = (jnp.where(is_even, odd, even), jnp.where(is_even, even, odd))
+        return jnp.concatenate(order, axis=0).astype(BF)
+
+    for chip in range(half):
+        for f in range(2):
+            even = drive[32 * chip + 8 * f : 32 * chip + 8 * f + 8, :]
+            odd = drive[32 * chip + 8 * f + 16 : 32 * chip + 8 * f + 24, :]
+            columns = slice(10 * lanes + f * lanes, 11 * lanes + f * lanes)
+            give[chip, 0:8, columns] = jnp.where(is_even, odd, even).astype(BF)
+            stay[chip, :, f * lanes : f * lanes + lanes] = jnp.where(is_even, even, odd).astype(BF)
+    turned[...] = partners_first(drive[...].astype(BF).T)
     for tap in range(9):
-        term = jnp.dot(turned[...], taps[:, lanes * tap : lanes * tap + lanes], preferred_element_type=F32)
-        out[:, :, lanes * tap : lanes * tap + lanes] = term.astype(BF).reshape(sources, share, lanes)
-    term = jnp.dot(states[...].T, slopes[...], preferred_element_type=F32)
-    out[:, :, 9 * lanes : 10 * lanes] = term.astype(BF).reshape(sources, share, lanes)
+        columns = slice(lanes * tap, lanes * tap + lanes)
+        term = jnp.dot(turned[...], taps[:, columns], preferred_element_type=F32)
+        give[:, :, columns] = term[: lanes // 2].astype(BF).reshape(half, share, lanes)
+        keep[:, :, columns] = term[lanes // 2 :].reshape(half, share, lanes)
+    turned[...] = partners_first(states[...].T)
+    columns = slice(9 * lanes, 10 * lanes)
+    term = jnp.dot(turned[...], slopes[...], preferred_element_type=F32)
+    give[:, :, columns] = term[: lanes // 2].astype(BF).reshape(half, share, lanes)
+    keep[:, :, columns] = term[lanes // 2 :].reshape(half, share, lanes)
+
+
+def merge_body(taken, keep, stay, out):
+    lanes = stay.shape[2] // 2
+    for chip in range(out.shape[0]):
+        total = keep[chip] + taken[chip, :, : 10 * lanes].astype(F32)
+        out[chip, :, : 10 * lanes] = total.astype(BF)
+    is_even = lax.axis_index("tm") % 2 == 0
+
+    @pl.when(is_even)
+    def _():
+        out[:, 0:8, 10 * lanes : 12 * lanes] = stay[...]
+        out[:, 0:8, 12 * lanes : 14 * lanes] = taken[:, 0:8, 10 * lanes : 12 * lanes]
+
+    @pl.when(jnp.logical_not(is_even))
+    def _():
+        out[:, 0:8, 10 * lanes : 12 * lanes] = taken[:, 0:8, 10 * lanes : 12 * lanes]
+        out[:, 0:8, 12 * lanes : 14 * lanes] = stay[...]
 
 
 def join_body(bands, got, total, frames, top, cells, grid):
-    sources, share, width = got.shape
-    lanes = width // 12
+    chips, share, width = got.shape
+    sources = 2 * chips
+    lanes = width // 14
 
     def add(source, carried):
         return carried + got[source, :, : 10 * lanes].astype(F32)
 
-    sums = lax.fori_loop(0, sources, add, jnp.zeros((share, 10 * lanes), F32), unroll=2)
+    sums = lax.fori_loop(0, chips, add, jnp.zeros((share, 10 * lanes), F32), unroll=2)
     block = lanes // bands
     for band in range(bands):
         total[band] = jnp.concatenate(
@@ -284,8 +323,8 @@
     for f in range(2):
         for part in range(lanes // 128):
             for source in range(sources):
-                first = (10 + f) * lanes + 128 * part
-                cells[8 * source : 8 * source + 8, :] = got[source, 0:8, first : first + 128].astype(F32)
+                first = (10 + f + 2 * (source % 2)) * lanes + 128 * part
+                cells[8 * source : 8 * source + 8, :] = got[source // 2, 0:8, first : first + 128].astype(F32)
             for place, (row, column) in enumerate(CELLS):
                 grid[pl.ds(column, sources, stride=2), :] = cells[pl.ds(place, sources, stride=8), :]
                 if column == 1:
@@ -402,10 +441,15 @@
         ],
     )(own, pieces, edge)
     got = lax.all_to_all(send, "tm", 0, 0)
-    send = call(
+    half = sources // 2
+    give, keep, stay = call(
         cell_body,
         "cells",
-        shape((sources, max(8, share), 12 * lanes), BF),
+        (
+            shape((half, share, 12 * lanes), BF),
+            shape((half, share, 10 * lanes), F32),
+            shape((half, 8, 2 * lanes), BF),
+        ),
         [VMEM] * 5,
         [
             pltpu.VMEM((2 * sources, 24, lanes), F32),
@@ -421,7 +465,10 @@
         flops=2 * cells * lanes * lanes * 21,
         moved=4 << 20,
     )(got, kernel.reshape(9 * lanes, lanes), readout, begin, edge)
-    got = lax.all_to_all(send, "tm", 0, 0)
+    taken = lax.ppermute(give, "tm", [(i, i ^ 1) for i in range(sources)])
+    send = call(merge_body, "merge", shape((half, share, 14 * lanes), BF), [VMEM] * 3, [])(taken, keep, stay)
+    groups = [[2 * chip + core for chip in range(half)] for core in range(2)]
+    got = lax.all_to_all(send, "tm", 0, 0, axis_index_groups=groups)
     partial, drive, top = call(
         functools.partial(join_body, bands),
         "join",

time: 101 us -> 96.5 us (0.955)
  blocking collectives: 53.6 us -> 44.1 us
  starting transfers between devices: 15.5 us -> 18.4 us
  waiting for transfers between devices: 15.2 us -> 17.2 us
    all_to_all x2 -> x1, blocking collectives: 53.6 us -> 27.2 us  [local(): got = lax.all_to_all(send, 'tm', 0, 0)]
    all_to_all x0 -> x1, blocking collectives: none -> 16.9 us  [local(): got = lax.all_to_all(send, 'tm', 0, 0, axis_index_groups=groups)]
    all_to_all x1, starting transfers between devices: 5.05 us -> 7.42 us  [local(): whole = lax.all_to_all(partial, 'tm', 0, 0)]
    ppermute x0 -> x1, waiting for transfers between devices: none -> 1.91 us  [local(): taken = lax.ppermute(give, 'tm', [(i, i ^ 1) for i in range(sources)])]
    pallas_call x1 -> x2, Pallas kernels: 4.65 us -> 4.83 us  [the longest x1 4.66 us: local(): call(cell_body, 'cells', (shape((half, share, 12 * lanes), BF), shape((ha...]
  transfers between devices with their start and end apart: 4 -> 5, of which waited for: 3 -> 4; matrix products, arithmetic and copies ran while one was open for 0% -> 0% of each run, Pallas kernels for 4% -> 5%
where the time goes in v5:
time: 96.5 us; the launch traced here: 96.1 us
  blocking collectives  44.1 us (46%)
  starting transfers between devices  18.4 us (19%)
  waiting for transfers between devices  17.2 us (18%)
  Pallas kernels  13 us (13%)
  local copies, waits for them, and re-layouts  2.61 us (3%)
    all_to_all x1, blocking collectives, local(): got = lax.all_to_all(send, 'tm', 0, 0)  27.2 us
    all_to_all x1, blocking collectives, local(): got = lax.all_to_all(send, 'tm', 0, 0, axis_index_groups=groups)  16.9 us
    all_to_all x1, starting transfers between devices, local(): whole = lax.all_to_all(partial, 'tm', 0, 0)  7.42 us
    ppermute x1, waiting for transfers between devices, local(): edge = lax.ppermute(edge, 'row', down)  5.65 us
    all_to_all x1, starting transfers between devices, local(): partial = lax.all_to_all(partial, 'row', 0, 0)  5.29 us
    all_to_all x1, waiting for transfers between devices, local(): whole = lax.all_to_all(partial, 'tm', 0, 0)  5.15 us
    pallas_call x1, Pallas kernels, local(): call(cell_body, 'cells', (shape((half, share, 12 * lanes), BF), shape((ha...  4.66 us
    all_to_all x1, waiting for transfers between devices, local(): partial = lax.all_to_all(partial, 'row', 0, 0)  4.46 us
  transfers between devices with their start and end apart: 5, of which 4 were waited for; matrix products, arithmetic and copies ran while one was open for 0% of the time, Pallas kernels for 5%

profile of v5, /device:TPU:1, one launch (start us, length us, event | category | flops | bytes accessed | tf_op | source)
XLA Modules:
  0.0 96.1 jit_solution(12522061909885412066)
XLA Ops:
  0.6 1.7 %halo.1 = (bf16[392,256]{1,0:T(8,128)(2,1)}, f32[8,256]{1,0:T(8,128)}) custom-call(bf16[2,4,64,256]{3,2,1,0:T(8,128)(2,1)} %frames.3, bf16[2,4,64,256]{3,2,1,0:T(8,128)(2,1)} %refs_3_.1, f32[4,64,256]{2,1,0:T(8,128)} %start.1), custom_call_target="tpu_custom_call" | custom-call | flops 1048576 | bytes 1048576 | tf_op jit(solution)/shard_map/halo/pallas_call | solution.py:403
  2.3 2.5 %collective-permute-start = (bf16[392,256]{1,0:T(8,128)(2,1)}, bf16[392,256]{1,0:T(8,128)(2,1)S(1)}, u32[]{:S(2)}, u32[]{:S(2)}) collective-permute-start(bf16[392,256]{1,0:T(8,128)(2,1)} %get-tuple-element.17), channel_id=1, source_target_pairs={{0,1},{1,2},{2,3},{3,4},{4,5},{5,6},{6,7},{7,0},{8,9},{9,10},{10,1... | collective-permute-start | bytes 602120 | tf_op jit(solution)/shard_map/ppermute | solution.py:416
  4.8 0.9 copy-done.1
  5.8 0.9 copy-done.3
  6.8 0.7 copy-done.5
  7.4 0.6 own.1
  8.0 5.7 %collective-permute-done.halo = bf16[392,256]{1,0:T(8,128)(2,1)S(1)} collective-permute-done((bf16[392,256]{1,0:T(8,128)(2,1)}, bf16[392,256]{1,0:T(8,128)(2,1)S(1)}, u32[]{:S(2)}, u32[]{:S(2)}) %collective-permute-start) | collective-permute-done | bytes 200736 | tf_op jit(solution)/shard_map/ppermute | solution.py:416
  13.7 0.3 spread.1
  14.0 0.0 copy-start
  14.0 0.0 copy-start.6
  14.0 0.0 copy-start.7
  14.0 27.2 %all_to_all.20.got = bf16[32,72,256]{2,1,0:T(8,128)(2,1)S(1)} all-to-all(bf16[32,72,256]{2,1,0:T(8,128)(2,1)S(1)} %spread.1), channel_id=1, replica_groups=mesh['tm'=32,'row'=8] {'tm'}, dimensions={0} | all-to-all | bytes 2359296 | tf_op jit(solution)/shard_map/all_to_all | solution.py:443
  41.2 0.0 copy-done
  41.2 0.0 copy-done.6
  41.2 0.0 copy-done.7
  41.2 4.7 %cells.1 = (bf16[16,8,3072]{2,1,0:T(8,128)(2,1)S(1)}, f32[16,8,2560]{2,1,0:T(8,128)S(1)}, bf16[16,8,512]{2,1,0:T(8,128)(2,1)S(1)}) custom-call(bf16[32,72,256]{2,1,0:T(8,128)(2,1)S(1)} %all_to_all.20.got, bf16[2304,256]{1,0:T(8,128)(2,1)S(1)} %bitcast.3, bf16[256,256]{1,0:T(8,128)(2,1)S(1)} %copy-done.6, f32[8,256]{1,0:T(8,128)S(1)} %copy-done.7, ...), custom_call_target="tpu_custom_call" | custom-call | flops 1409286144 | bytes 4194304 | tf_op jit(solution)/shard_map/cells/pallas_call | solution.py:445
  45.9 0.5 collective-permute-start.1
  46.4 1.9 %collective-permute-done.1.taken = bf16[16,8,3072]{2,1,0:T(8,128)(2,1)S(1)} collective-permute-done((bf16[16,8,3072]{2,1,0:T(8,128)(2,1)S(1)}, bf16[16,8,3072]{2,1,0:T(8,128)(2,1)S(1)}, u32[]{:S(2)}, u32[]{:S(2)}) %collective-permute-start.1) | collective-permute-done | bytes 786464 | tf_op jit(solution)/shard_map/ppermute | solution.py:468
  48.3 0.2 merge.1
  48.5 16.9 %all_to_all.21.got = bf16[16,8,3584]{2,1,0:T(8,128)(2,1)S(1)} all-to-all(bf16[16,8,3584]{2,1,0:T(8,128)(2,1)S(1)} %merge.1), channel_id=1, replica_groups={{0,16,32,48,64,80,96,112,128,144,160,176,192,208,224,240},{8,24,40,56,7..., dimensions={0} | all-to-all | bytes 1835008 | tf_op jit(solution)/shard_map/all_to_all | solution.py:471
  65.4 1.0 %join.1 = (bf16[8,8,320]{2,1,0:T(8,128)(2,1)}, bf16[2,4,64,256]{3,2,1,0:T(8,128)(2,1)S(1)}, bf16[2,2,64,256]{3,2,1,0:T(8,128)(2,1)S(1)}) custom-call(bf16[16,8,3584]{2,1,0:T(8,128)(2,1)S(1)} %all_to_all.21.got), custom_call_target="tpu_custom_call" | custom-call | flops 1048576 | bytes 1048576 | tf_op jit(solution)/shard_map/join/pallas_call | solution.py:472
  66.4 5.3 %all-to-all-start.2 = ((bf16[8,8,320]{2,1,0:T(8,128)(2,1)}), bf16[8,8,320]{2,1,0:T(8,128)(2,1)S(1)}, u32[]{:S(2)}, u32[]{:S(2)}) async-start(bf16[8,8,320]{2,1,0:T(8,128)(2,1)} %get-tuple-element.24), calls=%async_computation.2 | async-start | bytes 98304 | tf_op jit(solution)/shard_map/all_to_all | solution.py:484
  71.7 2.7 %collective-permute-start.2 = (bf16[2,2,64,256]{3,2,1,0:T(8,128)(2,1)S(1)}, bf16[2,2,64,256]{3,2,1,0:T(8,128)(2,1)S(1)}, u32[]{:S(2)}, u32[]{:S(2)}) collective-permute-start(bf16[2,2,64,256]{3,2,1,0:T(8,128)(2,1)S(1)} %get-tuple-element.23), channel_id=1, source_target_pairs={{1,0},{2,1},{3,2},{4,3},{5,4},{6,5},{7,6},{0,7},{9,8},{10,9},{11,1... | collective-permute-start | bytes 393224 | tf_op jit(solution)/shard_map/ppermute | solution.py:483
  74.3 4.5 %all-to-all-done.2.got = bf16[8,8,320]{2,1,0:T(8,128)(2,1)S(1)} async-done(((bf16[8,8,320]{2,1,0:T(8,128)(2,1)}), bf16[8,8,320]{2,1,0:T(8,128)(2,1)S(1)}, u32[]{:S(2)}, u32[]{:S(2)}) %all-to-all-start.2) | async-done | bytes 40992 | tf_op jit(solution)/shard_map/all_to_all | solution.py:484
  78.8 0.7 sum.1
  79.5 7.4 %all-to-all-start.3 = ((bf16[32,8,320]{2,1,0:T(8,128)(2,1)}), bf16[32,8,320]{2,1,0:T(8,128)(2,1)S(1)}, u32[]{:S(2)}, u32[]{:S(2)}) async-start(bf16[32,8,320]{2,1,0:T(8,128)(2,1)} %sum.1), calls=%async_computation.3 | async-start | bytes 393216 | tf_op jit(solution)/shard_map/all_to_all | solution.py:513
  86.9 0.0 copy-done.2
  86.9 1.6 %back.2.refs_5_ = bf16[2,4,64,256]{3,2,1,0:T(8,128)(2,1)} custom-call(bf16[2,4,64,256]{3,2,1,0:T(8,128)(2,1)S(1)} %get-tuple-element.22.refs_0_, bf16[9,256,256]{2,1,0:T(8,128)(2,1)S(1)} %copy-done, bf16[2,4,64,256]{3,2,1,0:T(8,128)(2,1)S(1)} %copy-done.2, f32[1,256]{1,0:T(1,128)S(1)} %bitcast.4), custom_call_target="tpu_custom_call" | custom-call | flops 301989888 | bytes 2097152 | tf_op jit(solution)/shard_map/back/pallas_call | solution.py:509
  88.5 0.0 collective-permute-done.2.refs_1_
  88.5 1.6 %back.3 = bf16[2,4,64,256]{3,2,1,0:T(8,128)(2,1)} custom-call(bf16[2,4,64,256]{3,2,1,0:T(8,128)(2,1)S(1)} %get-tuple-element.22.refs_0_, bf16[2,2,64,256]{3,2,1,0:T(8,128)(2,1)S(1)} %collective-permute-done.2.refs_1_, bf16[9,256,256]{2,1,0:T(8,128)(2,1)S(1)} %copy-done, bf16[2,4,64,256]{3,2,1,0:T(8,128)(2,1)S(1)} %copy-done.2, ...), custom_call_target="tpu_custom_call", output_to_operand_aliasing={{}: (5, {})} | custom-call | flops 301989888 | bytes 2097152 | tf_op jit(solution)/shard_map/back/pallas_call | solution.py:510
  90.1 5.1 %all-to-all-done.3.got = bf16[32,8,320]{2,1,0:T(8,128)(2,1)S(1)} async-done(((bf16[32,8,320]{2,1,0:T(8,128)(2,1)}), bf16[32,8,320]{2,1,0:T(8,128)(2,1)S(1)}, u32[]{:S(2)}, u32[]{:S(2)}) %all-to-all-start.3) | async-done | bytes 163872 | tf_op jit(solution)/shard_map/all_to_all | solution.py:513
  95.2 0.9 last.1
  (6 shorter events, 0.0 us)
Async XLA Ops:
  2.3 11.4 %collective-permute-start = (bf16[392,256]{1,0:T(8,128)(2,1)}, bf16[392,256]{1,0:T(8,128)(2,1)S(1)}, u32[]{:S(2)}, u32[]{:S(2)}) collective-permute-start(bf16[392,256]{1,0:T(8,128)(2,1)} %get-tuple-element.17), channel_id=1, source_target_pairs={{0,1},{1,2},{2,3},{3,4},{4,5},{5,6},{6,7},{7,0},{8,9},{9,10},{10,1... | collective-permute-start | bytes 602120 | tf_op jit(solution)/shard_map/ppermute | solution.py:416
  4.8 0.9 copy-start.1
  5.8 0.9 copy-start.3
  6.7 0.7 copy-start.5
  14.0 27.2 %copy-start = (bf16[9,256,256]{2,1,0:T(8,128)(2,1)S(1)}, bf16[9,256,256]{2,1,0:T(8,128)(2,1)}, u32[]{:S(2)}) copy-start(bf16[9,256,256]{2,1,0:T(8,128)(2,1)} %refs_2_.3) | copy-start | bytes 3538948
  14.0 27.2 %copy-start.6 = (bf16[256,256]{1,0:T(8,128)(2,1)S(1)}, bf16[256,256]{1,0:T(8,128)(2,1)}, u32[]{:S(2)}) copy-start(bf16[256,256]{1,0:T(8,128)(2,1)} %readout.1) | copy-start | bytes 393220
  14.0 27.2 %copy-start.7 = (f32[8,256]{1,0:T(8,128)S(1)}, f32[8,256]{1,0:T(8,128)}, u32[]{:S(2)}) copy-start(f32[8,256]{1,0:T(8,128)} %get-tuple-element.18.start) | copy-start | bytes 24580
  45.9 2.4 %collective-permute-start.1 = (bf16[16,8,3072]{2,1,0:T(8,128)(2,1)S(1)}, bf16[16,8,3072]{2,1,0:T(8,128)(2,1)S(1)}, u32[]{:S(2)}, u32[]{:S(2)}) collective-permute-start(bf16[16,8,3072]{2,1,0:T(8,128)(2,1)S(1)} %get-tuple-element.19), channel_id=1, source_target_pairs={{0,8},{8,0},{16,24},{24,16},{32,40},{40,32},{48,56},{56,48},{64,72... | collective-permute-start | bytes 2359304 | tf_op jit(solution)/shard_map/ppermute | solution.py:468
  65.4 21.5 %copy-start.2 = (bf16[2,4,64,256]{3,2,1,0:T(8,128)(2,1)S(1)}, bf16[2,4,64,256]{3,2,1,0:T(8,128)(2,1)}, u32[]{:S(2)}) copy-start(bf16[2,4,64,256]{3,2,1,0:T(8,128)(2,1)} %refs_3_.1) | copy-start | bytes 786436
  65.4 21.5 %copy-start.4 = (f32[256]{0:T(256)S(1)}, f32[256]{0:T(256)}, u32[]{:S(2)}) copy-start(f32[256]{0:T(256)} %param.11) | copy-start | bytes 3076
  66.4 12.4 %all-to-all-start.2 = ((bf16[8,8,320]{2,1,0:T(8,128)(2,1)}), bf16[8,8,320]{2,1,0:T(8,128)(2,1)S(1)}, u32[]{:S(2)}, u32[]{:S(2)}) async-start(bf16[8,8,320]{2,1,0:T(8,128)(2,1)} %get-tuple-element.24), calls=%async_computation.2 | async-start | bytes 98304 | tf_op jit(solution)/shard_map/all_to_all | solution.py:484
  71.7 16.9 %collective-permute-start.2 = (bf16[2,2,64,256]{3,2,1,0:T(8,128)(2,1)S(1)}, bf16[2,2,64,256]{3,2,1,0:T(8,128)(2,1)S(1)}, u32[]{:S(2)}, u32[]{:S(2)}) collective-permute-start(bf16[2,2,64,256]{3,2,1,0:T(8,128)(2,1)S(1)} %get-tuple-element.23), channel_id=1, source_target_pairs={{1,0},{2,1},{3,2},{4,3},{5,4},{6,5},{7,6},{0,7},{9,8},{10,9},{11,1... | collective-permute-start | bytes 393224 | tf_op jit(solution)/shard_map/ppermute | solution.py:483
  79.5 15.7 %all-to-all-start.3 = ((bf16[32,8,320]{2,1,0:T(8,128)(2,1)}), bf16[32,8,320]{2,1,0:T(8,128)(2,1)S(1)}, u32[]{:S(2)}, u32[]{:S(2)}) async-start(bf16[32,8,320]{2,1,0:T(8,128)(2,1)} %sum.1), calls=%async_computation.3 | async-start | bytes 393216 | tf_op jit(solution)/shard_map/all_to_all | solution.py:513

commit v6 on v5

--- a/solution.py
+++ b/solution.py
@@ -13,7 +13,7 @@
 BF = jnp.bfloat16
 F32 = jnp.float32
 PAD = 8
-CELLS = ((0, 0), (0, 1), (2, 0), (2, 1), (1, 0), (1, 1), (3, 0), (3, 1))
+CELLS = ((0, 0), (0, 1), (1, 0), (1, 1), (2, 0), (2, 1), (3, 0), (3, 1))
 VMEM = pl.BlockSpec(memory_space=pltpu.VMEM)
 HBM = pl.BlockSpec(memory_space=pltpu.MemorySpace.HBM)
 
@@ -72,7 +72,7 @@
     offset = 2 * (mine % 4)
     step = sublane(begin.shape)
     total = jnp.zeros(begin.shape, F32)
-    for place, row in ((2, 1), (4, 0), (6, 2)):
+    for place, row in ((2, 0), (4, 1), (6, 2)):
         moved = pltpu.roll(starts[row], (8 + place - offset) % 8, 0)
         total = jnp.where((step >= place) & (step < place + 2), moved, total)
     begin[...] = total
@@ -83,8 +83,13 @@
     out[pl.ds(6 * wide, 8), :] = total.astype(BF)
 
 
-def own_body(frames, cotangent, decay, out, pieces, grid, slopes, rows, given, rates, parts, sems):
+def places(pair, chips):
+    return [(chip, pair - 2 * chip) for chip in range(chips) if 0 <= pair - 2 * chip <= 2]
+
+
+def own_body(frames, cotangent, decay, out, grid, slopes, rows, given, rates, parts, sems):
     wide, lanes = frames.shape[2:]
+    chips = out.shape[0]
     copies = (
         pltpu.make_async_copy(frames, rows, sems.at[0]),
         pltpu.make_async_copy(cotangent, given, sems.at[1]),
@@ -106,28 +111,41 @@
     for place, piece in enumerate(split3(rates[...])):
         parts[2 * place : 2 * place + 2, :] = piece
     parts[6:8, :] = jnp.zeros((2, lanes), F32)
-    pieces[...] = parts[...].astype(BF)
     step = sublane((8, lanes))
+
+    def stack(f, terms, first):
+        block = None
+        for place, row in terms:
+            value = grid[f, row, first - place : first - place + 8, :]
+            block = value if block is None else jnp.where(step < place, block, value)
+        return block.astype(BF)
+
+    for pair in range(wide // 2 + 1):
+        first = PAD + 2 * pair - 1
+        blocks = (
+            stack(0, ((4, 0), (6, 1)), first),
+            stack(0, ((0, 2), (2, 3)), first),
+            stack(1, ((0, 0), (2, 1), (4, 2), (6, 3)), first),
+        )
+        for chip, place in places(pair, chips):
+            for group in range(3):
+                out[chip, 24 * place + 8 * group : 24 * place + 8 * group + 8, :] = blocks[group]
     for target in range(wide // 2):
         first = PAD + 2 * target
         for f in range(2):
-            for pair in range(2):
-                start = first - 1
-                block = jnp.where(
-                    step < 4,
-                    grid[f, 2 * pair, start : start + 8, :],
-                    grid[f, 2 * pair + 1, start - 4 : start + 4, :],
-                )
-                out[target, 16 * f + 8 * pair : 16 * f + 8 * pair + 8, :] = block.astype(BF)
-            block = slopes[f, 1, first - 2 : first + 6, :]
-            for place, row in ((4, 0), (6, 2)):
+            block = slopes[f, 0, first - 2 : first + 6, :]
+            for place, row in ((4, 1), (6, 2)):
                 block = jnp.where(step < place, block, slopes[f, row, first - place : first - place + 8, :])
-            out[target, 32 + 8 * f : 40 + 8 * f, :] = block.astype(BF)
-
-
-def spread_body(own, pieces, halo, out, grid, slopes):
+            row = 72 + 16 * (target % 2) + 8 * f
+            out[target // 2, row : row + 8, :] = block.astype(BF)
+    for chip in range(chips):
+        out[chip, 104:112, :] = parts[...].astype(BF)
+
+
+def spread_body(own, halo, out, grid, slopes):
     wide = (halo.shape[0] - 8) // 6
     lanes = halo.shape[1]
+    chips = out.shape[0]
     for f in range(2):
         for row in range(2):
             grid[f, row, 0:PAD, :] = jnp.zeros((PAD, lanes), F32)
@@ -135,55 +153,99 @@
             grid[f, row, PAD : PAD + wide, :] = halo[pl.ds((2 * f + row) * wide, wide), :].astype(F32)
         slopes[f, PAD : PAD + wide, :] = halo[pl.ds((4 + f) * wide, wide), :].astype(F32)
     step = sublane((8, lanes))
+    for pair in range(wide // 2 + 1):
+        first = PAD + 2 * pair - 1
+        upper = jnp.where(step < 2, grid[0, 0, first : first + 8, :], grid[0, 1, first - 2 : first + 6, :])
+        lower = jnp.where(step < 6, grid[1, 0, first - 4 : first + 4, :], grid[1, 1, first - 6 : first + 2, :])
+        for chip, place in places(pair, chips):
+            row = 24 * place
+            block = jnp.where(step < 4, upper, own[chip, row : row + 8, :].astype(F32))
+            out[chip, row : row + 8, :] = block.astype(BF)
+            block = jnp.where(step < 4, own[chip, row + 8 : row + 16, :].astype(F32), lower)
+            out[chip, row + 8 : row + 16, :] = block.astype(BF)
+            out[chip, row + 16 : row + 24, :] = own[chip, row + 16 : row + 24, :]
     for target in range(wide // 2):
         first = PAD + 2 * target
         for f in range(2):
-            start = first - 1
-            block = jnp.where(step < 4, grid[f, 0, start : start + 8, :], grid[f, 1, start - 4 : start + 4, :])
-            out[target, 32 * f : 32 * f + 8, :] = block.astype(BF)
-            out[target, 32 * f + 8 : 32 * f + 24, :] = own[target, 16 * f : 16 * f + 16, :]
-            block = own[target, 32 + 8 * f : 40 + 8 * f, :].astype(F32)
+            row = 72 + 16 * (target % 2) + 8 * f
+            block = own[target // 2, row : row + 8, :].astype(F32)
             block = jnp.where(step < 2, slopes[f, first : first + 8, :], block)
-            out[target, 32 * f + 24 : 32 * f + 32, :] = block.astype(BF)
-        out[target, 64:72, :] = pieces[...]
+            out[target // 2, row : row + 8, :] = block.astype(BF)
+    for chip in range(chips):
+        out[chip, 104:112, :] = own[chip, 104:112, :]
 
 
 def cell_body(
-    got, kernel, readout, start, halo, give, keep, stay, grid, decay, gain, taps, driven, states, slopes, drive, turned
+    mine,
+    theirs,
+    kernel,
+    readout,
+    start,
+    halo,
+    give,
+    keep,
+    stay,
+    grid,
+    upstream,
+    decay,
+    gain,
+    taps,
+    driven,
+    states,
+    slopes,
+    drive,
+    turned,
 ):
-    sources = got.shape[0]
+    sources = 2 * mine.shape[0]
     count = sources * 16
     wide = (halo.shape[0] - 8) // 6
-    lanes = got.shape[2]
+    lanes = mine.shape[2]
+    core = lax.axis_index("tm") % 2
     step = sublane((8, lanes))
     is_first = lax.axis_index("row") == 0
     low = jnp.where(is_first & (step < 2), 0.0, 1.0)
-    high = jnp.where(is_first & (step >= 4) & (step < 6), 0.0, 1.0)
-    near = (step % 4) < 2
-
-    def unpack(source, _):
-        for f in range(2):
-            grid[2 * source + f] = got[source, 32 * f : 32 * f + 24, :].astype(F32)
-        piece = got[source, 64:72, :].astype(F32)
-        rate = piece + pltpu.roll(piece, 6, 0) + pltpu.roll(piece, 4, 0)
-        decay[source] = rate
-        gain[source] = jnp.sqrt(1.0 - rate * rate)
+    high = jnp.where(is_first & (step >= 2) & (step < 4), 0.0, 1.0)
+    is_left = (step % 2) == 0
+
+    def unpack(chip, _):
+        for buffer, other in ((mine, core), (theirs, 1 - core)):
+            source = 2 * chip + other
+            for part in range(2):
+                first = 24 * core + 24 * part
+                group = [
+                    buffer[chip, pl.ds(pl.multiple_of(first + 8 * g, 8), 8), :].astype(F32) for g in range(3)
+                ]
+                grid[2 * source, part, 8:16, :] = group[0]
+                grid[2 * source, part, 16:24, :] = group[1]
+                grid[2 * source + 1, part, 8:16, :] = group[1]
+                grid[2 * source + 1, part, 16:24, :] = group[2]
+            for f in range(2):
+                first = pl.multiple_of(72 + 16 * core + 8 * f, 8)
+                upstream[2 * source + f] = buffer[chip, pl.ds(first, 8), :].astype(F32)
+            piece = buffer[chip, 104:112, :].astype(F32)
+            rate = piece + pltpu.roll(piece, 6, 0) + pltpu.roll(piece, 4, 0)
+            decay[source] = rate
+            gain[source] = jnp.sqrt(1.0 - rate * rate)
         return _
 
-    lax.fori_loop(0, sources, unpack, 0, unroll=4)
+    lax.fori_loop(0, sources // 2, unpack, 0, unroll=2)
 
     def gather(source, _):
         rows = pl.ds(pl.multiple_of(16 * source, 16), 16)
         for i in range(3):
             for j in range(3):
-                place = 4 * i + j
                 pair = []
                 for f in range(2):
-                    value = jnp.where(
-                        near,
-                        grid[2 * source + f, place : place + 8, :],
-                        grid[2 * source + f, place + 6 : place + 14, :],
-                    )
+                    frame = 2 * source + f
+                    first = 8 + 4 * f + 2 * i
+                    if j == 1:
+                        value = jnp.where(
+                            is_left,
+                            grid[frame, 0, first + 1 : first + 9, :],
+                            grid[frame, 1, first - 1 : first + 7, :],
+                        )
+                    else:
+                        value = grid[frame, j // 2, first : first + 8, :]
                     if i == 2:
                         value = value * low
                     if i == 0:
@@ -224,15 +286,8 @@
     def mix(part, _):
         rows = pl.ds(pl.multiple_of(part * 64, 64), 64)
         mixture = jnp.dot(states[rows, :], readout[...], preferred_element_type=F32)
-        upstream = jnp.concatenate(
-            [
-                got[4 * part + source, 32 * f + 24 : 32 * f + 32, :].astype(F32)
-                for source in range(4)
-                for f in range(2)
-            ],
-            axis=0,
-        )
-        slope = (upstream * gelu_slope(mixture)).astype(BF)
+        given = upstream[pl.ds(pl.multiple_of(part * 8, 8), 8)].reshape(64, lanes)
+        slope = (given * gelu_slope(mixture)).astype(BF)
         slopes[rows, :] = slope
         driven[rows, :] = lax.dot_general(
             slope, readout[...], (((1,), (1,)), ((), ())), preferred_element_type=F32
@@ -414,10 +469,13 @@
         grant=63 << 20,
     )(frames_in, cotangent, start_state)
     edge = lax.ppermute(edge, "row", down)
-    own, pieces = call(
+    half = sources // 2
+    groups = [[2 * chip + core for chip in range(half)] for core in range(2)]
+    swap = [(i, i ^ 1) for i in range(sources)]
+    own = call(
         own_body,
         "own",
-        (shape((sources, 48, lanes), BF), shape((8, lanes), BF)),
+        shape((half, 112, lanes), BF),
         [HBM] * 3,
         [
             pltpu.VMEM((2, 4, wide + 2 * PAD, lanes), F32),
@@ -433,15 +491,15 @@
     send = call(
         spread_body,
         "spread",
-        shape((sources, 72, lanes), BF),
-        [VMEM] * 3,
+        shape((half, 112, lanes), BF),
+        [VMEM] * 2,
         [
             pltpu.VMEM((2, 2, wide + 2 * PAD, lanes), F32),
             pltpu.VMEM((2, wide + 2 * PAD, lanes), F32),
         ],
-    )(own, pieces, edge)
-    got = lax.all_to_all(send, "tm", 0, 0)
-    half = sources // 2
+    )(own, edge)
+    mine = lax.all_to_all(send, "tm", 0, 0, axis_index_groups=groups)
+    theirs = lax.ppermute(mine, "tm", swap)
     give, keep, stay = call(
         cell_body,
         "cells",
@@ -450,9 +508,10 @@
             shape((half, share, 10 * lanes), F32),
             shape((half, 8, 2 * lanes), BF),
         ),
-        [VMEM] * 5,
+        [VMEM] * 6,
         [
-            pltpu.VMEM((2 * sources, 24, lanes), F32),
+            pltpu.VMEM((2 * sources, 2, 32, lanes), F32),
+            pltpu.VMEM((2 * sources, 8, lanes), F32),
             pltpu.VMEM((sources, 8, lanes), F32),
             pltpu.VMEM((sources, 8, lanes), F32),
             pltpu.VMEM((cells, 9 * lanes), BF),
@@ -464,10 +523,9 @@
         ],
         flops=2 * cells * lanes * lanes * 21,
         moved=4 << 20,
-    )(got, kernel.reshape(9 * lanes, lanes), readout, begin, edge)
-    taken = lax.ppermute(give, "tm", [(i, i ^ 1) for i in range(sources)])
+    )(mine, theirs, kernel.reshape(9 * lanes, lanes), readout, begin, edge)
+    taken = lax.ppermute(give, "tm", swap)
     send = call(merge_body, "merge", shape((half, share, 14 * lanes), BF), [VMEM] * 3, [])(taken, keep, stay)
-    groups = [[2 * chip + core for chip in range(half)] for core in range(2)]
     got = lax.all_to_all(send, "tm", 0, 0, axis_index_groups=groups)
     partial, drive, top = call(
         functools.partial(join_body, bands),

time: 96.5 us -> 94.8 us (0.982)
  blocking collectives: 44.1 us -> 37.9 us
  starting transfers between devices: 18.4 us -> 20.7 us
  waiting for transfers between devices: 17.2 us -> 19.3 us
    all_to_all x1, blocking collectives: 27.2 us -> 20.5 us  [local(): mine = lax.all_to_all(send, 'tm', 0, 0, axis_index_groups=groups)]
    ppermute x1 -> x2, starting transfers between devices: 0.49 us -> 3.06 us  [the longest x1 2.6 us: local(): theirs = lax.ppermute(mine, 'tm', swap)]
    ppermute x1 -> x2, waiting for transfers between devices: 1.91 us -> 4.01 us  [the longest x1 2.1 us: local(): theirs = lax.ppermute(mine, 'tm', swap)]
  transfers between devices with their start and end apart: 5 -> 6, of which waited for: 4 -> 5; matrix products, arithmetic and copies ran while one was open for 0% -> 0% of each run, Pallas kernels for 5% -> 5%
where the time goes in v6:
time: 94.8 us; the launch traced here: 94.4 us
  blocking collectives  37.9 us (40%)
  starting transfers between devices  20.7 us (22%)
  waiting for transfers between devices  19.3 us (20%)
  Pallas kernels  13.1 us (14%)
  local copies, waits for them, and re-layouts  2.61 us (3%)
    all_to_all x1, blocking collectives, local(): mine = lax.all_to_all(send, 'tm', 0, 0, axis_index_groups=groups)  20.5 us
    all_to_all x1, blocking collectives, local(): got = lax.all_to_all(send, 'tm', 0, 0, axis_index_groups=groups)  17.5 us
    all_to_all x1, starting transfers between devices, local(): whole = lax.all_to_all(partial, 'tm', 0, 0)  7.42 us
    ppermute x1, waiting for transfers between devices, local(): edge = lax.ppermute(edge, 'row', down)  5.64 us
    all_to_all x1, waiting for transfers between devices, local(): whole = lax.all_to_all(partial, 'tm', 0, 0)  5.14 us
    all_to_all x1, starting transfers between devices, local(): partial = lax.all_to_all(partial, 'row', 0, 0)  5.05 us
    pallas_call x1, Pallas kernels, local(): call(cell_body, 'cells', (shape((half, share, 12 * lanes), BF), shape((ha...  4.63 us
    all_to_all x1, waiting for transfers between devices, local(): partial = lax.all_to_all(partial, 'row', 0, 0)  4.46 us
  transfers between devices with their start and end apart: 6, of which 5 were waited for; matrix products, arithmetic and copies ran while one was open for 0% of the time, Pallas kernels for 5%

profile of v6, /device:TPU:1, one launch (start us, length us, event | category | flops | bytes accessed | tf_op | source)
XLA Modules:
  0.0 94.4 jit_solution(17255878256670788205)
XLA Ops:
  0.6 1.7 %halo.1 = (bf16[392,256]{1,0:T(8,128)(2,1)}, f32[8,256]{1,0:T(8,128)}) custom-call(bf16[2,4,64,256]{3,2,1,0:T(8,128)(2,1)} %frames.3, bf16[2,4,64,256]{3,2,1,0:T(8,128)(2,1)} %refs_3_.1, f32[4,64,256]{2,1,0:T(8,128)} %start.1), custom_call_target="tpu_custom_call" | custom-call | flops 1048576 | bytes 1048576 | tf_op jit(solution)/shard_map/halo/pallas_call | solution.py:458
  2.3 2.5 %collective-permute-start = (bf16[392,256]{1,0:T(8,128)(2,1)}, bf16[392,256]{1,0:T(8,128)(2,1)S(1)}, u32[]{:S(2)}, u32[]{:S(2)}) collective-permute-start(bf16[392,256]{1,0:T(8,128)(2,1)} %get-tuple-element.13), channel_id=1, source_target_pairs={{0,1},{1,2},{2,3},{3,4},{4,5},{5,6},{6,7},{7,0},{8,9},{9,10},{10,1... | collective-permute-start | bytes 602120 | tf_op jit(solution)/shard_map/ppermute | solution.py:471
  4.8 0.9 %copy-done.1 = bf16[2,4,64,256]{3,2,1,0:T(8,128)(2,1)S(1)} copy-done((bf16[2,4,64,256]{3,2,1,0:T(8,128)(2,1)S(1)}, bf16[2,4,64,256]{3,2,1,0:T(8,128)(2,1)}, u32[]{:S(2)}) %copy-start.1) | copy-done | bytes 262168
  5.8 0.9 %copy-done.3 = bf16[2,4,64,256]{3,2,1,0:T(8,128)(2,1)S(1)} copy-done((bf16[2,4,64,256]{3,2,1,0:T(8,128)(2,1)S(1)}, bf16[2,4,64,256]{3,2,1,0:T(8,128)(2,1)}, u32[]{:S(2)}) %copy-start.3) | copy-done | bytes 262168
  6.8 0.7 copy-done.5
  7.4 0.6 own.1
  8.0 5.6 %collective-permute-done.halo = bf16[392,256]{1,0:T(8,128)(2,1)S(1)} collective-permute-done((bf16[392,256]{1,0:T(8,128)(2,1)}, bf16[392,256]{1,0:T(8,128)(2,1)S(1)}, u32[]{:S(2)}, u32[]{:S(2)}) %collective-permute-start) | collective-permute-done | bytes 200736 | tf_op jit(solution)/shard_map/ppermute | solution.py:471
  13.7 0.3 spread.1
  14.0 0.0 copy-start
  14.0 0.0 copy-start.6
  14.0 0.0 copy-start.7
  14.1 20.5 %all_to_all.20.mine = bf16[16,112,256]{2,1,0:T(8,128)(2,1)S(1)} all-to-all(bf16[16,112,256]{2,1,0:T(8,128)(2,1)S(1)} %spread.1), channel_id=1, replica_groups={{0,16,32,48,64,80,96,112,128,144,160,176,192,208,224,240},{8,24,40,56,7..., dimensions={0} | all-to-all | bytes 1835008 | tf_op jit(solution)/shard_map/all_to_all | solution.py:501
  34.5 2.6 %collective-permute-start.1 = (bf16[16,112,256]{2,1,0:T(8,128)(2,1)S(1)}, bf16[16,112,256]{2,1,0:T(8,128)(2,1)S(1)}, u32[]{:S(2)}, u32[]{:S(2)}) collective-permute-start(bf16[16,112,256]{2,1,0:T(8,128)(2,1)S(1)} %all_to_all.20.mine), channel_id=1, source_target_pairs={{0,8},{8,0},{16,24},{24,16},{32,40},{40,32},{48,56},{56,48},{64,72... | collective-permute-start | bytes 2752520 | tf_op jit(solution)/shard_map/ppermute | solution.py:502
  37.1 2.1 %collective-permute-done.1.theirs = bf16[16,112,256]{2,1,0:T(8,128)(2,1)S(1)} collective-permute-done((bf16[16,112,256]{2,1,0:T(8,128)(2,1)S(1)}, bf16[16,112,256]{2,1,0:T(8,128)(2,1)S(1)}, u32[]{:S(2)}, u32[]{:S(2)}) %collective-permute-start.1) | collective-permute-done | bytes 917536 | tf_op jit(solution)/shard_map/ppermute | solution.py:502
  39.2 4.6 %cells.1 = (bf16[16,8,3072]{2,1,0:T(8,128)(2,1)S(1)}, f32[16,8,2560]{2,1,0:T(8,128)S(1)}, bf16[16,8,512]{2,1,0:T(8,128)(2,1)S(1)}) custom-call(bf16[16,112,256]{2,1,0:T(8,128)(2,1)S(1)} %all_to_all.20.mine, bf16[16,112,256]{2,1,0:T(8,128)(2,1)S(1)} %collective-permute-done.1.theirs, bf16[2304,256]{1,0:T(8,128)(2,1)S(1)} %bitcast.3, ...), custom_call_target="tpu_custom_call" | custom-call | flops 1409286144 | bytes 4194304 | tf_op jit(solution)/shard_map/cells/pallas_call | solution.py:503
  43.9 0.5 collective-permute-start.2
  44.4 1.9 %collective-permute-done.2.taken = bf16[16,8,3072]{2,1,0:T(8,128)(2,1)S(1)} collective-permute-done((bf16[16,8,3072]{2,1,0:T(8,128)(2,1)S(1)}, bf16[16,8,3072]{2,1,0:T(8,128)(2,1)S(1)}, u32[]{:S(2)}, u32[]{:S(2)}) %collective-permute-start.2) | collective-permute-done | bytes 786464 | tf_op jit(solution)/shard_map/ppermute | solution.py:527
  46.3 0.2 merge.1
  46.4 0.0 copy-start.2
  46.5 0.0 copy-start.4
  46.5 17.5 %all_to_all.21.got = bf16[16,8,3584]{2,1,0:T(8,128)(2,1)S(1)} all-to-all(bf16[16,8,3584]{2,1,0:T(8,128)(2,1)S(1)} %merge.1), channel_id=1, replica_groups={{0,16,32,48,64,80,96,112,128,144,160,176,192,208,224,240},{8,24,40,56,7..., dimensions={0} | all-to-all | bytes 1835008 | tf_op jit(solution)/shard_map/all_to_all | solution.py:529
  63.9 1.0 %join.1 = (bf16[8,8,320]{2,1,0:T(8,128)(2,1)}, bf16[2,4,64,256]{3,2,1,0:T(8,128)(2,1)S(1)}, bf16[2,2,64,256]{3,2,1,0:T(8,128)(2,1)S(1)}) custom-call(bf16[16,8,3584]{2,1,0:T(8,128)(2,1)S(1)} %all_to_all.21.got), custom_call_target="tpu_custom_call" | custom-call | flops 1048576 | bytes 1048576 | tf_op jit(solution)/shard_map/join/pallas_call | solution.py:530
  64.9 5.0 %all-to-all-start.2 = ((bf16[8,8,320]{2,1,0:T(8,128)(2,1)}), bf16[8,8,320]{2,1,0:T(8,128)(2,1)S(1)}, u32[]{:S(2)}, u32[]{:S(2)}) async-start(bf16[8,8,320]{2,1,0:T(8,128)(2,1)} %get-tuple-element.20), calls=%async_computation.2 | async-start | bytes 98304 | tf_op jit(solution)/shard_map/all_to_all | solution.py:542
  69.9 2.7 %collective-permute-start.3 = (bf16[2,2,64,256]{3,2,1,0:T(8,128)(2,1)S(1)}, bf16[2,2,64,256]{3,2,1,0:T(8,128)(2,1)S(1)}, u32[]{:S(2)}, u32[]{:S(2)}) collective-permute-start(bf16[2,2,64,256]{3,2,1,0:T(8,128)(2,1)S(1)} %get-tuple-element.19), channel_id=1, source_target_pairs={{1,0},{2,1},{3,2},{4,3},{5,4},{6,5},{7,6},{0,7},{9,8},{10,9},{11,1... | collective-permute-start | bytes 393224 | tf_op jit(solution)/shard_map/ppermute | solution.py:541
  72.6 4.5 %all-to-all-done.2.got = bf16[8,8,320]{2,1,0:T(8,128)(2,1)S(1)} async-done(((bf16[8,8,320]{2,1,0:T(8,128)(2,1)}), bf16[8,8,320]{2,1,0:T(8,128)(2,1)S(1)}, u32[]{:S(2)}, u32[]{:S(2)}) %all-to-all-start.2) | async-done | bytes 40992 | tf_op jit(solution)/shard_map/all_to_all | solution.py:542
  77.1 0.7 sum.1
  77.8 7.4 %all-to-all-start.3 = ((bf16[32,8,320]{2,1,0:T(8,128)(2,1)}), bf16[32,8,320]{2,1,0:T(8,128)(2,1)S(1)}, u32[]{:S(2)}, u32[]{:S(2)}) async-start(bf16[32,8,320]{2,1,0:T(8,128)(2,1)} %sum.1), calls=%async_computation.3 | async-start | bytes 393216 | tf_op jit(solution)/shard_map/all_to_all | solution.py:571
  85.2 1.6 %back.2.refs_5_ = bf16[2,4,64,256]{3,2,1,0:T(8,128)(2,1)} custom-call(bf16[2,4,64,256]{3,2,1,0:T(8,128)(2,1)S(1)} %get-tuple-element.18.refs_0_, bf16[9,256,256]{2,1,0:T(8,128)(2,1)S(1)} %copy-done, bf16[2,4,64,256]{3,2,1,0:T(8,128)(2,1)S(1)} %copy-done.2, f32[1,256]{1,0:T(1,128)S(1)} %bitcast.4), custom_call_target="tpu_custom_call" | custom-call | flops 301989888 | bytes 2097152 | tf_op jit(solution)/shard_map/back/pallas_call | solution.py:567
  86.8 0.0 collective-permute-done.3.refs_1_
  86.8 1.6 %back.3 = bf16[2,4,64,256]{3,2,1,0:T(8,128)(2,1)} custom-call(bf16[2,4,64,256]{3,2,1,0:T(8,128)(2,1)S(1)} %get-tuple-element.18.refs_0_, bf16[2,2,64,256]{3,2,1,0:T(8,128)(2,1)S(1)} %collective-permute-done.3.refs_1_, bf16[9,256,256]{2,1,0:T(8,128)(2,1)S(1)} %copy-done, bf16[2,4,64,256]{3,2,1,0:T(8,128)(2,1)S(1)} %copy-done.2, ...), custom_call_target="tpu_custom_call", output_to_operand_aliasing={{}: (5, {})} | custom-call | flops 301989888 | bytes 2097152 | tf_op jit(solution)/shard_map/back/pallas_call | solution.py:568
  88.4 5.1 %all-to-all-done.3.got = bf16[32,8,320]{2,1,0:T(8,128)(2,1)S(1)} async-done(((bf16[32,8,320]{2,1,0:T(8,128)(2,1)}), bf16[32,8,320]{2,1,0:T(8,128)(2,1)S(1)}, u32[]{:S(2)}, u32[]{:S(2)}) %all-to-all-start.3) | async-done | bytes 163872 | tf_op jit(solution)/shard_map/all_to_all | solution.py:571
  93.5 0.9 last.1
  (8 shorter events, 0.0 us)
Async XLA Ops:
  2.3 11.4 %collective-permute-start = (bf16[392,256]{1,0:T(8,128)(2,1)}, bf16[392,256]{1,0:T(8,128)(2,1)S(1)}, u32[]{:S(2)}, u32[]{:S(2)}) collective-permute-start(bf16[392,256]{1,0:T(8,128)(2,1)} %get-tuple-element.13), channel_id=1, source_target_pairs={{0,1},{1,2},{2,3},{3,4},{4,5},{5,6},{6,7},{7,0},{8,9},{9,10},{10,1... | collective-permute-start | bytes 602120 | tf_op jit(solution)/shard_map/ppermute | solution.py:471
  4.8 0.9 %copy-start.1 = (bf16[2,4,64,256]{3,2,1,0:T(8,128)(2,1)S(1)}, bf16[2,4,64,256]{3,2,1,0:T(8,128)(2,1)}, u32[]{:S(2)}) copy-start(bf16[2,4,64,256]{3,2,1,0:T(8,128)(2,1)} %refs_3_.1) | copy-start | bytes 786436
  5.8 0.9 %copy-start.3 = (bf16[2,4,64,256]{3,2,1,0:T(8,128)(2,1)S(1)}, bf16[2,4,64,256]{3,2,1,0:T(8,128)(2,1)}, u32[]{:S(2)}) copy-start(bf16[2,4,64,256]{3,2,1,0:T(8,128)(2,1)} %frames.3) | copy-start | bytes 786436
  6.7 0.7 copy-start.5
  14.0 25.2 %copy-start = (bf16[9,256,256]{2,1,0:T(8,128)(2,1)S(1)}, bf16[9,256,256]{2,1,0:T(8,128)(2,1)}, u32[]{:S(2)}) copy-start(bf16[9,256,256]{2,1,0:T(8,128)(2,1)} %refs_2_.3) | copy-start | bytes 3538948
  14.0 25.2 %copy-start.6 = (bf16[256,256]{1,0:T(8,128)(2,1)S(1)}, bf16[256,256]{1,0:T(8,128)(2,1)}, u32[]{:S(2)}) copy-start(bf16[256,256]{1,0:T(8,128)(2,1)} %readout.1) | copy-start | bytes 393220
  14.0 25.2 %copy-start.7 = (f32[8,256]{1,0:T(8,128)S(1)}, f32[8,256]{1,0:T(8,128)}, u32[]{:S(2)}) copy-start(f32[8,256]{1,0:T(8,128)} %get-tuple-element.14.start) | copy-start | bytes 24580
  34.5 4.7 %collective-permute-start.1 = (bf16[16,112,256]{2,1,0:T(8,128)(2,1)S(1)}, bf16[16,112,256]{2,1,0:T(8,128)(2,1)S(1)}, u32[]{:S(2)}, u32[]{:S(2)}) collective-permute-start(bf16[16,112,256]{2,1,0:T(8,128)(2,1)S(1)} %all_to_all.20.mine), channel_id=1, source_target_pairs={{0,8},{8,0},{16,24},{24,16},{32,40},{40,32},{48,56},{56,48},{64,72... | collective-permute-start | bytes 2752520 | tf_op jit(solution)/shard_map/ppermute | solution.py:502
  43.9 2.4 %collective-permute-start.2 = (bf16[16,8,3072]{2,1,0:T(8,128)(2,1)S(1)}, bf16[16,8,3072]{2,1,0:T(8,128)(2,1)S(1)}, u32[]{:S(2)}, u32[]{:S(2)}) collective-permute-start(bf16[16,8,3072]{2,1,0:T(8,128)(2,1)S(1)} %get-tuple-element.15), channel_id=1, source_target_pairs={{0,8},{8,0},{16,24},{24,16},{32,40},{40,32},{48,56},{56,48},{64,72... | collective-permute-start | bytes 2359304 | tf_op jit(solution)/shard_map/ppermute | solution.py:527
  46.4 38.8 %copy-start.2 = (bf16[2,4,64,256]{3,2,1,0:T(8,128)(2,1)S(1)}, bf16[2,4,64,256]{3,2,1,0:T(8,128)(2,1)}, u32[]{:S(2)}) copy-start(bf16[2,4,64,256]{3,2,1,0:T(8,128)(2,1)} %refs_3_.1) | copy-start | bytes 786436
  46.5 38.8 %copy-start.4 = (f32[256]{0:T(256)S(1)}, f32[256]{0:T(256)}, u32[]{:S(2)}) copy-start(f32[256]{0:T(256)} %param.11) | copy-start | bytes 3076
  64.9 12.2 %all-to-all-start.2 = ((bf16[8,8,320]{2,1,0:T(8,128)(2,1)}), bf16[8,8,320]{2,1,0:T(8,128)(2,1)S(1)}, u32[]{:S(2)}, u32[]{:S(2)}) async-start(bf16[8,8,320]{2,1,0:T(8,128)(2,1)} %get-tuple-element.20), calls=%async_computation.2 | async-start | bytes 98304 | tf_op jit(solution)/shard_map/all_to_all | solution.py:542
  69.9 16.9 %collective-permute-start.3 = (bf16[2,2,64,256]{3,2,1,0:T(8,128)(2,1)S(1)}, bf16[2,2,64,256]{3,2,1,0:T(8,128)(2,1)S(1)}, u32[]{:S(2)}, u32[]{:S(2)}) collective-permute-start(bf16[2,2,64,256]{3,2,1,0:T(8,128)(2,1)S(1)} %get-tuple-element.19), channel_id=1, source_target_pairs={{1,0},{2,1},{3,2},{4,3},{5,4},{6,5},{7,6},{0,7},{9,8},{10,9},{11,1... | collective-permute-start | bytes 393224 | tf_op jit(solution)/shard_map/ppermute | solution.py:541
  77.8 15.7 %all-to-all-start.3 = ((bf16[32,8,320]{2,1,0:T(8,128)(2,1)}), bf16[32,8,320]{2,1,0:T(8,128)(2,1)S(1)}, u32[]{:S(2)}, u32[]{:S(2)}) async-start(bf16[32,8,320]{2,1,0:T(8,128)(2,1)} %sum.1), calls=%async_computation.3 | async-start | bytes 393216 | tf_op jit(solution)/shard_map/all_to_all | solution.py:571

commit v7 on v6

--- a/solution.py
+++ b/solution.py
@@ -255,16 +255,12 @@
                 taps[rows, lanes * tap : lanes * tap + lanes] = jnp.concatenate(pair, axis=0).astype(BF)
         return _
 
-    lax.fori_loop(0, sources, gather, 0, unroll=2)
-
-    chunk = min(count, 256)
-
-    def convolve(part, _):
-        rows = pl.ds(pl.multiple_of(part * chunk, chunk), chunk)
+    chunk = min(count, 128)
+    for part in range(count // chunk):
+        for source in range(chunk // 16):
+            gather(part * (chunk // 16) + source, 0)
+        rows = slice(part * chunk, part * chunk + chunk)
         driven[rows, :] = jnp.dot(taps[rows, :], kernel[...], preferred_element_type=F32)
-        return _
-
-    lax.fori_loop(0, count // chunk, convolve, 0)
 
     tail = halo[6 * wide : 6 * wide + 8, :].astype(F32)
     tail = tail + pltpu.roll(tail, 6, 0) + pltpu.roll(tail, 4, 0)
@@ -294,7 +290,7 @@
         )
         return _
 
-    lax.fori_loop(0, count // 64, mix, 0, unroll=4)
+    lax.fori_loop(0, count // 64, mix, 0, unroll=8)
 
     def retreat(turn, carried):
         adjoint, later = carried
@@ -436,9 +432,12 @@
         out[target] = total
 
 
-def last_body(got, kernel_out, readout_out):
-    sources, share, width = got.shape
-    turned = got[...].astype(F32).reshape(sources * share, width).T
+def last_body(mine, theirs, kernel_out, readout_out):
+    chips, share, width = mine.shape
+    is_even = lax.axis_index("tm") % 2 == 0
+    here, there = mine[...].astype(F32), theirs[...].astype(F32)
+    pairs = [jnp.where(is_even, here, there), jnp.where(is_even, there, here)]
+    turned = jnp.stack(pairs, axis=1).reshape(2 * chips * share, width).T
     block = width // 10
     for k in range(9):
         kernel_out[k] = turned[block * k : block * k + block]
@@ -542,7 +541,7 @@
     partial = lax.all_to_all(partial, "row", 0, 0)
     scaling = 1.0 / math.sqrt(here * sources * band_rows * bands * wide)
     partial = call(
-        functools.partial(sum_body, scaling), "sum", shape((sources, share, 10 * block), BF), [VMEM], []
+        functools.partial(sum_body, scaling), "sum", shape((half, share, 10 * block), BF), [VMEM], []
     )(partial)
 
     def back(first, ins, **more):
@@ -568,10 +567,12 @@
     grad_frames = back(2, [VMEM] * 5 + [HBM], alias={5: 0})(
         drive, below, kernel, cotangent, through, grad_frames
     )
-    whole = lax.all_to_all(partial, "tm", 0, 0)
+    whole = lax.all_to_all(partial, "tm", 0, 0, axis_index_groups=groups)
+    whole, grad_frames = lax.optimization_barrier((whole, grad_frames))
+    other = lax.ppermute(whole, "tm", swap)
     grad_kernel, grad_readout = call(
-        last_body, "last", (shape((9, block, lanes), F32), shape((block, lanes), F32)), [VMEM], []
-    )(whole)
+        last_body, "last", (shape((9, block, lanes), F32), shape((block, lanes), F32)), [VMEM] * 2, []
+    )(whole, other)
     return grad_frames, grad_kernel, grad_readout.T
 
 

time: 94.8 us -> 94 us (level)
  blocking collectives: 37.9 us -> 48.9 us
  waiting for transfers between devices: 19.3 us -> 14 us
  starting transfers between devices: 20.7 us -> 15.8 us
  Pallas kernels: 13.1 us -> 11.5 us
    all_to_all x0 -> x1, blocking collectives: none -> 10.9 us  [local(): partial = lax.all_to_all(partial, 'row', 0, 0)]
    all_to_all x2 -> x1, starting transfers between devices: 12.5 us -> 4.23 us  [local(): whole = lax.all_to_all(partial, 'tm', 0, 0, axis_index_groups=groups)]
    all_to_all x2 -> x1, waiting for transfers between devices: 9.61 us -> 3.44 us  [local(): whole = lax.all_to_all(partial, 'tm', 0, 0, axis_index_groups=groups)]
    ppermute x0 -> x1, starting transfers between devices: none -> 4.65 us  [local(): other = lax.ppermute(whole, 'tm', swap)]
    ppermute x1, starting transfers between devices: 2.67 us -> 1.3 us  [local(): below = lax.ppermute(top, 'row', up)]
where the time goes in v7:
time: 94 us; the launch traced here: 93.6 us
  blocking collectives  48.9 us (52%)
  starting transfers between devices  15.8 us (17%)
  waiting for transfers between devices  14 us (15%)
  Pallas kernels  11.5 us (12%)
  local copies, waits for them, and re-layouts  2.61 us (3%)
    all_to_all x1, blocking collectives, local(): mine = lax.all_to_all(send, 'tm', 0, 0, axis_index_groups=groups)  20.5 us
    all_to_all x1, blocking collectives, local(): got = lax.all_to_all(send, 'tm', 0, 0, axis_index_groups=groups)  17.5 us
    all_to_all x1, blocking collectives, local(): partial = lax.all_to_all(partial, 'row', 0, 0)  10.9 us
    ppermute x1, waiting for transfers between devices, local(): edge = lax.ppermute(edge, 'row', down)  5.64 us
    ppermute x1, starting transfers between devices, local(): other = lax.ppermute(whole, 'tm', swap)  4.65 us
    all_to_all x1, starting transfers between devices, local(): whole = lax.all_to_all(partial, 'tm', 0, 0, axis_index_groups=groups)  4.23 us
    pallas_call x1, Pallas kernels, local(): call(cell_body, 'cells', (shape((half, share, 12 * lanes), BF), shape((ha...  3.72 us
    all_to_all x1, waiting for transfers between devices, local(): whole = lax.all_to_all(partial, 'tm', 0, 0, axis_index_groups=groups)  3.44 us
  transfers between devices with their start and end apart: 6, of which 5 were waited for; matrix products, arithmetic and copies ran while one was open for 0% of the time, Pallas kernels for 5%

profile of v7, /device:TPU:1, one launch (start us, length us, event | category | flops | bytes accessed | tf_op | source)
XLA Modules:
  0.0 93.6 jit_solution(14025479493919701344)
XLA Ops:
  0.6 1.7 %halo.1 = (bf16[392,256]{1,0:T(8,128)(2,1)}, f32[8,256]{1,0:T(8,128)}) custom-call(bf16[2,4,64,256]{3,2,1,0:T(8,128)(2,1)} %frames.3, bf16[2,4,64,256]{3,2,1,0:T(8,128)(2,1)} %refs_3_.1, f32[4,64,256]{2,1,0:T(8,128)} %start.1), custom_call_target="tpu_custom_call" | custom-call | flops 1048576 | bytes 1048576 | tf_op jit(solution)/shard_map/halo/pallas_call | solution.py:457
  2.3 2.5 %collective-permute-start = (bf16[392,256]{1,0:T(8,128)(2,1)}, bf16[392,256]{1,0:T(8,128)(2,1)S(1)}, u32[]{:S(2)}, u32[]{:S(2)}) collective-permute-start(bf16[392,256]{1,0:T(8,128)(2,1)} %get-tuple-element.15), channel_id=1, source_target_pairs={{0,1},{1,2},{2,3},{3,4},{4,5},{5,6},{6,7},{7,0},{8,9},{9,10},{10,1... | collective-permute-start | bytes 602120 | tf_op jit(solution)/shard_map/ppermute | solution.py:470
  4.8 0.9 %copy-done.1 = bf16[2,4,64,256]{3,2,1,0:T(8,128)(2,1)S(1)} copy-done((bf16[2,4,64,256]{3,2,1,0:T(8,128)(2,1)S(1)}, bf16[2,4,64,256]{3,2,1,0:T(8,128)(2,1)}, u32[]{:S(2)}) %copy-start.1) | copy-done | bytes 262168
  5.8 0.9 %copy-done.3 = bf16[2,4,64,256]{3,2,1,0:T(8,128)(2,1)S(1)} copy-done((bf16[2,4,64,256]{3,2,1,0:T(8,128)(2,1)S(1)}, bf16[2,4,64,256]{3,2,1,0:T(8,128)(2,1)}, u32[]{:S(2)}) %copy-start.3) | copy-done | bytes 262168
  6.8 0.7 copy-done.5
  7.4 0.6 own.1
  8.0 5.6 %collective-permute-done.halo = bf16[392,256]{1,0:T(8,128)(2,1)S(1)} collective-permute-done((bf16[392,256]{1,0:T(8,128)(2,1)}, bf16[392,256]{1,0:T(8,128)(2,1)S(1)}, u32[]{:S(2)}, u32[]{:S(2)}) %collective-permute-start) | collective-permute-done | bytes 200736 | tf_op jit(solution)/shard_map/ppermute | solution.py:470
  13.7 0.3 spread.1
  14.0 0.0 copy-start
  14.0 0.0 copy-start.6
  14.0 0.0 copy-start.7
  14.1 20.5 %all_to_all.20.mine = bf16[16,112,256]{2,1,0:T(8,128)(2,1)S(1)} all-to-all(bf16[16,112,256]{2,1,0:T(8,128)(2,1)S(1)} %spread.1), channel_id=1, replica_groups={{0,16,32,48,64,80,96,112,128,144,160,176,192,208,224,240},{8,24,40,56,7..., dimensions={0} | all-to-all | bytes 1835008 | tf_op jit(solution)/shard_map/all_to_all | solution.py:500
  34.5 2.6 %collective-permute-start.1 = (bf16[16,112,256]{2,1,0:T(8,128)(2,1)S(1)}, bf16[16,112,256]{2,1,0:T(8,128)(2,1)S(1)}, u32[]{:S(2)}, u32[]{:S(2)}) collective-permute-start(bf16[16,112,256]{2,1,0:T(8,128)(2,1)S(1)} %all_to_all.20.mine), channel_id=1, source_target_pairs={{0,8},{8,0},{16,24},{24,16},{32,40},{40,32},{48,56},{56,48},{64,72... | collective-permute-start | bytes 2752520 | tf_op jit(solution)/shard_map/ppermute | solution.py:501
  37.1 2.1 %collective-permute-done.1.theirs = bf16[16,112,256]{2,1,0:T(8,128)(2,1)S(1)} collective-permute-done((bf16[16,112,256]{2,1,0:T(8,128)(2,1)S(1)}, bf16[16,112,256]{2,1,0:T(8,128)(2,1)S(1)}, u32[]{:S(2)}, u32[]{:S(2)}) %collective-permute-start.1) | collective-permute-done | bytes 917536 | tf_op jit(solution)/shard_map/ppermute | solution.py:501
  39.2 3.7 %cells.1 = (bf16[16,8,3072]{2,1,0:T(8,128)(2,1)S(1)}, f32[16,8,2560]{2,1,0:T(8,128)S(1)}, bf16[16,8,512]{2,1,0:T(8,128)(2,1)S(1)}) custom-call(bf16[16,112,256]{2,1,0:T(8,128)(2,1)S(1)} %all_to_all.20.mine, bf16[16,112,256]{2,1,0:T(8,128)(2,1)S(1)} %collective-permute-done.1.theirs, bf16[2304,256]{1,0:T(8,128)(2,1)S(1)} %bitcast.3, ...), custom_call_target="tpu_custom_call" | custom-call | flops 1409286144 | bytes 4194304 | tf_op jit(solution)/shard_map/cells/pallas_call | solution.py:502
  43.0 0.5 collective-permute-start.2
  43.4 1.9 %collective-permute-done.2.taken = bf16[16,8,3072]{2,1,0:T(8,128)(2,1)S(1)} collective-permute-done((bf16[16,8,3072]{2,1,0:T(8,128)(2,1)S(1)}, bf16[16,8,3072]{2,1,0:T(8,128)(2,1)S(1)}, u32[]{:S(2)}, u32[]{:S(2)}) %collective-permute-start.2) | collective-permute-done | bytes 786464 | tf_op jit(solution)/shard_map/ppermute | solution.py:526
  45.4 0.2 merge.1
  45.5 0.0 copy-start.2
  45.5 0.0 copy-start.4
  45.6 17.5 %all_to_all.21.got = bf16[16,8,3584]{2,1,0:T(8,128)(2,1)S(1)} all-to-all(bf16[16,8,3584]{2,1,0:T(8,128)(2,1)S(1)} %merge.1), channel_id=1, replica_groups={{0,16,32,48,64,80,96,112,128,144,160,176,192,208,224,240},{8,24,40,56,7..., dimensions={0} | all-to-all | bytes 1835008 | tf_op jit(solution)/shard_map/all_to_all | solution.py:528
  63.0 0.4 join.1
  63.4 1.3 %collective-permute-start.3 = (bf16[2,2,64,256]{3,2,1,0:T(8,128)(2,1)S(1)}, bf16[2,2,64,256]{3,2,1,0:T(8,128)(2,1)S(1)}, u32[]{:S(2)}, u32[]{:S(2)}) collective-permute-start(bf16[2,2,64,256]{3,2,1,0:T(8,128)(2,1)S(1)} %get-tuple-element.22), channel_id=1, source_target_pairs={{1,0},{2,1},{3,2},{4,3},{5,4},{6,5},{7,6},{0,7},{9,8},{10,9},{11,1... | collective-permute-start | bytes 393224 | tf_op jit(solution)/shard_map/ppermute | solution.py:540
  64.7 10.9 %all_to_all.22.got = bf16[8,8,320]{2,1,0:T(8,128)(2,1)S(1)} all-to-all(bf16[8,8,320]{2,1,0:T(8,128)(2,1)S(1)} %get-tuple-element.20), channel_id=1, replica_groups=mesh['tm'=32,'row'=8] {'row'}, dimensions={0} | all-to-all | bytes 81920 | tf_op jit(solution)/shard_map/all_to_all | solution.py:541
  75.6 0.7 sum.1
  76.3 4.2 %all-to-all-start.3 = ((bf16[16,8,320]{2,1,0:T(8,128)(2,1)}), bf16[16,8,320]{2,1,0:T(8,128)(2,1)S(1)}, u32[]{:S(2)}, u32[]{:S(2)}) async-start(bf16[16,8,320]{2,1,0:T(8,128)(2,1)} %sum.1), calls=%async_computation.3 | async-start | bytes 196608 | tf_op jit(solution)/shard_map/all_to_all | solution.py:570
  80.5 1.6 %back.2.refs_5_ = bf16[2,4,64,256]{3,2,1,0:T(8,128)(2,1)} custom-call(bf16[2,4,64,256]{3,2,1,0:T(8,128)(2,1)S(1)} %get-tuple-element.21.refs_0_, bf16[9,256,256]{2,1,0:T(8,128)(2,1)S(1)} %copy-done, bf16[2,4,64,256]{3,2,1,0:T(8,128)(2,1)S(1)} %copy-done.2, f32[1,256]{1,0:T(1,128)S(1)} %bitcast.4), custom_call_target="tpu_custom_call" | custom-call | flops 301989888 | bytes 2097152 | tf_op jit(solution)/shard_map/back/pallas_call | solution.py:566
  82.1 1.6 %back.3 = bf16[2,4,64,256]{3,2,1,0:T(8,128)(2,1)} custom-call(bf16[2,4,64,256]{3,2,1,0:T(8,128)(2,1)S(1)} %get-tuple-element.21.refs_0_, bf16[2,2,64,256]{3,2,1,0:T(8,128)(2,1)S(1)} %collective-permute-done.3.refs_1_, bf16[9,256,256]{2,1,0:T(8,128)(2,1)S(1)} %copy-done, bf16[2,4,64,256]{3,2,1,0:T(8,128)(2,1)S(1)} %copy-done.2, ...), custom_call_target="tpu_custom_call", output_to_operand_aliasing={{}: (5, {})} | custom-call | flops 301989888 | bytes 2097152 | tf_op jit(solution)/shard_map/back/pallas_call | solution.py:567
  83.7 3.4 %all-to-all-done.3.mine = bf16[16,8,320]{2,1,0:T(8,128)(2,1)S(1)} async-done(((bf16[16,8,320]{2,1,0:T(8,128)(2,1)}), bf16[16,8,320]{2,1,0:T(8,128)(2,1)S(1)}, u32[]{:S(2)}, u32[]{:S(2)}) %all-to-all-start.3) | async-done | bytes 81952 | tf_op jit(solution)/shard_map/all_to_all | solution.py:570
  87.1 4.7 %collective-permute-start.4 = (bf16[16,8,320]{2,1,0:T(8,128)(2,1)S(1)}, bf16[16,8,320]{2,1,0:T(8,128)(2,1)S(1)}, u32[]{:S(2)}, u32[]{:S(2)}) collective-permute-start(bf16[16,8,320]{2,1,0:T(8,128)(2,1)S(1)} %all-to-all-done.3.mine), channel_id=1, source_target_pairs={{0,8},{8,0},{16,24},{24,16},{32,40},{40,32},{48,56},{56,48},{64,72... | collective-permute-start | bytes 245768 | tf_op jit(solution)/shard_map/ppermute | solution.py:572
  91.8 0.9 %collective-permute-done.4.theirs = bf16[16,8,320]{2,1,0:T(8,128)(2,1)S(1)} collective-permute-done((bf16[16,8,320]{2,1,0:T(8,128)(2,1)S(1)}, bf16[16,8,320]{2,1,0:T(8,128)(2,1)S(1)}, u32[]{:S(2)}, u32[]{:S(2)}) %collective-permute-start.4) | collective-permute-done | bytes 81952 | tf_op jit(solution)/shard_map/ppermute | solution.py:572
  92.7 0.9 last.1
  (9 shorter events, 0.0 us)
Async XLA Ops:
  2.3 11.4 %collective-permute-start = (bf16[392,256]{1,0:T(8,128)(2,1)}, bf16[392,256]{1,0:T(8,128)(2,1)S(1)}, u32[]{:S(2)}, u32[]{:S(2)}) collective-permute-start(bf16[392,256]{1,0:T(8,128)(2,1)} %get-tuple-element.15), channel_id=1, source_target_pairs={{0,1},{1,2},{2,3},{3,4},{4,5},{5,6},{6,7},{7,0},{8,9},{9,10},{10,1... | collective-permute-start | bytes 602120 | tf_op jit(solution)/shard_map/ppermute | solution.py:470
  4.8 0.9 %copy-start.1 = (bf16[2,4,64,256]{3,2,1,0:T(8,128)(2,1)S(1)}, bf16[2,4,64,256]{3,2,1,0:T(8,128)(2,1)}, u32[]{:S(2)}) copy-start(bf16[2,4,64,256]{3,2,1,0:T(8,128)(2,1)} %refs_3_.1) | copy-start | bytes 786436
  5.8 0.9 %copy-start.3 = (bf16[2,4,64,256]{3,2,1,0:T(8,128)(2,1)S(1)}, bf16[2,4,64,256]{3,2,1,0:T(8,128)(2,1)}, u32[]{:S(2)}) copy-start(bf16[2,4,64,256]{3,2,1,0:T(8,128)(2,1)} %frames.3) | copy-start | bytes 786436
  6.7 0.7 copy-start.5
  14.0 25.2 %copy-start = (bf16[9,256,256]{2,1,0:T(8,128)(2,1)S(1)}, bf16[9,256,256]{2,1,0:T(8,128)(2,1)}, u32[]{:S(2)}) copy-start(bf16[9,256,256]{2,1,0:T(8,128)(2,1)} %refs_2_.3) | copy-start | bytes 3538948
  14.0 25.2 %copy-start.6 = (bf16[256,256]{1,0:T(8,128)(2,1)S(1)}, bf16[256,256]{1,0:T(8,128)(2,1)}, u32[]{:S(2)}) copy-start(bf16[256,256]{1,0:T(8,128)(2,1)} %readout.1) | copy-start | bytes 393220
  14.0 25.2 %copy-start.7 = (f32[8,256]{1,0:T(8,128)S(1)}, f32[8,256]{1,0:T(8,128)}, u32[]{:S(2)}) copy-start(f32[8,256]{1,0:T(8,128)} %get-tuple-element.16.start) | copy-start | bytes 24580
  34.5 4.7 %collective-permute-start.1 = (bf16[16,112,256]{2,1,0:T(8,128)(2,1)S(1)}, bf16[16,112,256]{2,1,0:T(8,128)(2,1)S(1)}, u32[]{:S(2)}, u32[]{:S(2)}) collective-permute-start(bf16[16,112,256]{2,1,0:T(8,128)(2,1)S(1)} %all_to_all.20.mine), channel_id=1, source_target_pairs={{0,8},{8,0},{16,24},{24,16},{32,40},{40,32},{48,56},{56,48},{64,72... | collective-permute-start | bytes 2752520 | tf_op jit(solution)/shard_map/ppermute | solution.py:501
  43.0 2.4 %collective-permute-start.2 = (bf16[16,8,3072]{2,1,0:T(8,128)(2,1)S(1)}, bf16[16,8,3072]{2,1,0:T(8,128)(2,1)S(1)}, u32[]{:S(2)}, u32[]{:S(2)}) collective-permute-start(bf16[16,8,3072]{2,1,0:T(8,128)(2,1)S(1)} %get-tuple-element.17), channel_id=1, source_target_pairs={{0,8},{8,0},{16,24},{24,16},{32,40},{40,32},{48,56},{56,48},{64,72... | collective-permute-start | bytes 2359304 | tf_op jit(solution)/shard_map/ppermute | solution.py:526
  45.5 35.0 %copy-start.2 = (bf16[2,4,64,256]{3,2,1,0:T(8,128)(2,1)S(1)}, bf16[2,4,64,256]{3,2,1,0:T(8,128)(2,1)}, u32[]{:S(2)}) copy-start(bf16[2,4,64,256]{3,2,1,0:T(8,128)(2,1)} %refs_3_.1) | copy-start | bytes 786436
  45.5 35.0 %copy-start.4 = (f32[256]{0:T(256)S(1)}, f32[256]{0:T(256)}, u32[]{:S(2)}) copy-start(f32[256]{0:T(256)} %param.11) | copy-start | bytes 3076
  63.4 18.7 %collective-permute-start.3 = (bf16[2,2,64,256]{3,2,1,0:T(8,128)(2,1)S(1)}, bf16[2,2,64,256]{3,2,1,0:T(8,128)(2,1)S(1)}, u32[]{:S(2)}, u32[]{:S(2)}) collective-permute-start(bf16[2,2,64,256]{3,2,1,0:T(8,128)(2,1)S(1)} %get-tuple-element.22), channel_id=1, source_target_pairs={{1,0},{2,1},{3,2},{4,3},{5,4},{6,5},{7,6},{0,7},{9,8},{10,9},{11,1... | collective-permute-start | bytes 393224 | tf_op jit(solution)/shard_map/ppermute | solution.py:540
  76.3 10.8 %all-to-all-start.3 = ((bf16[16,8,320]{2,1,0:T(8,128)(2,1)}), bf16[16,8,320]{2,1,0:T(8,128)(2,1)S(1)}, u32[]{:S(2)}, u32[]{:S(2)}) async-start(bf16[16,8,320]{2,1,0:T(8,128)(2,1)} %sum.1), calls=%async_computation.3 | async-start | bytes 196608 | tf_op jit(solution)/shard_map/all_to_all | solution.py:570
  87.1 5.6 %collective-permute-start.4 = (bf16[16,8,320]{2,1,0:T(8,128)(2,1)S(1)}, bf16[16,8,320]{2,1,0:T(8,128)(2,1)S(1)}, u32[]{:S(2)}, u32[]{:S(2)}) collective-permute-start(bf16[16,8,320]{2,1,0:T(8,128)(2,1)S(1)} %all-to-all-done.3.mine), channel_id=1, source_target_pairs={{0,8},{8,0},{16,24},{24,16},{32,40},{40,32},{48,56},{56,48},{64,72... | collective-permute-start | bytes 245768 | tf_op jit(solution)/shard_map/ppermute | solution.py:572

commit v8 on v7

--- a/solution.py
+++ b/solution.py
@@ -18,11 +18,10 @@
 HBM = pl.BlockSpec(memory_space=pltpu.MemorySpace.HBM)
 
 
-def call(body, name, outs, ins, scratch, flops=1 << 20, moved=1 << 20, grant=40 << 20, to=None, alias=None):
+def call(body, outs, ins, scratch, flops=1 << 20, moved=1 << 20, grant=40 << 20, to=None, alias=None):
     many = isinstance(outs, (list, tuple))
     return pl.pallas_call(
         body,
-        name=name,
         out_shape=outs,
         in_specs=ins,
         out_specs=[VMEM] * len(outs) if many else (to or VMEM),
@@ -432,12 +431,9 @@
         out[target] = total
 
 
-def last_body(mine, theirs, kernel_out, readout_out):
-    chips, share, width = mine.shape
-    is_even = lax.axis_index("tm") % 2 == 0
-    here, there = mine[...].astype(F32), theirs[...].astype(F32)
-    pairs = [jnp.where(is_even, here, there), jnp.where(is_even, there, here)]
-    turned = jnp.stack(pairs, axis=1).reshape(2 * chips * share, width).T
+def last_body(got, kernel_out, readout_out):
+    sources, share, width = got.shape
+    turned = got[...].astype(F32).reshape(sources * share, width).T
     block = width // 10
     for k in range(9):
         kernel_out[k] = turned[block * k : block * k + block]
@@ -456,7 +452,6 @@
 
     edge, begin = call(
         halo_body,
-        "halo",
         (shape((6 * wide + 8, lanes), BF), shape((8, lanes), F32)),
         [HBM] * 3,
         [
@@ -473,7 +468,6 @@
     swap = [(i, i ^ 1) for i in range(sources)]
     own = call(
         own_body,
-        "own",
         shape((half, 112, lanes), BF),
         [HBM] * 3,
         [
@@ -489,7 +483,6 @@
     )(frames_in, cotangent, decay_rate)
     send = call(
         spread_body,
-        "spread",
         shape((half, 112, lanes), BF),
         [VMEM] * 2,
         [
@@ -501,7 +494,6 @@
     theirs = lax.ppermute(mine, "tm", swap)
     give, keep, stay = call(
         cell_body,
-        "cells",
         (
             shape((half, share, 12 * lanes), BF),
             shape((half, share, 10 * lanes), F32),
@@ -524,11 +516,10 @@
         moved=4 << 20,
     )(mine, theirs, kernel.reshape(9 * lanes, lanes), readout, begin, edge)
     taken = lax.ppermute(give, "tm", swap)
-    send = call(merge_body, "merge", shape((half, share, 14 * lanes), BF), [VMEM] * 3, [])(taken, keep, stay)
+    send = call(merge_body, shape((half, share, 14 * lanes), BF), [VMEM] * 3, [])(taken, keep, stay)
     got = lax.all_to_all(send, "tm", 0, 0, axis_index_groups=groups)
     partial, drive, top = call(
         functools.partial(join_body, bands),
-        "join",
         (
             shape((bands, share, 10 * block), BF),
             shape((2, 4, wide, lanes), BF),
@@ -540,14 +531,11 @@
     below = lax.ppermute(top, "row", up)
     partial = lax.all_to_all(partial, "row", 0, 0)
     scaling = 1.0 / math.sqrt(here * sources * band_rows * bands * wide)
-    partial = call(
-        functools.partial(sum_body, scaling), "sum", shape((half, share, 10 * block), BF), [VMEM], []
-    )(partial)
+    partial = call(functools.partial(sum_body, scaling), shape((sources, share, 10 * block), BF), [VMEM], [])(partial)
 
     def back(first, ins, **more):
         return call(
             functools.partial(back_body, first, bands),
-            "back",
             shape(frames_in.shape, BF),
             ins,
             [
@@ -567,12 +555,11 @@
     grad_frames = back(2, [VMEM] * 5 + [HBM], alias={5: 0})(
         drive, below, kernel, cotangent, through, grad_frames
     )
-    whole = lax.all_to_all(partial, "tm", 0, 0, axis_index_groups=groups)
+    whole = lax.all_to_all(partial, "tm", 0, 0)
     whole, grad_frames = lax.optimization_barrier((whole, grad_frames))
-    other = lax.ppermute(whole, "tm", swap)
     grad_kernel, grad_readout = call(
-        last_body, "last", (shape((9, block, lanes), F32), shape((block, lanes), F32)), [VMEM] * 2, []
-    )(whole, other)
+        last_body, (shape((9, block, lanes), F32), shape((block, lanes), F32)), [VMEM], []
+    )(whole)
     return grad_frames, grad_kernel, grad_readout.T
 
 
@@ -586,6 +573,7 @@
         P("tm", None),
         P("row", None, None),
     )
+
     return jax.shard_map(
         local,
         mesh=mesh,

time: 94 us -> 93.9 us (level)
  blocking collectives: 48.9 us -> 37.9 us
  waiting for transfers between devices: 14 us -> 19.3 us
  starting transfers between devices: 15.8 us -> 20.7 us
    all_to_all x1 -> x0, blocking collectives: 10.9 us -> none  [local(): partial = lax.all_to_all(partial, 'row', 0, 0)]
    all_to_all x1 -> x2, starting transfers between devices: 4.23 us -> 12.5 us  [the longest x1 7.42 us: local(): whole = lax.all_to_all(partial, 'tm', 0, 0)]
    all_to_all x1 -> x2, waiting for transfers between devices: 3.44 us -> 9.61 us  [the longest x1 5.15 us: local(): whole = lax.all_to_all(partial, 'tm', 0, 0)]
    ppermute x1 -> x0, starting transfers between devices: 4.65 us -> none  [local(): other = lax.ppermute(whole, 'tm', swap)]
    ppermute x1, starting transfers between devices: 1.3 us -> 2.67 us  [local(): below = lax.ppermute(top, 'row', up)]
    ppermute x1 -> x0, waiting for transfers between devices: 0.94 us -> none  [local(): other = lax.ppermute(whole, 'tm', swap)]
where the time goes in v8:
time: 93.9 us; the launch traced here: 93.5 us
  blocking collectives  37.9 us (40%)
  starting transfers between devices  20.7 us (22%)
  waiting for transfers between devices  19.3 us (21%)
  Pallas kernels  12.1 us (13%)
  local copies, waits for them, and re-layouts  2.61 us (3%)
    all_to_all x1, blocking collectives, local(): mine = lax.all_to_all(send, 'tm', 0, 0, axis_index_groups=groups)  20.5 us
    all_to_all x1, blocking collectives, local(): got = lax.all_to_all(send, 'tm', 0, 0, axis_index_groups=groups)  17.5 us
    all_to_all x1, starting transfers between devices, local(): whole = lax.all_to_all(partial, 'tm', 0, 0)  7.42 us
    ppermute x1, waiting for transfers between devices, local(): edge = lax.ppermute(edge, 'row', down)  5.64 us
    all_to_all x1, waiting for transfers between devices, local(): whole = lax.all_to_all(partial, 'tm', 0, 0)  5.15 us
    all_to_all x1, starting transfers between devices, local(): partial = lax.all_to_all(partial, 'row', 0, 0)  5.05 us
    all_to_all x1, waiting for transfers between devices, local(): partial = lax.all_to_all(partial, 'row', 0, 0)  4.46 us
    pallas_call x1, Pallas kernels, local(): call(cell_body, (shape((half, share, 12 * lanes), BF), shape((half, share...  3.72 us
  transfers between devices with their start and end apart: 6, of which 5 were waited for; matrix products, arithmetic and copies ran while one was open for 0% of the time, Pallas kernels for 5%

profile of v8, /device:TPU:1, one launch (start us, length us, event | category | flops | bytes accessed | tf_op | source)
XLA Modules:
  0.0 93.5 jit_solution(9603041957062091606)
XLA Ops:
  0.6 1.7 %shard_map.95 = (bf16[392,256]{1,0:T(8,128)(2,1)}, f32[8,256]{1,0:T(8,128)}) custom-call(bf16[2,4,64,256]{3,2,1,0:T(8,128)(2,1)} %frames.3, bf16[2,4,64,256]{3,2,1,0:T(8,128)(2,1)} %refs_3_.1, f32[4,64,256]{2,1,0:T(8,128)} %start.1), custom_call_target="tpu_custom_call" | custom-call | flops 1048576 | bytes 1048576 | tf_op jit(solution)/shard_map/pallas_call | solution.py:453
  2.3 2.5 %collective-permute-start = (bf16[392,256]{1,0:T(8,128)(2,1)}, bf16[392,256]{1,0:T(8,128)(2,1)S(1)}, u32[]{:S(2)}, u32[]{:S(2)}) collective-permute-start(bf16[392,256]{1,0:T(8,128)(2,1)} %get-tuple-element.15), channel_id=1, source_target_pairs={{0,1},{1,2},{2,3},{3,4},{4,5},{5,6},{6,7},{7,0},{8,9},{9,10},{10,1... | collective-permute-start | bytes 602120 | tf_op jit(solution)/shard_map/ppermute | solution.py:465
  4.8 0.9 %copy-done.1 = bf16[2,4,64,256]{3,2,1,0:T(8,128)(2,1)S(1)} copy-done((bf16[2,4,64,256]{3,2,1,0:T(8,128)(2,1)S(1)}, bf16[2,4,64,256]{3,2,1,0:T(8,128)(2,1)}, u32[]{:S(2)}) %copy-start.1) | copy-done | bytes 262168
  5.8 0.9 %copy-done.3 = bf16[2,4,64,256]{3,2,1,0:T(8,128)(2,1)S(1)} copy-done((bf16[2,4,64,256]{3,2,1,0:T(8,128)(2,1)S(1)}, bf16[2,4,64,256]{3,2,1,0:T(8,128)(2,1)}, u32[]{:S(2)}) %copy-start.3) | copy-done | bytes 262168
  6.8 0.7 copy-done.5
  7.4 0.6 shard_map.94.own
  8.0 5.6 %collective-permute-done.halo = bf16[392,256]{1,0:T(8,128)(2,1)S(1)} collective-permute-done((bf16[392,256]{1,0:T(8,128)(2,1)}, bf16[392,256]{1,0:T(8,128)(2,1)S(1)}, u32[]{:S(2)}, u32[]{:S(2)}) %collective-permute-start) | collective-permute-done | bytes 200736 | tf_op jit(solution)/shard_map/ppermute | solution.py:465
  13.7 0.3 shard_map.96
  14.0 0.0 copy-start
  14.0 0.0 copy-start.6
  14.0 0.0 copy-start.7
  14.1 20.5 %all_to_all.20.mine = bf16[16,112,256]{2,1,0:T(8,128)(2,1)S(1)} all-to-all(bf16[16,112,256]{2,1,0:T(8,128)(2,1)S(1)} %shard_map.96), channel_id=1, replica_groups={{0,16,32,48,64,80,96,112,128,144,160,176,192,208,224,240},{8,24,40,56,7..., dimensions={0} | all-to-all | bytes 1835008 | tf_op jit(solution)/shard_map/all_to_all | solution.py:493
  34.5 2.6 %collective-permute-start.1 = (bf16[16,112,256]{2,1,0:T(8,128)(2,1)S(1)}, bf16[16,112,256]{2,1,0:T(8,128)(2,1)S(1)}, u32[]{:S(2)}, u32[]{:S(2)}) collective-permute-start(bf16[16,112,256]{2,1,0:T(8,128)(2,1)S(1)} %all_to_all.20.mine), channel_id=1, source_target_pairs={{0,8},{8,0},{16,24},{24,16},{32,40},{40,32},{48,56},{56,48},{64,72... | collective-permute-start | bytes 2752520 | tf_op jit(solution)/shard_map/ppermute | solution.py:494
  37.1 2.1 %collective-permute-done.1.theirs = bf16[16,112,256]{2,1,0:T(8,128)(2,1)S(1)} collective-permute-done((bf16[16,112,256]{2,1,0:T(8,128)(2,1)S(1)}, bf16[16,112,256]{2,1,0:T(8,128)(2,1)S(1)}, u32[]{:S(2)}, u32[]{:S(2)}) %collective-permute-start.1) | collective-permute-done | bytes 917536 | tf_op jit(solution)/shard_map/ppermute | solution.py:494
  39.2 3.7 %shard_map.97 = (bf16[16,8,3072]{2,1,0:T(8,128)(2,1)S(1)}, f32[16,8,2560]{2,1,0:T(8,128)S(1)}, bf16[16,8,512]{2,1,0:T(8,128)(2,1)S(1)}) custom-call(bf16[16,112,256]{2,1,0:T(8,128)(2,1)S(1)} %all_to_all.20.mine, bf16[16,112,256]{2,1,0:T(8,128)(2,1)S(1)} %collective-permute-done.1.theirs, bf16[2304,256]{1,0:T(8,128)(2,1)S(1)} %bitcast.3, ...), custom_call_target="tpu_custom_call" | custom-call | flops 1409286144 | bytes 4194304 | tf_op jit(solution)/shard_map/pallas_call | solution.py:495
  43.0 0.5 collective-permute-start.2
  43.4 1.9 %collective-permute-done.2.taken = bf16[16,8,3072]{2,1,0:T(8,128)(2,1)S(1)} collective-permute-done((bf16[16,8,3072]{2,1,0:T(8,128)(2,1)S(1)}, bf16[16,8,3072]{2,1,0:T(8,128)(2,1)S(1)}, u32[]{:S(2)}, u32[]{:S(2)}) %collective-permute-start.2) | collective-permute-done | bytes 786464 | tf_op jit(solution)/shard_map/ppermute | solution.py:518
  45.4 0.2 shard_map.98
  45.5 0.0 copy-start.2
  45.5 0.0 copy-start.4
  45.6 17.5 %all_to_all.21.got = bf16[16,8,3584]{2,1,0:T(8,128)(2,1)S(1)} all-to-all(bf16[16,8,3584]{2,1,0:T(8,128)(2,1)S(1)} %shard_map.98), channel_id=1, replica_groups={{0,16,32,48,64,80,96,112,128,144,160,176,192,208,224,240},{8,24,40,56,7..., dimensions={0} | all-to-all | bytes 1835008 | tf_op jit(solution)/shard_map/all_to_all | solution.py:520
  63.0 1.0 %shard_map.99 = (bf16[8,8,320]{2,1,0:T(8,128)(2,1)}, bf16[2,4,64,256]{3,2,1,0:T(8,128)(2,1)S(1)}, bf16[2,2,64,256]{3,2,1,0:T(8,128)(2,1)S(1)}) custom-call(bf16[16,8,3584]{2,1,0:T(8,128)(2,1)S(1)} %all_to_all.21.got), custom_call_target="tpu_custom_call" | custom-call | flops 1048576 | bytes 1048576 | tf_op jit(solution)/shard_map/pallas_call | solution.py:521
  64.0 5.0 %all-to-all-start.2 = ((bf16[8,8,320]{2,1,0:T(8,128)(2,1)}), bf16[8,8,320]{2,1,0:T(8,128)(2,1)S(1)}, u32[]{:S(2)}, u32[]{:S(2)}) async-start(bf16[8,8,320]{2,1,0:T(8,128)(2,1)} %get-tuple-element.20), calls=%async_computation.2 | async-start | bytes 98304 | tf_op jit(solution)/shard_map/all_to_all | solution.py:532
  69.0 2.7 %collective-permute-start.3 = (bf16[2,2,64,256]{3,2,1,0:T(8,128)(2,1)S(1)}, bf16[2,2,64,256]{3,2,1,0:T(8,128)(2,1)S(1)}, u32[]{:S(2)}, u32[]{:S(2)}) collective-permute-start(bf16[2,2,64,256]{3,2,1,0:T(8,128)(2,1)S(1)} %get-tuple-element.22), channel_id=1, source_target_pairs={{1,0},{2,1},{3,2},{4,3},{5,4},{6,5},{7,6},{0,7},{9,8},{10,9},{11,1... | collective-permute-start | bytes 393224 | tf_op jit(solution)/shard_map/ppermute | solution.py:531
  71.7 4.5 %all-to-all-done.2.got = bf16[8,8,320]{2,1,0:T(8,128)(2,1)S(1)} async-done(((bf16[8,8,320]{2,1,0:T(8,128)(2,1)}), bf16[8,8,320]{2,1,0:T(8,128)(2,1)S(1)}, u32[]{:S(2)}, u32[]{:S(2)}) %all-to-all-start.2) | async-done | bytes 40992 | tf_op jit(solution)/shard_map/all_to_all | solution.py:532
  76.2 0.7 shard_map.100
  76.9 7.4 %all-to-all-start.3 = ((bf16[32,8,320]{2,1,0:T(8,128)(2,1)}), bf16[32,8,320]{2,1,0:T(8,128)(2,1)S(1)}, u32[]{:S(2)}, u32[]{:S(2)}) async-start(bf16[32,8,320]{2,1,0:T(8,128)(2,1)} %shard_map.100), calls=%async_computation.3 | async-start | bytes 393216 | tf_op jit(solution)/shard_map/all_to_all | solution.py:558
  84.3 1.6 %shard_map.101.refs_5_ = bf16[2,4,64,256]{3,2,1,0:T(8,128)(2,1)} custom-call(bf16[2,4,64,256]{3,2,1,0:T(8,128)(2,1)S(1)} %get-tuple-element.21.refs_0_, bf16[9,256,256]{2,1,0:T(8,128)(2,1)S(1)} %copy-done, bf16[2,4,64,256]{3,2,1,0:T(8,128)(2,1)S(1)} %copy-done.2, f32[1,256]{1,0:T(1,128)S(1)} %bitcast.4), custom_call_target="tpu_custom_call" | custom-call | flops 301989888 | bytes 2097152 | tf_op jit(solution)/shard_map/pallas_call | solution.py:554
  85.9 0.0 collective-permute-done.3.refs_1_
  85.9 1.6 %shard_map.102 = bf16[2,4,64,256]{3,2,1,0:T(8,128)(2,1)} custom-call(bf16[2,4,64,256]{3,2,1,0:T(8,128)(2,1)S(1)} %get-tuple-element.21.refs_0_, bf16[2,2,64,256]{3,2,1,0:T(8,128)(2,1)S(1)} %collective-permute-done.3.refs_1_, bf16[9,256,256]{2,1,0:T(8,128)(2,1)S(1)} %copy-done, bf16[2,4,64,256]{3,2,1,0:T(8,128)(2,1)S(1)} %copy-done.2, ...), custom_call_target="tpu_custom_call", output_to_operand_aliasing={{}: (5, {})} | custom-call | flops 301989888 | bytes 2097152 | tf_op jit(solution)/shard_map/pallas_call | solution.py:555
  87.5 5.1 %all-to-all-done.3.got = bf16[32,8,320]{2,1,0:T(8,128)(2,1)S(1)} async-done(((bf16[32,8,320]{2,1,0:T(8,128)(2,1)}), bf16[32,8,320]{2,1,0:T(8,128)(2,1)S(1)}, u32[]{:S(2)}, u32[]{:S(2)}) %all-to-all-start.3) | async-done | bytes 163872 | tf_op jit(solution)/shard_map/all_to_all | solution.py:558
  92.6 0.9 shard_map.103
  (8 shorter events, 0.0 us)
Async XLA Ops:
  2.3 11.4 %collective-permute-start = (bf16[392,256]{1,0:T(8,128)(2,1)}, bf16[392,256]{1,0:T(8,128)(2,1)S(1)}, u32[]{:S(2)}, u32[]{:S(2)}) collective-permute-start(bf16[392,256]{1,0:T(8,128)(2,1)} %get-tuple-element.15), channel_id=1, source_target_pairs={{0,1},{1,2},{2,3},{3,4},{4,5},{5,6},{6,7},{7,0},{8,9},{9,10},{10,1... | collective-permute-start | bytes 602120 | tf_op jit(solution)/shard_map/ppermute | solution.py:465
  4.8 0.9 %copy-start.1 = (bf16[2,4,64,256]{3,2,1,0:T(8,128)(2,1)S(1)}, bf16[2,4,64,256]{3,2,1,0:T(8,128)(2,1)}, u32[]{:S(2)}) copy-start(bf16[2,4,64,256]{3,2,1,0:T(8,128)(2,1)} %refs_3_.1) | copy-start | bytes 786436
  5.8 0.9 %copy-start.3 = (bf16[2,4,64,256]{3,2,1,0:T(8,128)(2,1)S(1)}, bf16[2,4,64,256]{3,2,1,0:T(8,128)(2,1)}, u32[]{:S(2)}) copy-start(bf16[2,4,64,256]{3,2,1,0:T(8,128)(2,1)} %frames.3) | copy-start | bytes 786436
  6.7 0.7 copy-start.5
  14.0 25.2 %copy-start = (bf16[9,256,256]{2,1,0:T(8,128)(2,1)S(1)}, bf16[9,256,256]{2,1,0:T(8,128)(2,1)}, u32[]{:S(2)}) copy-start(bf16[9,256,256]{2,1,0:T(8,128)(2,1)} %refs_2_.3) | copy-start | bytes 3538948
  14.0 25.2 %copy-start.6 = (bf16[256,256]{1,0:T(8,128)(2,1)S(1)}, bf16[256,256]{1,0:T(8,128)(2,1)}, u32[]{:S(2)}) copy-start(bf16[256,256]{1,0:T(8,128)(2,1)} %readout.1) | copy-start | bytes 393220
  14.0 25.2 %copy-start.7 = (f32[8,256]{1,0:T(8,128)S(1)}, f32[8,256]{1,0:T(8,128)}, u32[]{:S(2)}) copy-start(f32[8,256]{1,0:T(8,128)} %get-tuple-element.16.start) | copy-start | bytes 24580
  34.5 4.7 %collective-permute-start.1 = (bf16[16,112,256]{2,1,0:T(8,128)(2,1)S(1)}, bf16[16,112,256]{2,1,0:T(8,128)(2,1)S(1)}, u32[]{:S(2)}, u32[]{:S(2)}) collective-permute-start(bf16[16,112,256]{2,1,0:T(8,128)(2,1)S(1)} %all_to_all.20.mine), channel_id=1, source_target_pairs={{0,8},{8,0},{16,24},{24,16},{32,40},{40,32},{48,56},{56,48},{64,72... | collective-permute-start | bytes 2752520 | tf_op jit(solution)/shard_map/ppermute | solution.py:494
  43.0 2.4 %collective-permute-start.2 = (bf16[16,8,3072]{2,1,0:T(8,128)(2,1)S(1)}, bf16[16,8,3072]{2,1,0:T(8,128)(2,1)S(1)}, u32[]{:S(2)}, u32[]{:S(2)}) collective-permute-start(bf16[16,8,3072]{2,1,0:T(8,128)(2,1)S(1)} %get-tuple-element.17), channel_id=1, source_target_pairs={{0,8},{8,0},{16,24},{24,16},{32,40},{40,32},{48,56},{56,48},{64,72... | collective-permute-start | bytes 2359304 | tf_op jit(solution)/shard_map/ppermute | solution.py:518
  45.5 38.8 %copy-start.2 = (bf16[2,4,64,256]{3,2,1,0:T(8,128)(2,1)S(1)}, bf16[2,4,64,256]{3,2,1,0:T(8,128)(2,1)}, u32[]{:S(2)}) copy-start(bf16[2,4,64,256]{3,2,1,0:T(8,128)(2,1)} %refs_3_.1) | copy-start | bytes 786436
  45.5 38.8 %copy-start.4 = (f32[256]{0:T(256)S(1)}, f32[256]{0:T(256)}, u32[]{:S(2)}) copy-start(f32[256]{0:T(256)} %param.11) | copy-start | bytes 3076
  64.0 12.2 %all-to-all-start.2 = ((bf16[8,8,320]{2,1,0:T(8,128)(2,1)}), bf16[8,8,320]{2,1,0:T(8,128)(2,1)S(1)}, u32[]{:S(2)}, u32[]{:S(2)}) async-start(bf16[8,8,320]{2,1,0:T(8,128)(2,1)} %get-tuple-element.20), calls=%async_computation.2 | async-start | bytes 98304 | tf_op jit(solution)/shard_map/all_to_all | solution.py:532
  69.0 16.9 %collective-permute-start.3 = (bf16[2,2,64,256]{3,2,1,0:T(8,128)(2,1)S(1)}, bf16[2,2,64,256]{3,2,1,0:T(8,128)(2,1)S(1)}, u32[]{:S(2)}, u32[]{:S(2)}) collective-permute-start(bf16[2,2,64,256]{3,2,1,0:T(8,128)(2,1)S(1)} %get-tuple-element.22), channel_id=1, source_target_pairs={{1,0},{2,1},{3,2},{4,3},{5,4},{6,5},{7,6},{0,7},{9,8},{10,9},{11,1... | collective-permute-start | bytes 393224 | tf_op jit(solution)/shard_map/ppermute | solution.py:531
  76.9 15.7 %all-to-all-start.3 = ((bf16[32,8,320]{2,1,0:T(8,128)(2,1)}), bf16[32,8,320]{2,1,0:T(8,128)(2,1)S(1)}, u32[]{:S(2)}, u32[]{:S(2)}) async-start(bf16[32,8,320]{2,1,0:T(8,128)(2,1)} %shard_map.100), calls=%async_computation.3 | async-start | bytes 393216 | tf_op jit(solution)/shard_map/all_to_all | solution.py:558

commit v9 on v7

--- a/solution.py
+++ b/solution.py
@@ -228,7 +228,7 @@
             gain[source] = jnp.sqrt(1.0 - rate * rate)
         return _
 
-    lax.fori_loop(0, sources // 2, unpack, 0, unroll=2)
+    lax.fori_loop(0, sources // 2, unpack, 0, unroll=4)
 
     def gather(source, _):
         rows = pl.ds(pl.multiple_of(16 * source, 16), 16)
@@ -277,7 +277,7 @@
         states[pl.ds(pl.multiple_of(16 * source, 16), 16), :] = jnp.concatenate(pair, axis=0).astype(BF)
         return state
 
-    lax.fori_loop(0, sources, advance, begin, unroll=4)
+    lax.fori_loop(0, sources, advance, begin, unroll=8)
 
     def mix(part, _):
         rows = pl.ds(pl.multiple_of(part * 64, 64), 64)
@@ -306,7 +306,7 @@
         return adjoint, later
 
     nothing = jnp.zeros((8, lanes), F32)
-    lax.fori_loop(0, sources, retreat, (nothing, nothing), unroll=4)
+    lax.fori_loop(0, sources, retreat, (nothing, nothing), unroll=8)
 
     half = sources // 2
     share = lanes // sources

time: 94 us -> 93.9 us (level)
  no operation moved by 1% of the time
where the time goes in v9:
time: 93.9 us; the launch traced here: 93.5 us
  blocking collectives  48.9 us (52%)
  starting transfers between devices  15.8 us (17%)
  waiting for transfers between devices  14 us (15%)
  Pallas kernels  11.4 us (12%)
  local copies, waits for them, and re-layouts  2.61 us (3%)
    all_to_all x1, blocking collectives, local(): mine = lax.all_to_all(send, 'tm', 0, 0, axis_index_groups=groups)  20.5 us
    all_to_all x1, blocking collectives, local(): got = lax.all_to_all(send, 'tm', 0, 0, axis_index_groups=groups)  17.5 us
    all_to_all x1, blocking collectives, local(): partial = lax.all_to_all(partial, 'row', 0, 0)  10.9 us
    ppermute x1, waiting for transfers between devices, local(): edge = lax.ppermute(edge, 'row', down)  5.64 us
    ppermute x1, starting transfers between devices, local(): other = lax.ppermute(whole, 'tm', swap)  4.65 us
    all_to_all x1, starting transfers between devices, local(): whole = lax.all_to_all(partial, 'tm', 0, 0, axis_index_groups=groups)  4.23 us
    pallas_call x1, Pallas kernels, local(): call(cell_body, 'cells', (shape((half, share, 12 * lanes), BF), shape((ha...  3.66 us
    all_to_all x1, waiting for transfers between devices, local(): whole = lax.all_to_all(partial, 'tm', 0, 0, axis_index_groups=groups)  3.44 us
  transfers between devices with their start and end apart: 6, of which 5 were waited for; matrix products, arithmetic and copies ran while one was open for 0% of the time, Pallas kernels for 5%

profile of v9, /device:TPU:1, one launch (start us, length us, event | category | flops | bytes accessed | tf_op | source)
XLA Modules:
  0.0 93.5 jit_solution(470196527593132602)
XLA Ops:
  0.6 1.7 %halo.1 = (bf16[392,256]{1,0:T(8,128)(2,1)}, f32[8,256]{1,0:T(8,128)}) custom-call(bf16[2,4,64,256]{3,2,1,0:T(8,128)(2,1)} %frames.3, bf16[2,4,64,256]{3,2,1,0:T(8,128)(2,1)} %refs_3_.1, f32[4,64,256]{2,1,0:T(8,128)} %start.1), custom_call_target="tpu_custom_call" | custom-call | flops 1048576 | bytes 1048576 | tf_op jit(solution)/shard_map/halo/pallas_call | solution.py:457
  2.3 2.5 %collective-permute-start = (bf16[392,256]{1,0:T(8,128)(2,1)}, bf16[392,256]{1,0:T(8,128)(2,1)S(1)}, u32[]{:S(2)}, u32[]{:S(2)}) collective-permute-start(bf16[392,256]{1,0:T(8,128)(2,1)} %get-tuple-element.15), channel_id=1, source_target_pairs={{0,1},{1,2},{2,3},{3,4},{4,5},{5,6},{6,7},{7,0},{8,9},{9,10},{10,1... | collective-permute-start | bytes 602120 | tf_op jit(solution)/shard_map/ppermute | solution.py:470
  4.8 0.9 %copy-done.1 = bf16[2,4,64,256]{3,2,1,0:T(8,128)(2,1)S(1)} copy-done((bf16[2,4,64,256]{3,2,1,0:T(8,128)(2,1)S(1)}, bf16[2,4,64,256]{3,2,1,0:T(8,128)(2,1)}, u32[]{:S(2)}) %copy-start.1) | copy-done | bytes 262168
  5.8 0.9 %copy-done.3 = bf16[2,4,64,256]{3,2,1,0:T(8,128)(2,1)S(1)} copy-done((bf16[2,4,64,256]{3,2,1,0:T(8,128)(2,1)S(1)}, bf16[2,4,64,256]{3,2,1,0:T(8,128)(2,1)}, u32[]{:S(2)}) %copy-start.3) | copy-done | bytes 262168
  6.8 0.7 copy-done.5
  7.4 0.6 own.1
  8.0 5.6 %collective-permute-done.halo = bf16[392,256]{1,0:T(8,128)(2,1)S(1)} collective-permute-done((bf16[392,256]{1,0:T(8,128)(2,1)}, bf16[392,256]{1,0:T(8,128)(2,1)S(1)}, u32[]{:S(2)}, u32[]{:S(2)}) %collective-permute-start) | collective-permute-done | bytes 200736 | tf_op jit(solution)/shard_map/ppermute | solution.py:470
  13.7 0.3 spread.1
  14.0 0.0 copy-start
  14.0 0.0 copy-start.6
  14.0 0.0 copy-start.7
  14.1 20.5 %all_to_all.20.mine = bf16[16,112,256]{2,1,0:T(8,128)(2,1)S(1)} all-to-all(bf16[16,112,256]{2,1,0:T(8,128)(2,1)S(1)} %spread.1), channel_id=1, replica_groups={{0,16,32,48,64,80,96,112,128,144,160,176,192,208,224,240},{8,24,40,56,7..., dimensions={0} | all-to-all | bytes 1835008 | tf_op jit(solution)/shard_map/all_to_all | solution.py:500
  34.5 2.6 %collective-permute-start.1 = (bf16[16,112,256]{2,1,0:T(8,128)(2,1)S(1)}, bf16[16,112,256]{2,1,0:T(8,128)(2,1)S(1)}, u32[]{:S(2)}, u32[]{:S(2)}) collective-permute-start(bf16[16,112,256]{2,1,0:T(8,128)(2,1)S(1)} %all_to_all.20.mine), channel_id=1, source_target_pairs={{0,8},{8,0},{16,24},{24,16},{32,40},{40,32},{48,56},{56,48},{64,72... | collective-permute-start | bytes 2752520 | tf_op jit(solution)/shard_map/ppermute | solution.py:501
  37.1 2.1 %collective-permute-done.1.theirs = bf16[16,112,256]{2,1,0:T(8,128)(2,1)S(1)} collective-permute-done((bf16[16,112,256]{2,1,0:T(8,128)(2,1)S(1)}, bf16[16,112,256]{2,1,0:T(8,128)(2,1)S(1)}, u32[]{:S(2)}, u32[]{:S(2)}) %collective-permute-start.1) | collective-permute-done | bytes 917536 | tf_op jit(solution)/shard_map/ppermute | solution.py:501
  39.2 3.7 %cells.1 = (bf16[16,8,3072]{2,1,0:T(8,128)(2,1)S(1)}, f32[16,8,2560]{2,1,0:T(8,128)S(1)}, bf16[16,8,512]{2,1,0:T(8,128)(2,1)S(1)}) custom-call(bf16[16,112,256]{2,1,0:T(8,128)(2,1)S(1)} %all_to_all.20.mine, bf16[16,112,256]{2,1,0:T(8,128)(2,1)S(1)} %collective-permute-done.1.theirs, bf16[2304,256]{1,0:T(8,128)(2,1)S(1)} %bitcast.3, ...), custom_call_target="tpu_custom_call" | custom-call | flops 1409286144 | bytes 4194304 | tf_op jit(solution)/shard_map/cells/pallas_call | solution.py:502
  42.9 0.5 collective-permute-start.2
  43.4 1.9 %collective-permute-done.2.taken = bf16[16,8,3072]{2,1,0:T(8,128)(2,1)S(1)} collective-permute-done((bf16[16,8,3072]{2,1,0:T(8,128)(2,1)S(1)}, bf16[16,8,3072]{2,1,0:T(8,128)(2,1)S(1)}, u32[]{:S(2)}, u32[]{:S(2)}) %collective-permute-start.2) | collective-permute-done | bytes 786464 | tf_op jit(solution)/shard_map/ppermute | solution.py:526
  45.3 0.2 merge.1
  45.5 0.0 copy-start.2
  45.5 0.0 copy-start.4
  45.5 17.5 %all_to_all.21.got = bf16[16,8,3584]{2,1,0:T(8,128)(2,1)S(1)} all-to-all(bf16[16,8,3584]{2,1,0:T(8,128)(2,1)S(1)} %merge.1), channel_id=1, replica_groups={{0,16,32,48,64,80,96,112,128,144,160,176,192,208,224,240},{8,24,40,56,7..., dimensions={0} | all-to-all | bytes 1835008 | tf_op jit(solution)/shard_map/all_to_all | solution.py:528
  63.0 0.4 join.1
  63.3 1.3 %collective-permute-start.3 = (bf16[2,2,64,256]{3,2,1,0:T(8,128)(2,1)S(1)}, bf16[2,2,64,256]{3,2,1,0:T(8,128)(2,1)S(1)}, u32[]{:S(2)}, u32[]{:S(2)}) collective-permute-start(bf16[2,2,64,256]{3,2,1,0:T(8,128)(2,1)S(1)} %get-tuple-element.22), channel_id=1, source_target_pairs={{1,0},{2,1},{3,2},{4,3},{5,4},{6,5},{7,6},{0,7},{9,8},{10,9},{11,1... | collective-permute-start | bytes 393224 | tf_op jit(solution)/shard_map/ppermute | solution.py:540
  64.6 10.9 %all_to_all.22.got = bf16[8,8,320]{2,1,0:T(8,128)(2,1)S(1)} all-to-all(bf16[8,8,320]{2,1,0:T(8,128)(2,1)S(1)} %get-tuple-element.20), channel_id=1, replica_groups=mesh['tm'=32,'row'=8] {'row'}, dimensions={0} | all-to-all | bytes 81920 | tf_op jit(solution)/shard_map/all_to_all | solution.py:541
  75.6 0.7 sum.1
  76.2 4.2 %all-to-all-start.3 = ((bf16[16,8,320]{2,1,0:T(8,128)(2,1)}), bf16[16,8,320]{2,1,0:T(8,128)(2,1)S(1)}, u32[]{:S(2)}, u32[]{:S(2)}) async-start(bf16[16,8,320]{2,1,0:T(8,128)(2,1)} %sum.1), calls=%async_computation.3 | async-start | bytes 196608 | tf_op jit(solution)/shard_map/all_to_all | solution.py:570
  80.5 1.6 %back.2.refs_5_ = bf16[2,4,64,256]{3,2,1,0:T(8,128)(2,1)} custom-call(bf16[2,4,64,256]{3,2,1,0:T(8,128)(2,1)S(1)} %get-tuple-element.21.refs_0_, bf16[9,256,256]{2,1,0:T(8,128)(2,1)S(1)} %copy-done, bf16[2,4,64,256]{3,2,1,0:T(8,128)(2,1)S(1)} %copy-done.2, f32[1,256]{1,0:T(1,128)S(1)} %bitcast.4), custom_call_target="tpu_custom_call" | custom-call | flops 301989888 | bytes 2097152 | tf_op jit(solution)/shard_map/back/pallas_call | solution.py:566
  82.1 1.6 %back.3 = bf16[2,4,64,256]{3,2,1,0:T(8,128)(2,1)} custom-call(bf16[2,4,64,256]{3,2,1,0:T(8,128)(2,1)S(1)} %get-tuple-element.21.refs_0_, bf16[2,2,64,256]{3,2,1,0:T(8,128)(2,1)S(1)} %collective-permute-done.3.refs_1_, bf16[9,256,256]{2,1,0:T(8,128)(2,1)S(1)} %copy-done, bf16[2,4,64,256]{3,2,1,0:T(8,128)(2,1)S(1)} %copy-done.2, ...), custom_call_target="tpu_custom_call", output_to_operand_aliasing={{}: (5, {})} | custom-call | flops 301989888 | bytes 2097152 | tf_op jit(solution)/shard_map/back/pallas_call | solution.py:567
  83.6 3.4 %all-to-all-done.3.mine = bf16[16,8,320]{2,1,0:T(8,128)(2,1)S(1)} async-done(((bf16[16,8,320]{2,1,0:T(8,128)(2,1)}), bf16[16,8,320]{2,1,0:T(8,128)(2,1)S(1)}, u32[]{:S(2)}, u32[]{:S(2)}) %all-to-all-start.3) | async-done | bytes 81952 | tf_op jit(solution)/shard_map/all_to_all | solution.py:570
  87.1 4.7 %collective-permute-start.4 = (bf16[16,8,320]{2,1,0:T(8,128)(2,1)S(1)}, bf16[16,8,320]{2,1,0:T(8,128)(2,1)S(1)}, u32[]{:S(2)}, u32[]{:S(2)}) collective-permute-start(bf16[16,8,320]{2,1,0:T(8,128)(2,1)S(1)} %all-to-all-done.3.mine), channel_id=1, source_target_pairs={{0,8},{8,0},{16,24},{24,16},{32,40},{40,32},{48,56},{56,48},{64,72... | collective-permute-start | bytes 245768 | tf_op jit(solution)/shard_map/ppermute | solution.py:572
  91.7 0.9 %collective-permute-done.4.theirs = bf16[16,8,320]{2,1,0:T(8,128)(2,1)S(1)} collective-permute-done((bf16[16,8,320]{2,1,0:T(8,128)(2,1)S(1)}, bf16[16,8,320]{2,1,0:T(8,128)(2,1)S(1)}, u32[]{:S(2)}, u32[]{:S(2)}) %collective-permute-start.4) | collective-permute-done | bytes 81952 | tf_op jit(solution)/shard_map/ppermute | solution.py:572
  92.7 0.9 last.1
  (9 shorter events, 0.0 us)
Async XLA Ops:
  2.3 11.4 %collective-permute-start = (bf16[392,256]{1,0:T(8,128)(2,1)}, bf16[392,256]{1,0:T(8,128)(2,1)S(1)}, u32[]{:S(2)}, u32[]{:S(2)}) collective-permute-start(bf16[392,256]{1,0:T(8,128)(2,1)} %get-tuple-element.15), channel_id=1, source_target_pairs={{0,1},{1,2},{2,3},{3,4},{4,5},{5,6},{6,7},{7,0},{8,9},{9,10},{10,1... | collective-permute-start | bytes 602120 | tf_op jit(solution)/shard_map/ppermute | solution.py:470
  4.8 0.9 %copy-start.1 = (bf16[2,4,64,256]{3,2,1,0:T(8,128)(2,1)S(1)}, bf16[2,4,64,256]{3,2,1,0:T(8,128)(2,1)}, u32[]{:S(2)}) copy-start(bf16[2,4,64,256]{3,2,1,0:T(8,128)(2,1)} %refs_3_.1) | copy-start | bytes 786436
  5.8 0.9 %copy-start.3 = (bf16[2,4,64,256]{3,2,1,0:T(8,128)(2,1)S(1)}, bf16[2,4,64,256]{3,2,1,0:T(8,128)(2,1)}, u32[]{:S(2)}) copy-start(bf16[2,4,64,256]{3,2,1,0:T(8,128)(2,1)} %frames.3) | copy-start | bytes 786436
  6.7 0.7 copy-start.5
  14.0 25.2 %copy-start = (bf16[9,256,256]{2,1,0:T(8,128)(2,1)S(1)}, bf16[9,256,256]{2,1,0:T(8,128)(2,1)}, u32[]{:S(2)}) copy-start(bf16[9,256,256]{2,1,0:T(8,128)(2,1)} %refs_2_.3) | copy-start | bytes 3538948
  14.0 25.2 %copy-start.6 = (bf16[256,256]{1,0:T(8,128)(2,1)S(1)}, bf16[256,256]{1,0:T(8,128)(2,1)}, u32[]{:S(2)}) copy-start(bf16[256,256]{1,0:T(8,128)(2,1)} %readout.1) | copy-start | bytes 393220
  14.0 25.2 %copy-start.7 = (f32[8,256]{1,0:T(8,128)S(1)}, f32[8,256]{1,0:T(8,128)}, u32[]{:S(2)}) copy-start(f32[8,256]{1,0:T(8,128)} %get-tuple-element.16.start) | copy-start | bytes 24580
  34.5 4.7 %collective-permute-start.1 = (bf16[16,112,256]{2,1,0:T(8,128)(2,1)S(1)}, bf16[16,112,256]{2,1,0:T(8,128)(2,1)S(1)}, u32[]{:S(2)}, u32[]{:S(2)}) collective-permute-start(bf16[16,112,256]{2,1,0:T(8,128)(2,1)S(1)} %all_to_all.20.mine), channel_id=1, source_target_pairs={{0,8},{8,0},{16,24},{24,16},{32,40},{40,32},{48,56},{56,48},{64,72... | collective-permute-start | bytes 2752520 | tf_op jit(solution)/shard_map/ppermute | solution.py:501
  42.9 2.4 %collective-permute-start.2 = (bf16[16,8,3072]{2,1,0:T(8,128)(2,1)S(1)}, bf16[16,8,3072]{2,1,0:T(8,128)(2,1)S(1)}, u32[]{:S(2)}, u32[]{:S(2)}) collective-permute-start(bf16[16,8,3072]{2,1,0:T(8,128)(2,1)S(1)} %get-tuple-element.17), channel_id=1, source_target_pairs={{0,8},{8,0},{16,24},{24,16},{32,40},{40,32},{48,56},{56,48},{64,72... | collective-permute-start | bytes 2359304 | tf_op jit(solution)/shard_map/ppermute | solution.py:526
  45.5 35.0 %copy-start.2 = (bf16[2,4,64,256]{3,2,1,0:T(8,128)(2,1)S(1)}, bf16[2,4,64,256]{3,2,1,0:T(8,128)(2,1)}, u32[]{:S(2)}) copy-start(bf16[2,4,64,256]{3,2,1,0:T(8,128)(2,1)} %refs_3_.1) | copy-start | bytes 786436
  45.5 35.0 %copy-start.4 = (f32[256]{0:T(256)S(1)}, f32[256]{0:T(256)}, u32[]{:S(2)}) copy-start(f32[256]{0:T(256)} %param.11) | copy-start | bytes 3076
  63.3 18.7 %collective-permute-start.3 = (bf16[2,2,64,256]{3,2,1,0:T(8,128)(2,1)S(1)}, bf16[2,2,64,256]{3,2,1,0:T(8,128)(2,1)S(1)}, u32[]{:S(2)}, u32[]{:S(2)}) collective-permute-start(bf16[2,2,64,256]{3,2,1,0:T(8,128)(2,1)S(1)} %get-tuple-element.22), channel_id=1, source_target_pairs={{1,0},{2,1},{3,2},{4,3},{5,4},{6,5},{7,6},{0,7},{9,8},{10,9},{11,1... | collective-permute-start | bytes 393224 | tf_op jit(solution)/shard_map/ppermute | solution.py:540
  76.2 10.8 %all-to-all-start.3 = ((bf16[16,8,320]{2,1,0:T(8,128)(2,1)}), bf16[16,8,320]{2,1,0:T(8,128)(2,1)S(1)}, u32[]{:S(2)}, u32[]{:S(2)}) async-start(bf16[16,8,320]{2,1,0:T(8,128)(2,1)} %sum.1), calls=%async_computation.3 | async-start | bytes 196608 | tf_op jit(solution)/shard_map/all_to_all | solution.py:570
  87.1 5.6 %collective-permute-start.4 = (bf16[16,8,320]{2,1,0:T(8,128)(2,1)S(1)}, bf16[16,8,320]{2,1,0:T(8,128)(2,1)S(1)}, u32[]{:S(2)}, u32[]{:S(2)}) collective-permute-start(bf16[16,8,320]{2,1,0:T(8,128)(2,1)S(1)} %all-to-all-done.3.mine), channel_id=1, source_target_pairs={{0,8},{8,0},{16,24},{24,16},{32,40},{40,32},{48,56},{56,48},{64,72... | collective-permute-start | bytes 245768 | tf_op jit(solution)/shard_map/ppermute | solution.py:572
